TPU v7x, 768 devices: a whole 4x8x12 slice. The times are simulated.
768 devices in a mesh: stream: 16 (over y_hi, x, core), cross: 48 (over z, y_lo).
Axes of the slice: x: 4, y: 8 (y_hi: 2, y_lo: 4; y = y_hi * 4 + y_lo), z: 12, core: 2. Of those that a mesh axis runs over, the one named last changes fastest.
Arguments:
- residual: bfloat16 [64, 384, 64, 128], P('stream', 'cross'), may hold values from -6 to 6
- approx_inverse: bfloat16 [16, 4608, 64, 256], P('stream', 'cross'), may hold values from -0.375 to 0.375
- pattern: int32 [16, 4608, 4], P('stream', 'cross'), may hold values from 0 to 95
- live_blocks: int32 [16, 48], P('stream', 'cross'), may hold values from 1 to 32, as said below
- block_aggregate: int32 [64, 384], P('stream', 'cross'), may hold values from 0 to 127
- coarse_inverse: float32 [512, 1536], P('stream', 'cross'), may hold values from -0.12 to 0.12
Outputs:
- correction: float32 [64, 384, 64, 128], P('stream', 'cross')
Inputs may be any that keep to these rules, and one draw needn't show every extreme that they name: `pattern`: block numbers of the extended grid, numbered row by row. `live_blocks`: some subdomain is full in every draw.
All inputs are finite; a program needn't handle non-finite values.
Results may differ from a plain program's by a relative error of at most 0.0065.
Values may be sent and summed in bfloat16 or wider, within the bound.
No kernel may reach another device: no remote copies, remote signals or barrier semaphores. Data moves between devices by JAX's collectives and lax.ppermute only.
A program may use at most 64 MiB of HBM per device.

v0:
```python
import jax
import jax.numpy as jnp
from jax import lax
from jax.sharding import PartitionSpec as P


def with_halo(cells, sides, width):
    for axis, dim in sides:
        count = lax.axis_size(axis)
        ends = count - 1
        head = lax.slice_in_dim(cells, 0, width, axis=dim)
        tail = lax.slice_in_dim(cells, cells.shape[dim] - width, cells.shape[dim], axis=dim)
        cells = jnp.concatenate(
            [
                lax.ppermute(tail, axis, [(i, (i + 1) % count) for i in range(ends)]),
                cells,
                lax.ppermute(head, axis, [((i + 1) % count, i) for i in range(ends)]),
            ],
            axis=dim,
        )
    return cells


def fold_margin(grid, along, length):
    middle = lax.slice_in_dim(grid, 4, length + 4, axis=along)
    lower = lax.slice_in_dim(grid, 0, 2, axis=along)
    upper = lax.slice_in_dim(grid, length + 6, length + 8, axis=along)
    low_pad = [(0, 0)] * grid.ndim
    high_pad = [(0, 0)] * grid.ndim
    low_pad[along] = (0, length - 2)
    high_pad[along] = (length - 2, 0)
    return middle + jnp.pad(lower, low_pad) + jnp.pad(upper, high_pad)


def body(residual, approx_inverse, pattern, live_blocks, block_aggregate, coarse_inverse):
    rows, columns, width, sides = residual.shape
    local = jnp.arange(rows)[:, None] * columns + jnp.arange(columns)[None, :]
    live = local < live_blocks[0, 0]
    masked = jnp.where(live[:, :, None, None], residual, jnp.zeros((), jnp.bfloat16))
    extent = (rows + 4) * (columns + 4)
    links = pattern[0]
    blocks = approx_inverse[0]
    depth = blocks.shape[2]
    extended = with_halo(masked, (("stream", 0), ("cross", 1)), 2)
    picked = extended.reshape(extent, width, sides)[links].reshape(extent, depth, sides)
    fixes = jnp.einsum("nac,ncr->nar", blocks, picked, preferred_element_type=jnp.float32)
    fixes = fixes.reshape(rows + 4, columns + 4, width, sides).astype(jnp.bfloat16)
    gathered = with_halo(fixes, (("stream", 0), ("cross", 1)), 2).astype(jnp.float32)
    fine = fold_margin(fold_margin(gathered, 0, rows), 1, columns)
    cells = width // 4
    per_block = masked.reshape(rows, columns, 4, cells, sides).astype(jnp.float32).sum(axis=3)
    per_block = per_block.reshape(rows * columns, 4 * sides)
    owned = coarse_inverse.shape[0] // 4
    groups = owned * lax.axis_size("stream")
    onehot = (
        block_aggregate.reshape(-1)[:, None] == jnp.arange(groups, dtype=jnp.int32)[None, :]
    ).astype(jnp.float32)
    chosen = onehot
    owned_sums = lax.psum_scatter(
        jnp.dot(chosen.T, per_block, precision=lax.Precision.HIGHEST).astype(jnp.bfloat16),
        "stream",
        scatter_dimension=0,
        tiled=True,
    ).astype(jnp.float32)
    coarse = jnp.dot(
        coarse_inverse, owned_sums.reshape(owned * 4, sides), precision=lax.Precision.HIGHEST
    )
    coarse = coarse.reshape(owned, 4 * sides)
    chosen = onehot
    prolonged = jnp.dot(
        chosen,
        lax.all_gather(coarse, "stream", axis=0, tiled=True),
        precision=lax.Precision.HIGHEST,
    )
    spread = jnp.broadcast_to(
        prolonged.reshape(rows, columns, 4, 1, sides), (rows, columns, 4, cells, sides)
    )
    spread = spread.reshape(rows, columns, width, sides)
    return jnp.where(live[:, :, None, None], fine + spread, jnp.zeros((), jnp.float32))


def solution(mesh):
    placed = (
        P("stream", "cross", None, None),
        P("stream", "cross", None, None),
        P("stream", "cross", None),
        P("stream", "cross"),
        P("stream", "cross"),
        P("stream", "cross"),
    )
    return jax.shard_map(
        body,
        mesh=mesh,
        in_specs=placed,
        out_specs=P("stream", "cross", None, None),
        check_vma=False,
    )
```

profile of v0, /device:TPU:73, one launch (start us, length us, event | category | flops | bytes accessed | tf_op | source)
XLA Modules:
  0.0 230.0 jit_solution(275498214412537680)
XLA Ops:
  6.5 0.0 copy-start
  6.5 0.0 copy-start.9
  6.5 0.0 copy-start.10
  6.5 0.0 reduce-scatter.2.cloned.1.call-start
  7.4 0.1 add_compare_fusion
  7.4 0.0 copy-start.7
  7.4 2.1 convert_reduce_fusion
  9.5 0.0 copy-start.3
  9.5 0.8 copy-done.3
  10.3 0.8 fusion.16
  11.1 3.7 %collective-permute-start = (bf16[2,8,64,128]{3,2,1,0:T(8,128)(2,1)}, bf16[2,8,64,128]{3,2,1,0:T(8,128)(2,1)S(1)}, u32[]{:S(2)}, u32[]{:S(2)}) collective-permute-start(bf16[2,8,64,128]{3,2,1,0:T(8,128)(2,1)} %get-tuple-element.13), channel_id=1, source_target_pairs={{0,48},{48,96},{96,144},{144,192},{192,240},{240,288},{288,336},{3... | collective-permute-start | bytes 786440 | tf_op jit(solution)/shard_map/ppermute | solution.py:15
  14.8 0.0 copy-done.7
  14.8 1.9 collective-permute-start.1
  16.7 0.0 copy-done.9
  16.8 0.1 eq.15
  16.8 1.6 collective-permute-done
  18.4 4.4 %collective-permute-done.1 = bf16[2,8,64,128]{3,2,1,0:T(8,128)(2,1)} collective-permute-done((bf16[2,8,64,128]{3,2,1,0:T(8,128)(2,1)}, bf16[2,8,64,128]{3,2,1,0:T(8,128)(2,1)}, u32[]{:S(2)}, u32[]{:S(2)}) %collective-permute-start.1) | collective-permute-done | bytes 262176 | tf_op jit(solution)/shard_map/ppermute | solution.py:17
  22.8 1.9 pad_maximum_fusion.6
  24.7 3.2 %collective-permute-start.2 = (bf16[8,2,64,128]{3,2,1,0:T(8,128)(2,1)}, bf16[8,2,64,128]{3,2,1,0:T(8,128)(2,1)}, u32[]{:S(2)}, u32[]{:S(2)}) collective-permute-start(bf16[8,2,64,128]{3,2,1,0:T(8,128)(2,1)} %get-tuple-element.11), channel_id=1, source_target_pairs={{0,1},{1,2},{2,3},{3,4},{4,5},{5,6},{6,7},{7,8},{8,9},{9,10},{10,1... | collective-permute-start | bytes 786440 | tf_op jit(solution)/shard_map/ppermute | solution.py:15
  27.9 2.1 collective-permute-start.3
  30.0 0.0 copy-done.10
  30.1 0.1 copy.8
  30.2 0.1 reshape.91
  30.3 9.9 %collective-permute-done.2 = bf16[8,2,64,128]{3,2,1,0:T(8,128)(2,1)} collective-permute-done((bf16[8,2,64,128]{3,2,1,0:T(8,128)(2,1)}, bf16[8,2,64,128]{3,2,1,0:T(8,128)(2,1)}, u32[]{:S(2)}, u32[]{:S(2)}) %collective-permute-start.2) | collective-permute-done | bytes 262176 | tf_op jit(solution)/shard_map/ppermute | solution.py:15
  40.2 1.1 collective-permute-done.3
  41.3 2.7 %pad_maximum_fusion = bf16[8,12,64,128]{3,2,1,0:T(8,128)(2,1)} fusion(bf16[8,2,64,128]{3,2,1,0:T(8,128)(2,1)} %collective-permute-done.3, bf16[2,8,64,128]{3,2,1,0:T(8,128)(2,1)} %collective-permute-done.1, bf16[4,8,64,128]{3,2,1,0:T(8,128)(2,1)} %copy-done.3, bf16[2,8,64,128]{3,2,1,0:T(8,128)(2,1)S(1)} %collective-permute-done, ...), kind=kLoop, calls=%fused_computation.8 | loop fusion | flops 3145728 | bytes 3145728 | tf_op jit(solution)/shard_map/concatenate | solution.py:13
  44.0 5.4 %gather_fusion = bf16[384,64,128]{2,1,0:T(8,128)(2,1)} fusion(bf16[96,64,128]{2,1,0:T(8,128)(2,1)} %bitcast.36, s32[1024]{0:T(1024)S(1)} %pad_clamp_fusion), kind=kCustom, calls=%fused_computation | custom fusion | bytes 12584448 | tf_op jit(solution)/shard_map/gather | solution.py:45
  49.4 0.0 copy-done
  49.4 4.0 %fusion.4 = bf16[96,128,64]{1,2,0:T(8,128)(2,1)S(1)} fusion(bf16[96,256,128]{2,1,0:T(8,128)(2,1)} %bitcast.41, bf16[1,96,64,256]{3,2,1,0:T(8,128)(2,1)S(1)} %copy-done), kind=kOutput, calls=%fused_computation.7 | convolution fusion | flops 403439616 | bytes 11010048 | tf_op jit(solution)/shard_map/nac,ncr->nar/dot_general | solution.py:46
  53.5 0.0 copy-start.1
  53.5 1.2 copy-done.1
  54.6 0.9 fusion.15
  55.5 1.9 collective-permute-start.5
  57.5 3.8 %collective-permute-start.4 = (bf16[2,12,64,128]{3,2,1,0:T(8,128)(2,1)}, bf16[2,12,64,128]{3,2,1,0:T(8,128)(2,1)}, u32[]{:S(2)}, u32[]{:S(2)}) collective-permute-start(bf16[2,12,64,128]{3,2,1,0:T(8,128)(2,1)} %bitcast.6), channel_id=1, source_target_pairs={{0,48},{48,96},{96,144},{144,192},{192,240},{240,288},{288,336},{3... | collective-permute-start | bytes 1179656 | tf_op jit(solution)/shard_map/ppermute | solution.py:15
  61.3 0.0 copy-done.6
  61.3 0.0 copy-done.4
  61.3 1.0 convolution_convert_fusion
  62.3 0.0 reduce-scatter.2.cloned.1.call-update
  62.3 105.8 %reduce-scatter.2.cloned.1.call-done = bf16[8,512]{1,0:T(8,128)(2,1)} async-done(((bf16[128,512]{1,0:T(8,128)(2,1)}), bf16[8,512]{1,0:T(8,128)(2,1)}) %reduce-scatter.2.cloned.1.call-update) | async-done | bytes 8208 | tf_op jit(solution)/shard_map/reduce_scatter | solution.py:59
  168.2 0.7 reshape.85
  168.9 0.0 copy-start.5
  168.9 0.0 collective-permute-done.5
  168.9 0.0 collective-permute-done.4
  168.9 2.0 pad_maximum_fusion.3
  170.9 2.2 collective-permute-start.6
  173.2 3.0 %collective-permute-start.7 = (bf16[12,2,64,128]{3,2,1,0:T(8,128)(2,1)}, bf16[12,2,64,128]{3,2,1,0:T(8,128)(2,1)}, u32[]{:S(2)}, u32[]{:S(2)}) collective-permute-start(bf16[12,2,64,128]{3,2,1,0:T(8,128)(2,1)} %get-tuple-element.8), channel_id=1, source_target_pairs={{1,0},{2,1},{3,2},{4,3},{5,4},{6,5},{7,6},{8,7},{9,8},{10,9},{11,1... | collective-permute-start | bytes 1179656 | tf_op jit(solution)/shard_map/ppermute | solution.py:17
  176.2 0.0 copy-done.5
  176.2 0.7 convolution_bitcast_fusion.1
  177.0 0.7 reshape.86
  177.7 39.2 %all_gather.3 = f32[128,512]{1,0:T(8,128)S(1)} all-gather(f32[8,512]{1,0:T(8,128)S(1)} %reshape.86), channel_id=1, replica_groups=mesh['stream'=16,'cross'=48] {'stream'}, dimensions={0}, use_global_device_ids=true | all-gather | bytes 278528 | tf_op jit(solution)/shard_map/all_gather | solution.py:72
  216.9 0.8 convolution_bitcast_fusion
  217.8 0.0 copy-start.2
  217.8 0.0 collective-permute-done.6
  217.8 0.0 collective-permute-done.7
  217.8 1.1 maximum_convert_fusion.1
  218.9 0.4 copy-done.2
  219.3 1.8 maximum_convert_fusion
  221.0 0.0 copy-done.12
  221.1 0.0 copy-start.8
  221.1 0.0 copy-start.11
  221.1 0.8 fusion.3
  221.9 0.0 copy-done.8
  221.9 0.0 copy-done.11
  221.9 1.2 fusion.10
  (8 shorter events, 0.1 us)
Async XLA Ops:
  6.5 42.9 %copy-start = (bf16[1,96,64,256]{3,2,1,0:T(8,128)(2,1)S(1)}, bf16[1,96,64,256]{3,2,1,0:T(8,128)(2,1)}, u32[]{:S(2)}) copy-start(bf16[1,96,64,256]{3,2,1,0:T(8,128)(2,1)} %param.7) | copy-start | bytes 9437188
  6.5 10.2 %copy-start.9 = (s32[4,8]{1,0:T(4,128)S(1)}, s32[4,8]{1,0:T(4,128)}, u32[]{:S(2)}) copy-start(s32[4,8]{1,0:T(4,128)} %param.10) | copy-start | bytes 388
  6.5 23.5 %copy-start.10 = (s32[1,96,4]{1,2,0:T(4,128)S(1)}, s32[1,96,4]{1,2,0:T(4,128)}, u32[]{:S(2)}) copy-start(s32[1,96,4]{1,2,0:T(4,128)} %param.8) | copy-start | bytes 4612
  6.5 161.6 %reduce-scatter.2.cloned.1.call-start = ((), (), s32[]{:S(2)}) async-start(), calls=%async_computation.1 | async-start | bytes 139264 | tf_op jit(solution)/shard_map/reduce_scatter | solution.py:59
  7.4 7.4 %copy-start.7 = (pred[4,8]{1,0:T(4,128)(4,1)}, pred[4,8]{1,0:T(4,128)(4,1)S(1)}, u32[]{:S(2)}) copy-start(pred[4,8]{1,0:T(4,128)(4,1)S(1)} %add_compare_fusion) | copy-start | bytes 100
  9.5 0.8 copy-start.3
  11.1 7.3 %collective-permute-start = (bf16[2,8,64,128]{3,2,1,0:T(8,128)(2,1)}, bf16[2,8,64,128]{3,2,1,0:T(8,128)(2,1)S(1)}, u32[]{:S(2)}, u32[]{:S(2)}) collective-permute-start(bf16[2,8,64,128]{3,2,1,0:T(8,128)(2,1)} %get-tuple-element.13), channel_id=1, source_target_pairs={{0,48},{48,96},{96,144},{144,192},{192,240},{240,288},{288,336},{3... | collective-permute-start | bytes 786440 | tf_op jit(solution)/shard_map/ppermute | solution.py:15
  14.8 8.0 %collective-permute-start.1 = (bf16[2,8,64,128]{3,2,1,0:T(8,128)(2,1)}, bf16[2,8,64,128]{3,2,1,0:T(8,128)(2,1)}, u32[]{:S(2)}, u32[]{:S(2)}) collective-permute-start(bf16[2,8,64,128]{3,2,1,0:T(8,128)(2,1)} %get-tuple-element.14), channel_id=1, source_target_pairs={{48,0},{96,48},{144,96},{192,144},{240,192},{288,240},{336,288},{3... | collective-permute-start | bytes 786440 | tf_op jit(solution)/shard_map/ppermute | solution.py:17
  16.8 44.4 %copy-start.6 = (s32[32]{0:T(128)}, s32[32]{0:T(128)S(1)}, u32[]{:S(2)}) copy-start(s32[32]{0:T(128)S(1)} %eq.15) | copy-start | bytes 388
  24.7 15.5 %collective-permute-start.2 = (bf16[8,2,64,128]{3,2,1,0:T(8,128)(2,1)}, bf16[8,2,64,128]{3,2,1,0:T(8,128)(2,1)}, u32[]{:S(2)}, u32[]{:S(2)}) collective-permute-start(bf16[8,2,64,128]{3,2,1,0:T(8,128)(2,1)} %get-tuple-element.11), channel_id=1, source_target_pairs={{0,1},{1,2},{2,3},{3,4},{4,5},{5,6},{6,7},{7,8},{8,9},{9,10},{10,1... | collective-permute-start | bytes 786440 | tf_op jit(solution)/shard_map/ppermute | solution.py:15
  27.9 13.4 %collective-permute-start.3 = (bf16[8,2,64,128]{3,2,1,0:T(8,128)(2,1)}, bf16[8,2,64,128]{3,2,1,0:T(8,128)(2,1)}, u32[]{:S(2)}, u32[]{:S(2)}) collective-permute-start(bf16[8,2,64,128]{3,2,1,0:T(8,128)(2,1)} %get-tuple-element.12), channel_id=1, source_target_pairs={{1,0},{2,1},{3,2},{4,3},{5,4},{6,5},{7,6},{8,7},{9,8},{10,9},{11,1... | collective-permute-start | bytes 786440 | tf_op jit(solution)/shard_map/ppermute | solution.py:17
  49.4 11.9 %copy-start.4 = (f32[4,8,4,128]{3,2,1,0:T(4,128)S(1)}, f32[4,8,4,128]{3,2,1,0:T(4,128)}, u32[]{:S(2)}) copy-start(f32[4,8,4,128]{3,2,1,0:T(4,128)} %get-tuple-element.5) | copy-start | bytes 196612
  53.5 1.2 copy-start.1
  55.5 113.4 %collective-permute-start.5 = (bf16[2,12,64,128]{3,2,1,0:T(8,128)(2,1)}, bf16[2,12,64,128]{3,2,1,0:T(8,128)(2,1)S(1)}, u32[]{:S(2)}, u32[]{:S(2)}) collective-permute-start(bf16[2,12,64,128]{3,2,1,0:T(8,128)(2,1)} %bitcast.8), channel_id=1, source_target_pairs={{48,0},{96,48},{144,96},{192,144},{240,192},{288,240},{336,288},{3... | collective-permute-start | bytes 1179656 | tf_op jit(solution)/shard_map/ppermute | solution.py:17
  57.5 111.4 %collective-permute-start.4 = (bf16[2,12,64,128]{3,2,1,0:T(8,128)(2,1)}, bf16[2,12,64,128]{3,2,1,0:T(8,128)(2,1)}, u32[]{:S(2)}, u32[]{:S(2)}) collective-permute-start(bf16[2,12,64,128]{3,2,1,0:T(8,128)(2,1)} %bitcast.6), channel_id=1, source_target_pairs={{0,48},{48,96},{96,144},{144,192},{192,240},{240,288},{288,336},{3... | collective-permute-start | bytes 1179656 | tf_op jit(solution)/shard_map/ppermute | solution.py:15
  168.9 7.3 %copy-start.5 = (f32[32,32]{1,0:T(8,128)S(1)}, f32[32,32]{1,0:T(8,128)}, u32[]{:S(2)}) copy-start(f32[32,32]{1,0:T(8,128)} %param.11) | copy-start | bytes 12292
  170.9 46.9 %collective-permute-start.6 = (bf16[12,2,64,128]{3,2,1,0:T(8,128)(2,1)}, bf16[12,2,64,128]{3,2,1,0:T(8,128)(2,1)}, u32[]{:S(2)}, u32[]{:S(2)}) collective-permute-start(bf16[12,2,64,128]{3,2,1,0:T(8,128)(2,1)} %get-tuple-element.7), channel_id=1, source_target_pairs={{0,1},{1,2},{2,3},{3,4},{4,5},{5,6},{6,7},{7,8},{8,9},{9,10},{10,1... | collective-permute-start | bytes 1179656 | tf_op jit(solution)/shard_map/ppermute | solution.py:15
  173.2 44.7 %collective-permute-start.7 = (bf16[12,2,64,128]{3,2,1,0:T(8,128)(2,1)}, bf16[12,2,64,128]{3,2,1,0:T(8,128)(2,1)}, u32[]{:S(2)}, u32[]{:S(2)}) collective-permute-start(bf16[12,2,64,128]{3,2,1,0:T(8,128)(2,1)} %get-tuple-element.8), channel_id=1, source_target_pairs={{1,0},{2,1},{3,2},{4,3},{5,4},{6,5},{7,6},{8,7},{9,8},{10,9},{11,1... | collective-permute-start | bytes 1179656 | tf_op jit(solution)/shard_map/ppermute | solution.py:17
  217.8 1.5 copy-start.2
  219.3 1.8 copy-start.12
  221.1 0.8 copy-start.8
  221.1 0.8 copy-start.11
Sparse Core Ops, SparseCore 0:
  62.5 105.6 reduce-scatter.1
where the time goes:
time: 231 us; the launch traced here: 230 us
  waiting for transfers between devices  123 us (53%)
  blocking collectives  39.2 us (17%)
  starting transfers between devices  21.8 us (9%)
  between operations  14.5 us (6%)
  other arithmetic  13.6 us (6%)
  local copies, waits for them, and re-layouts  11.3 us (5%)
  matrix products  6.66 us (3%)
    reduce_scatter x1, waiting for transfers between devices, body(): lax.psum_scatter(jnp.dot(chosen.T, per_block, precision=lax.Precision.HIG...  106 us
    all_gather x1, blocking collectives, body(): lax.all_gather(coarse, 'stream', axis=0, tiled=True)  39.2 us
    ppermute x4, starting transfers between devices, with_halo(): lax.ppermute(tail, axis, [(i, (i + 1) % count) for i in range(ends)])  12.9 us
    ppermute x4, waiting for transfers between devices, with_halo(): lax.ppermute(tail, axis, [(i, (i + 1) % count) for i in range(ends)])  11.5 us
    ppermute x4, starting transfers between devices, with_halo(): lax.ppermute(head, axis, [((i + 1) % count, i) for i in range(ends)])  8.96 us
    ppermute x4, waiting for transfers between devices, with_halo(): lax.ppermute(head, axis, [((i + 1) % count, i) for i in range(ends)])  5.52 us
    gather x1, local copies, waits for them, and re-layouts, body(): extended.reshape(extent, width, sides)[links].reshape(extent, depth, sides)  5.43 us
  transfers between devices with their start and end apart: 9, of which 5 were waited for; matrix products, arithmetic and copies ran while one was open for 2% of the time, Pallas kernels for 0%

commit v1 on v0

v1 whole, which is shorter than its diff:
```python
import jax
import jax.numpy as jnp
from jax import lax
from jax.experimental import pallas as pl
from jax.experimental.pallas import tpu as pltpu
from jax.sharding import PartitionSpec as P

BF16 = jnp.bfloat16
F32 = jnp.float32
MIB = 1 << 20
VMEM = pl.BlockSpec(memory_space=pltpu.VMEM)
SMEM = pl.BlockSpec(memory_space=pltpu.SMEM)
ANY = pl.BlockSpec(memory_space=pl.ANY)


def shift(values, axis, step):
    count = lax.axis_size(axis)
    pairs = [(i, i + step) for i in range(count) if 0 <= i + step < count]
    return lax.ppermute(values, axis, pairs)


def shaped(shape, dtype):
    return jax.ShapeDtypeStruct(shape, dtype)


def cost(flops, moved):
    return pl.CostEstimate(flops=flops, bytes_accessed=moved, transcendentals=0)


def mask_kernel(live_ref, residual_ref, top_ref, bottom_ref, left_ref, right_ref):
    rows, columns = residual_ref.shape[:2]
    half = rows // 2
    live = live_ref[0, 0]
    for i in range(rows):
        for j in range(columns):
            block = residual_ref[i, j]
            kept = jnp.where(i * columns + j < live, block, jnp.zeros_like(block))
            if i < half:
                top_ref[i, j] = kept
            else:
                bottom_ref[i - half, j] = kept
            if j < 2:
                left_ref[i, j] = kept
            if j >= columns - 2:
                right_ref[i, j - columns + 2] = kept


def mask_blocks(live, residual):
    rows, columns, width, sides = residual.shape
    wide = shaped((rows // 2, columns, width, sides), BF16)
    tall = shaped((rows, 2, width, sides), BF16)
    return pl.pallas_call(
        mask_kernel,
        out_shape=(wide, wide, tall, tall),
        in_specs=[SMEM, VMEM],
        out_specs=(VMEM,) * 4,
        cost_estimate=cost(0, 2 * residual.size * 2),
        compiler_params=pltpu.CompilerParams(vmem_limit_bytes=4 * MIB),
        name="mask_blocks",
    )(live, residual)


def labels_of(agg_ref, shape, axis):
    rows, columns = agg_ref.shape
    place = lax.broadcasted_iota(jnp.int32, shape, axis) // 4
    labels = jnp.zeros(shape, jnp.int32)
    for i in range(rows):
        for j in range(columns):
            labels = jnp.where(place == i * columns + j, agg_ref[i, j], labels)
    return labels


def partial_kernel(live_ref, agg_ref, residual_ref, out_ref):
    unknowns, sides = residual_ref.shape
    rows, columns = agg_ref.shape
    fields = rows * columns * 4
    cells = unknowns // fields
    owners, slot, _ = out_ref.shape
    row = lax.broadcasted_iota(jnp.int32, (fields, unknowns), 0)
    column = lax.broadcasted_iota(jnp.int32, (fields, unknowns), 1)
    picks = jnp.where((column // cells == row) & (row // 4 < live_ref[0, 0]), 1.0, 0.0)
    sums = jnp.dot(picks.astype(BF16), residual_ref[...], preferred_element_type=F32)
    labels = labels_of(agg_ref, (1, fields), 1)
    row = lax.broadcasted_iota(jnp.int32, (owners * slot, fields), 0)
    column = lax.broadcasted_iota(jnp.int32, (owners * slot, fields), 1)
    onehot = jnp.where((labels == row // 4) & (row % 4 == column % 4), 1.0, 0.0)
    total = jnp.dot(
        onehot, sums, precision=lax.Precision.HIGHEST, preferred_element_type=F32
    )
    out_ref[...] = total.astype(BF16).reshape(owners, slot, sides)


def partial_sums(live, agg, residual, owners, slot):
    sides = residual.shape[-1]
    flat = residual.reshape(-1, sides)
    return pl.pallas_call(
        partial_kernel,
        out_shape=shaped((owners, slot, sides), BF16),
        in_specs=[SMEM, SMEM, VMEM],
        out_specs=VMEM,
        cost_estimate=cost(2 * 128 * flat.size, 2 * flat.size),
        compiler_params=pltpu.CompilerParams(vmem_limit_bytes=6 * MIB),
        name="partial_sums",
    )(live, agg, flat)


def solve_kernel(parts_ref, inverse_ref, out_ref):
    owners = parts_ref.shape[0]
    total = parts_ref[0].astype(F32)
    for i in range(1, owners):
        total = total + parts_ref[i].astype(F32)
    coarse = jnp.dot(
        inverse_ref[...],
        total,
        precision=lax.Precision.HIGHEST,
        preferred_element_type=F32,
    ).astype(BF16)
    for i in range(owners):
        out_ref[i] = coarse


def coarse_solve(parts, inverse):
    return pl.pallas_call(
        solve_kernel,
        out_shape=shaped(parts.shape, BF16),
        in_specs=[VMEM, VMEM],
        out_specs=VMEM,
        cost_estimate=cost(2 * parts.shape[1] * parts.size, 4 * parts.size),
        compiler_params=pltpu.CompilerParams(vmem_limit_bytes=2 * MIB),
        name="coarse_solve",
    )(parts, inverse)


def corners_kernel(left_ref, right_ref, up_ref, down_ref):
    half = up_ref.shape[0]
    up_ref[:, :2] = left_ref[:half]
    up_ref[:, 2:] = right_ref[:half]
    down_ref[:, :2] = left_ref[half:]
    down_ref[:, 2:] = right_ref[half:]


def corners(left, right):
    rows, _, width, sides = left.shape
    piece = shaped((rows // 2, 4, width, sides), BF16)
    return pl.pallas_call(
        corners_kernel,
        out_shape=(piece, piece),
        in_specs=[VMEM, VMEM],
        out_specs=(VMEM, VMEM),
        cost_estimate=cost(0, 8 * left.size),
        compiler_params=pltpu.CompilerParams(vmem_limit_bytes=2 * MIB),
        name="corners",
    )(left, right)


def fix_kernel(
    pattern_ref,
    blocks_ref,
    above,
    below,
    top,
    bottom,
    left,
    right,
    corner_above,
    corner_below,
    up_main,
    down_main,
    up_corner,
    down_corner,
    side_left,
    side_right,
    center,
    grid_ref,
    fixes,
    in_sems,
    out_sems,
):
    step = pl.program_id(0)
    tall, wide = fixes.shape[:2]
    last = tall - 1
    columns = wide - 4
    half = (tall - 4) // 2
    inner, outer = pl.ds(2, columns), pl.ds(2 + columns, 2)
    first = pl.ds(0, 2)

    def moves_in():
        pieces = []
        for i in range(tall):
            if i < 2:
                row = (corner_above.at[i, first], above.at[i], corner_above.at[i, pl.ds(2, 2)])
            elif i < tall - 2:
                j = i - 2
                own = top.at[j] if j < half else bottom.at[j - half]
                row = (left.at[j], own, right.at[j])
            else:
                j = i - tall + 2
                row = (corner_below.at[j, first], below.at[j], corner_below.at[j, pl.ds(2, 2)])
            for piece, start, count in zip(row, (0, 2, 2 + columns), (2, columns, 2)):
                pieces.append((piece, pl.ds(i * wide + start, count)))
        return [
            pltpu.make_async_copy(piece, grid_ref.at[place], in_sems.at[i])
            for i, (piece, place) in enumerate(pieces)
        ]

    def moves_out(begin, end_at):
        own, end = pl.ds(2, tall - 4), pl.ds(tall - 2, 2)
        pieces = [
            (up_main, (first, inner)),
            (up_corner.at[:, pl.ds(0, 2)], (first, first)),
            (up_corner.at[:, pl.ds(2, 2)], (first, outer)),
            (side_left, (own, first)),
            (side_right, (own, outer)),
            (center, (own, inner)),
            (down_main, (end, inner)),
            (down_corner.at[:, pl.ds(0, 2)], (end, first)),
            (down_corner.at[:, pl.ds(2, 2)], (end, outer)),
        ]
        return [
            pltpu.make_async_copy(fixes.at[place], piece, out_sems.at[i])
            for i, (piece, place) in enumerate(pieces)
            if begin <= i < end_at
        ]

    @pl.when(step == 0)
    def _():
        copies = moves_in()
        for copy in copies:
            copy.start()
        for copy in copies:
            copy.wait()

    for j in range(wide):
        n = step * wide + j
        picked = jnp.concatenate([grid_ref[pattern_ref[k, n]] for k in range(4)], axis=0)
        fix = jnp.dot(blocks_ref[j], picked, preferred_element_type=F32)
        fixes[step, j] = fix.astype(BF16)

    @pl.when(step == 1)
    def _():
        for copy in moves_out(0, 3):
            copy.start()

    @pl.when(step == last - 2)
    def _():
        for copy in moves_out(3, 6):
            copy.start()

    @pl.when(step == last)
    def _():
        for copy in moves_out(6, 9):
            copy.start()
        for copy in moves_out(0, 9):
            copy.wait()


def local_fixes(pattern, blocks, pieces, rows, columns):
    count, width, depth = blocks.shape
    sides = pieces[0].shape[-1]
    tall, wide = rows + 4, columns + 4
    main = shaped((2, columns, width, sides), BF16)
    corner = shaped((2, 4, width, sides), BF16)
    side = shaped((rows, 2, width, sides), BF16)
    center = shaped((rows, columns, width, sides), BF16)
    return pl.pallas_call(
        fix_kernel,
        out_shape=(main, main, corner, corner, side, side, center),
        grid_spec=pltpu.PrefetchScalarGridSpec(
            num_scalar_prefetch=0,
            grid=(tall,),
            in_specs=[SMEM, pl.BlockSpec((wide, width, depth), lambda i: (i, 0, 0))]
            + [ANY] * 8,
            out_specs=[ANY] * 7,
            scratch_shapes=[
                pltpu.VMEM((count, width, sides), BF16),
                pltpu.VMEM((tall, wide, width, sides), BF16),
                pltpu.SemaphoreType.DMA((3 * tall,)),
                pltpu.SemaphoreType.DMA((9,)),
            ],
        ),
        cost_estimate=cost(2 * blocks.size * sides, 2 * blocks.size + 4 * count * width * sides),
        compiler_params=pltpu.CompilerParams(vmem_limit_bytes=8 * MIB),
        name="local_fixes",
    )(pattern, blocks, *pieces)


def fold_kernel(left_ref, right_ref, above_ref, below_ref, out_left, out_right):
    half = above_ref.shape[0]
    for i in range(2 * half):
        source = above_ref if i < half else below_ref
        for j in range(2):
            row = i % half
            out_left[i, j] = (
                left_ref[i, j].astype(F32) + source[row, j].astype(F32)
            ).astype(BF16)
            out_right[i, j] = (
                right_ref[i, j].astype(F32) + source[row, 2 + j].astype(F32)
            ).astype(BF16)


def fold_sides(left, right, above, below):
    return pl.pallas_call(
        fold_kernel,
        out_shape=(shaped(left.shape, BF16), shaped(left.shape, BF16)),
        in_specs=[VMEM] * 4,
        out_specs=(VMEM, VMEM),
        cost_estimate=cost(2 * left.size, 12 * left.size),
        compiler_params=pltpu.CompilerParams(vmem_limit_bytes=2 * MIB),
        name="fold_sides",
    )(left, right, above, below)


def join_kernel(
    live_ref,
    agg_ref,
    coarse_ref,
    center_ref,
    above_ref,
    below_ref,
    left_ref,
    right_ref,
    out_ref,
    spread,
):
    step = pl.program_id(0)
    rows, columns, width, sides = center_ref.shape
    cells = width // 4

    @pl.when(step == 0)
    def _():
        shape = (spread.shape[0], coarse_ref.shape[0])
        row = lax.broadcasted_iota(jnp.int32, shape, 0)
        column = lax.broadcasted_iota(jnp.int32, shape, 1)
        labels = labels_of(agg_ref, (shape[0], 1), 0)
        onehot = jnp.where((column // 4 == labels) & (column % 4 == row % 4), 1.0, 0.0)
        spread[...] = jnp.dot(
            onehot.astype(BF16), coarse_ref[...], preferred_element_type=F32
        )

    def half(base, source):
        for i in range(rows):
            for j in range(columns):
                block = base * columns + i * columns + j
                total = center_ref[i, j].astype(F32) + source[i, j].astype(F32)
                if j < 2:
                    total = total + left_ref[i, j].astype(F32)
                if j >= columns - 2:
                    total = total + right_ref[i, j - columns + 2].astype(F32)
                lifted = jnp.concatenate(
                    [
                        jnp.broadcast_to(spread[pl.ds(block * 4 + f, 1), :], (cells, sides))
                        for f in range(4)
                    ],
                    axis=0,
                )
                total = total + lifted
                out_ref[i, j] = jnp.where(
                    block < live_ref[0, 0], total, jnp.zeros_like(total)
                )

    @pl.when(step == 0)
    def _():
        half(0, above_ref)

    @pl.when(step == 1)
    def _():
        half(rows, below_ref)


def join(live, agg, coarse, center, above, below, left, right):
    rows, columns, width, sides = center.shape
    half = rows // 2
    whole = pl.BlockSpec((half, columns, width, sides), lambda i: (0, 0, 0, 0))
    moving = pl.BlockSpec((half, columns, width, sides), lambda i: (i, 0, 0, 0))
    thin = pl.BlockSpec((half, 2, width, sides), lambda i: (i, 0, 0, 0))
    flat = pl.BlockSpec(coarse.shape, lambda i: (0, 0))
    return pl.pallas_call(
        join_kernel,
        out_shape=shaped(center.shape, F32),
        grid_spec=pltpu.PrefetchScalarGridSpec(
            num_scalar_prefetch=0,
            grid=(2,),
            in_specs=[SMEM, SMEM, flat, moving, whole, whole, thin, thin],
            out_specs=moving,
            scratch_shapes=[pltpu.VMEM((rows * columns * 4, sides), F32)],
        ),
        cost_estimate=cost(8 * center.size, 10 * center.size),
        compiler_params=pltpu.CompilerParams(vmem_limit_bytes=10 * MIB),
        name="join",
    )(live, agg, coarse, center, above, below, left, right)


def body(residual, approx_inverse, pattern, live_blocks, block_aggregate, coarse_inverse):
    rows, columns, width, sides = residual.shape
    owners = lax.axis_size("stream")
    slot = coarse_inverse.shape[0]
    top, bottom, left, right = mask_blocks(live_blocks, residual)
    from_left = shift(right, "cross", 1)
    from_right = shift(left, "cross", -1)
    above = shift(bottom, "stream", 1)
    below = shift(top, "stream", -1)
    parts = partial_sums(live_blocks, block_aggregate, residual, owners, slot)
    corner_up, corner_down = corners(from_left, from_right)
    corner_above = shift(corner_down, "stream", 1)
    corner_below = shift(corner_up, "stream", -1)
    parts, _ = lax.optimization_barrier((parts, corner_up))
    parts = lax.all_to_all(parts, "stream", 0, 0)
    corner_above, parts = lax.optimization_barrier((corner_above, parts))
    pieces = (above, below, top, bottom, from_left, from_right, corner_above, corner_below)
    up_main, down_main, up_corner, down_corner, side_left, side_right, center = local_fixes(
        jnp.transpose(pattern[0]), approx_inverse[0], pieces, rows, columns
    )
    corner_above = shift(down_corner, "stream", 1)
    corner_below = shift(up_corner, "stream", -1)
    above = shift(down_main, "stream", 1)
    below = shift(up_main, "stream", -1)
    coarse = coarse_solve(parts, coarse_inverse)
    out_left, out_right = fold_sides(side_left, side_right, corner_above, corner_below)
    from_right = shift(out_left, "cross", -1)
    from_left = shift(out_right, "cross", 1)
    coarse, _ = lax.optimization_barrier((coarse, out_left))
    coarse = lax.all_to_all(coarse, "stream", 0, 0).reshape(owners * slot, sides)
    return join(
        live_blocks, block_aggregate, coarse, center, above, below, from_left, from_right
    )


def solution(mesh):
    placed = (
        P("stream", "cross", None, None),
        P("stream", "cross", None, None),
        P("stream", "cross", None),
        P("stream", "cross"),
        P("stream", "cross"),
        P("stream", "cross"),
    )
    return jax.shard_map(
        body,
        mesh=mesh,
        in_specs=placed,
        out_specs=P("stream", "cross", None, None),
        check_vma=False,
    )
```

time: 231 us -> 110 us (0.48)
  the two profiles are of different devices: /device:TPU:73 before, /device:TPU:248 now
where the time goes in v1:
time: 110 us; the launch traced here: 109 us
  starting transfers between devices  80.4 us (73%)
  waiting for transfers between devices  11.6 us (11%)
  Pallas kernels  10.6 us (10%)
  local copies, waits for them, and re-layouts  5.33 us (5%)
    ppermute x12, starting transfers between devices, shift(): return lax.ppermute(values, axis, pairs)  66 us
    ppermute x12, waiting for transfers between devices, shift(): return lax.ppermute(values, axis, pairs)  11.6 us
    all_to_all x1, starting transfers between devices, body(): parts = lax.all_to_all(parts, 'stream', 0, 0)  7.24 us
    all_to_all x1, starting transfers between devices, body(): lax.all_to_all(coarse, 'stream', 0, 0).reshape(owners * slot, sides)  7.24 us
    pallas_call x1, Pallas kernels, local_fixes(): pl.pallas_call(fix_kernel, out_shape=(main, main, corner, corner, side, s...  5.94 us
    unnamed x14, local copies, waits for them, and re-layouts  5.33 us
  transfers between devices with their start and end apart: 14, of which 4 were waited for; matrix products, arithmetic and copies ran while one was open for 0% of the time, Pallas kernels for 3%

profile of v1, /device:TPU:248, one launch (start us, length us, event | category | flops | bytes accessed | tf_op | source)
XLA Modules:
  0.0 108.9 jit_solution(1160244445714659287)
XLA Ops:
  0.7 0.0 copy-start.1
  0.7 1.0 copy-done.1
  1.7 0.0 copy-start.3
  1.7 0.1 mask_blocks.1
  1.9 7.8 %collective-permute-start = (bf16[4,2,64,128]{3,2,1,0:T(8,128)(2,1)S(1)}, bf16[4,2,64,128]{3,2,1,0:T(8,128)(2,1)S(1)}, u32[]{:S(2)}, u32[]{:S(2)}) collective-permute-start(bf16[4,2,64,128]{3,2,1,0:T(8,128)(2,1)S(1)} %get-tuple-element.24), channel_id=1, source_target_pairs={{0,1},{1,2},{2,3},{3,4},{4,5},{5,6},{6,7},{7,8},{8,9},{9,10},{10,1... | collective-permute-start | bytes 393224 | tf_op jit(solution)/shard_map/ppermute | solution.py:19
  9.7 1.9 %collective-permute-start.1 = (bf16[4,2,64,128]{3,2,1,0:T(8,128)(2,1)S(1)}, bf16[4,2,64,128]{3,2,1,0:T(8,128)(2,1)S(1)}, u32[]{:S(2)}, u32[]{:S(2)}) collective-permute-start(bf16[4,2,64,128]{3,2,1,0:T(8,128)(2,1)S(1)} %get-tuple-element.25), channel_id=1, source_target_pairs={{1,0},{2,1},{3,2},{4,3},{5,4},{6,5},{7,6},{8,7},{9,8},{10,9},{11,1... | collective-permute-start | bytes 393224 | tf_op jit(solution)/shard_map/ppermute | solution.py:19
  11.6 1.9 %collective-permute-start.3 = (bf16[2,8,64,128]{3,2,1,0:T(8,128)(2,1)S(1)}, bf16[2,8,64,128]{3,2,1,0:T(8,128)(2,1)S(1)}, u32[]{:S(2)}, u32[]{:S(2)}) collective-permute-start(bf16[2,8,64,128]{3,2,1,0:T(8,128)(2,1)S(1)} %get-tuple-element.30.bottom), channel_id=1, source_target_pairs={{0,48},{48,96},{96,144},{144,192},{192,240},{240,288},{288,336},{3... | collective-permute-start | bytes 786440 | tf_op jit(solution)/shard_map/ppermute | solution.py:19
  13.6 9.7 %collective-permute-start.4 = (bf16[2,8,64,128]{3,2,1,0:T(8,128)(2,1)S(1)}, bf16[2,8,64,128]{3,2,1,0:T(8,128)(2,1)S(1)}, u32[]{:S(2)}, u32[]{:S(2)}) collective-permute-start(bf16[2,8,64,128]{3,2,1,0:T(8,128)(2,1)S(1)} %get-tuple-element.31.top), channel_id=1, source_target_pairs={{48,0},{96,48},{144,96},{192,144},{240,192},{288,240},{336,288},{3... | collective-permute-start | bytes 786440 | tf_op jit(solution)/shard_map/ppermute | solution.py:19
  23.2 0.0 copy-start.2
  23.2 1.0 copy-done.2
  24.3 0.0 copy-start.4
  24.3 0.7 copy-done.4
  25.0 1.9 %partial_sums.1 = bf16[16,32,128]{2,1,0:T(8,128)(2,1)} custom-call(s32[1,1]{1,0:T(1,128)S(6)} %copy.7.live_ref, s32[4,8]{1,0:T(4,128)S(1)} %copy-done.4, bf16[2048,128]{1,0:T(8,128)(2,1)S(1)} %bitcast.7), custom_call_target="tpu_custom_call" | custom-call | flops 67108864 | bytes 524288 | tf_op jit(solution)/shard_map/partial_sums/pallas_call | solution.py:96
  26.8 0.0 copy-start.5
  26.8 0.0 collective-permute-done.left_ref.left
  26.8 0.0 collective-permute-done.1.right_ref.right
  26.9 7.2 %all-to-all-start = ((bf16[16,32,128]{2,1,0:T(8,128)(2,1)}), bf16[16,32,128]{2,1,0:T(8,128)(2,1)S(1)}, u32[]{:S(2)}, u32[]{:S(2)}) async-start(bf16[16,32,128]{2,1,0:T(8,128)(2,1)} %partial_sums.1), calls=%async_computation | async-start | bytes 262144 | tf_op jit(solution)/shard_map/all_to_all | solution.py:407
  34.1 2.0 %collective-permute-start.2 = (bf16[2,4,64,128]{3,2,1,0:T(8,128)(2,1)S(1)}, bf16[2,4,64,128]{3,2,1,0:T(8,128)(2,1)S(1)}, u32[]{:S(2)}, u32[]{:S(2)}) collective-permute-start(bf16[2,4,64,128]{3,2,1,0:T(8,128)(2,1)S(1)} %get-tuple-element.26), channel_id=1, source_target_pairs={{0,48},{48,96},{96,144},{144,192},{192,240},{240,288},{288,336},{3... | collective-permute-start | bytes 393224 | tf_op jit(solution)/shard_map/ppermute | solution.py:19
  36.1 9.5 %collective-permute-start.5 = (bf16[2,4,64,128]{3,2,1,0:T(8,128)(2,1)S(1)}, bf16[2,4,64,128]{3,2,1,0:T(8,128)(2,1)S(1)}, u32[]{:S(2)}, u32[]{:S(2)}) collective-permute-start(bf16[2,4,64,128]{3,2,1,0:T(8,128)(2,1)S(1)} %get-tuple-element.27), channel_id=1, source_target_pairs={{48,0},{96,48},{144,96},{192,144},{240,192},{288,240},{336,288},{3... | collective-permute-start | bytes 393224 | tf_op jit(solution)/shard_map/ppermute | solution.py:19
  45.7 0.7 collective-permute-done.2.corner_above
  46.4 0.0 all-to-all-done.parts_ref
  46.4 1.8 %collective-permute-done.5.corner_below = bf16[2,4,64,128]{3,2,1,0:T(8,128)(2,1)S(1)} collective-permute-done((bf16[2,4,64,128]{3,2,1,0:T(8,128)(2,1)S(1)}, bf16[2,4,64,128]{3,2,1,0:T(8,128)(2,1)S(1)}, u32[]{:S(2)}, u32[]{:S(2)}) %collective-permute-start.5) | collective-permute-done | bytes 131104 | tf_op jit(solution)/shard_map/ppermute | solution.py:19
  48.2 0.0 collective-permute-done.3.above
  48.2 0.0 collective-permute-done.4.below
  48.2 0.0 copy-start
  48.2 1.9 %copy-done = bf16[1,96,64,256]{3,2,1,0:T(8,128)(2,1)S(1)} copy-done((bf16[1,96,64,256]{3,2,1,0:T(8,128)(2,1)S(1)}, bf16[1,96,64,256]{3,2,1,0:T(8,128)(2,1)}, u32[]{:S(2)}) %copy-start) | copy-done | bytes 3145752
  50.1 0.0 copy-start.6
  50.1 0.7 copy-done.6
  50.8 5.9 %local_fixes.1 = (bf16[2,8,64,128]{3,2,1,0:T(8,128)(2,1)S(1)}, bf16[2,8,64,128]{3,2,1,0:T(8,128)(2,1)S(1)}, bf16[2,4,64,128]{3,2,1,0:T(8,128)(2,1)S(1)}, bf16[2,...) custom-call(s32[4,96]{1,0:T(4,128)S(1)} %bitcast.9, ...), custom_call_target="tpu_custom_call" | custom-call | flops 402653184 | bytes 6291456 | tf_op jit(solution)/shard_map/local_fixes/pallas_call | solution.py:265
  56.7 1.9 %collective-permute-start.6 = (bf16[2,4,64,128]{3,2,1,0:T(8,128)(2,1)S(1)}, bf16[2,4,64,128]{3,2,1,0:T(8,128)(2,1)S(1)}, u32[]{:S(2)}, u32[]{:S(2)}) collective-permute-start(bf16[2,4,64,128]{3,2,1,0:T(8,128)(2,1)S(1)} %get-tuple-element.35), channel_id=1, source_target_pairs={{0,48},{48,96},{96,144},{144,192},{192,240},{240,288},{288,336},{3... | collective-permute-start | bytes 393224 | tf_op jit(solution)/shard_map/ppermute | solution.py:19
  58.6 9.8 %collective-permute-start.7 = (bf16[2,4,64,128]{3,2,1,0:T(8,128)(2,1)S(1)}, bf16[2,4,64,128]{3,2,1,0:T(8,128)(2,1)S(1)}, u32[]{:S(2)}, u32[]{:S(2)}) collective-permute-start(bf16[2,4,64,128]{3,2,1,0:T(8,128)(2,1)S(1)} %get-tuple-element.36), channel_id=1, source_target_pairs={{48,0},{96,48},{144,96},{192,144},{240,192},{288,240},{336,288},{3... | collective-permute-start | bytes 393224 | tf_op jit(solution)/shard_map/ppermute | solution.py:19
  68.4 1.9 %collective-permute-start.8 = (bf16[2,8,64,128]{3,2,1,0:T(8,128)(2,1)S(1)}, bf16[2,8,64,128]{3,2,1,0:T(8,128)(2,1)S(1)}, u32[]{:S(2)}, u32[]{:S(2)}) collective-permute-start(bf16[2,8,64,128]{3,2,1,0:T(8,128)(2,1)S(1)} %get-tuple-element.40), channel_id=1, source_target_pairs={{0,48},{48,96},{96,144},{144,192},{192,240},{240,288},{288,336},{3... | collective-permute-start | bytes 786440 | tf_op jit(solution)/shard_map/ppermute | solution.py:19
  70.4 9.7 %collective-permute-start.9 = (bf16[2,8,64,128]{3,2,1,0:T(8,128)(2,1)S(1)}, bf16[2,8,64,128]{3,2,1,0:T(8,128)(2,1)S(1)}, u32[]{:S(2)}, u32[]{:S(2)}) collective-permute-start(bf16[2,8,64,128]{3,2,1,0:T(8,128)(2,1)S(1)} %get-tuple-element.41), channel_id=1, source_target_pairs={{48,0},{96,48},{144,96},{192,144},{240,192},{288,240},{336,288},{3... | collective-permute-start | bytes 786440 | tf_op jit(solution)/shard_map/ppermute | solution.py:19
  80.0 0.0 copy-done.3
  80.0 0.8 coarse_solve.1
  80.9 0.0 collective-permute-done.6.above_ref
  80.9 0.0 collective-permute-done.7.below_ref
  80.9 0.1 fold_sides.1
  80.9 7.2 %all-to-all-start.1 = ((bf16[16,32,128]{2,1,0:T(8,128)(2,1)}), bf16[16,32,128]{2,1,0:T(8,128)(2,1)S(1)}, u32[]{:S(2)}, u32[]{:S(2)}) async-start(bf16[16,32,128]{2,1,0:T(8,128)(2,1)} %coarse_solve.1), calls=%async_computation.1 | async-start | bytes 262144 | tf_op jit(solution)/shard_map/all_to_all | solution.py:422
  88.2 7.8 %collective-permute-start.10 = (bf16[4,2,64,128]{3,2,1,0:T(8,128)(2,1)S(1)}, bf16[4,2,64,128]{3,2,1,0:T(8,128)(2,1)S(1)}, u32[]{:S(2)}, u32[]{:S(2)}) collective-permute-start(bf16[4,2,64,128]{3,2,1,0:T(8,128)(2,1)S(1)} %get-tuple-element.42), channel_id=1, source_target_pairs={{0,1},{1,2},{2,3},{3,4},{4,5},{5,6},{6,7},{7,8},{8,9},{9,10},{10,1... | collective-permute-start | bytes 393224 | tf_op jit(solution)/shard_map/ppermute | solution.py:19
  96.0 1.9 %collective-permute-start.11 = (bf16[4,2,64,128]{3,2,1,0:T(8,128)(2,1)S(1)}, bf16[4,2,64,128]{3,2,1,0:T(8,128)(2,1)S(1)}, u32[]{:S(2)}, u32[]{:S(2)}) collective-permute-start(bf16[4,2,64,128]{3,2,1,0:T(8,128)(2,1)S(1)} %get-tuple-element.37), channel_id=1, source_target_pairs={{1,0},{2,1},{3,2},{4,3},{5,4},{6,5},{7,6},{8,7},{9,8},{10,9},{11,1... | collective-permute-start | bytes 393224 | tf_op jit(solution)/shard_map/ppermute | solution.py:19
  97.9 0.0 collective-permute-done.8.above_ref
  97.9 0.0 collective-permute-done.9.below_ref
  97.9 1.1 %collective-permute-done.10.left_ref = bf16[4,2,64,128]{3,2,1,0:T(8,128)(2,1)S(1)} collective-permute-done((bf16[4,2,64,128]{3,2,1,0:T(8,128)(2,1)S(1)}, bf16[4,2,64,128]{3,2,1,0:T(8,128)(2,1)S(1)}, u32[]{:S(2)}, u32[]{:S(2)}) %collective-permute-start.10) | collective-permute-done | bytes 131104 | tf_op jit(solution)/shard_map/ppermute | solution.py:19
  99.0 8.0 %collective-permute-done.11.right_ref = bf16[4,2,64,128]{3,2,1,0:T(8,128)(2,1)S(1)} collective-permute-done((bf16[4,2,64,128]{3,2,1,0:T(8,128)(2,1)S(1)}, bf16[4,2,64,128]{3,2,1,0:T(8,128)(2,1)S(1)}, u32[]{:S(2)}, u32[]{:S(2)}) %collective-permute-start.11) | collective-permute-done | bytes 131104 | tf_op jit(solution)/shard_map/ppermute | solution.py:19
  107.1 0.0 all-to-all-done.1
  107.1 0.0 copy-done.5
  107.1 1.8 %join.1 = f32[4,8,64,128]{3,2,1,0:T(8,128)} custom-call(s32[1,1]{1,0:T(1,128)S(6)} %copy.7.live_ref, s32[4,8]{1,0:T(4,128)S(1)} %copy-done.5, bf16[512,128]{1,0:T(8,128)(2,1)S(1)} %bitcast.8, bf16[4,8,64,128]{3,2,1,0:T(8,128)(2,1)S(1)} %get-tuple-element.39.center_ref, bf16[2,8,64,128]{3,2,1,0:T(8,128)(2,1)S(1)} %collective-permute-done.8.above_ref, ...), custom_call_target="tpu_custom_call" | custom-call | flops 2097152 | bytes 2621440 | tf_op jit(solution)/shard_map/join/pallas_call | solution.py:377
  (1 shorter events, 0.0 us)
Async XLA Ops:
  0.7 1.0 copy-start.1
  1.7 78.3 %copy-start.3 = (f32[32,32]{1,0:T(8,128)S(1)}, f32[32,32]{1,0:T(8,128)}, u32[]{:S(2)}) copy-start(f32[32,32]{1,0:T(8,128)} %inverse_ref.1) | copy-start | bytes 12292
  1.9 25.0 %collective-permute-start = (bf16[4,2,64,128]{3,2,1,0:T(8,128)(2,1)S(1)}, bf16[4,2,64,128]{3,2,1,0:T(8,128)(2,1)S(1)}, u32[]{:S(2)}, u32[]{:S(2)}) collective-permute-start(bf16[4,2,64,128]{3,2,1,0:T(8,128)(2,1)S(1)} %get-tuple-element.24), channel_id=1, source_target_pairs={{0,1},{1,2},{2,3},{3,4},{4,5},{5,6},{6,7},{7,8},{8,9},{9,10},{10,1... | collective-permute-start | bytes 393224 | tf_op jit(solution)/shard_map/ppermute | solution.py:19
  9.7 17.1 %collective-permute-start.1 = (bf16[4,2,64,128]{3,2,1,0:T(8,128)(2,1)S(1)}, bf16[4,2,64,128]{3,2,1,0:T(8,128)(2,1)S(1)}, u32[]{:S(2)}, u32[]{:S(2)}) collective-permute-start(bf16[4,2,64,128]{3,2,1,0:T(8,128)(2,1)S(1)} %get-tuple-element.25), channel_id=1, source_target_pairs={{1,0},{2,1},{3,2},{4,3},{5,4},{6,5},{7,6},{8,7},{9,8},{10,9},{11,1... | collective-permute-start | bytes 393224 | tf_op jit(solution)/shard_map/ppermute | solution.py:19
  11.6 36.5 %collective-permute-start.3 = (bf16[2,8,64,128]{3,2,1,0:T(8,128)(2,1)S(1)}, bf16[2,8,64,128]{3,2,1,0:T(8,128)(2,1)S(1)}, u32[]{:S(2)}, u32[]{:S(2)}) collective-permute-start(bf16[2,8,64,128]{3,2,1,0:T(8,128)(2,1)S(1)} %get-tuple-element.30.bottom), channel_id=1, source_target_pairs={{0,48},{48,96},{96,144},{144,192},{192,240},{240,288},{288,336},{3... | collective-permute-start | bytes 786440 | tf_op jit(solution)/shard_map/ppermute | solution.py:19
  13.6 34.6 %collective-permute-start.4 = (bf16[2,8,64,128]{3,2,1,0:T(8,128)(2,1)S(1)}, bf16[2,8,64,128]{3,2,1,0:T(8,128)(2,1)S(1)}, u32[]{:S(2)}, u32[]{:S(2)}) collective-permute-start(bf16[2,8,64,128]{3,2,1,0:T(8,128)(2,1)S(1)} %get-tuple-element.31.top), channel_id=1, source_target_pairs={{48,0},{96,48},{144,96},{192,144},{240,192},{288,240},{336,288},{3... | collective-permute-start | bytes 786440 | tf_op jit(solution)/shard_map/ppermute | solution.py:19
  23.2 1.0 copy-start.2
  24.3 0.7 copy-start.4
  26.8 80.3 %copy-start.5 = (s32[4,8]{1,0:T(4,128)S(1)}, s32[4,8]{1,0:T(4,128)}, u32[]{:S(2)}) copy-start(s32[4,8]{1,0:T(4,128)} %agg_ref.3) | copy-start | bytes 388
  26.9 19.5 %all-to-all-start = ((bf16[16,32,128]{2,1,0:T(8,128)(2,1)}), bf16[16,32,128]{2,1,0:T(8,128)(2,1)S(1)}, u32[]{:S(2)}, u32[]{:S(2)}) async-start(bf16[16,32,128]{2,1,0:T(8,128)(2,1)} %partial_sums.1), calls=%async_computation | async-start | bytes 262144 | tf_op jit(solution)/shard_map/all_to_all | solution.py:407
  34.1 12.3 %collective-permute-start.2 = (bf16[2,4,64,128]{3,2,1,0:T(8,128)(2,1)S(1)}, bf16[2,4,64,128]{3,2,1,0:T(8,128)(2,1)S(1)}, u32[]{:S(2)}, u32[]{:S(2)}) collective-permute-start(bf16[2,4,64,128]{3,2,1,0:T(8,128)(2,1)S(1)} %get-tuple-element.26), channel_id=1, source_target_pairs={{0,48},{48,96},{96,144},{144,192},{192,240},{240,288},{288,336},{3... | collective-permute-start | bytes 393224 | tf_op jit(solution)/shard_map/ppermute | solution.py:19
  36.1 12.0 %collective-permute-start.5 = (bf16[2,4,64,128]{3,2,1,0:T(8,128)(2,1)S(1)}, bf16[2,4,64,128]{3,2,1,0:T(8,128)(2,1)S(1)}, u32[]{:S(2)}, u32[]{:S(2)}) collective-permute-start(bf16[2,4,64,128]{3,2,1,0:T(8,128)(2,1)S(1)} %get-tuple-element.27), channel_id=1, source_target_pairs={{48,0},{96,48},{144,96},{192,144},{240,192},{288,240},{336,288},{3... | collective-permute-start | bytes 393224 | tf_op jit(solution)/shard_map/ppermute | solution.py:19
  48.2 1.9 %copy-start = (bf16[1,96,64,256]{3,2,1,0:T(8,128)(2,1)S(1)}, bf16[1,96,64,256]{3,2,1,0:T(8,128)(2,1)}, u32[]{:S(2)}) copy-start(bf16[1,96,64,256]{3,2,1,0:T(8,128)(2,1)} %param.7) | copy-start | bytes 9437188
  50.1 0.7 copy-start.6
  56.7 24.2 %collective-permute-start.6 = (bf16[2,4,64,128]{3,2,1,0:T(8,128)(2,1)S(1)}, bf16[2,4,64,128]{3,2,1,0:T(8,128)(2,1)S(1)}, u32[]{:S(2)}, u32[]{:S(2)}) collective-permute-start(bf16[2,4,64,128]{3,2,1,0:T(8,128)(2,1)S(1)} %get-tuple-element.35), channel_id=1, source_target_pairs={{0,48},{48,96},{96,144},{144,192},{192,240},{240,288},{288,336},{3... | collective-permute-start | bytes 393224 | tf_op jit(solution)/shard_map/ppermute | solution.py:19
  58.6 22.2 %collective-permute-start.7 = (bf16[2,4,64,128]{3,2,1,0:T(8,128)(2,1)S(1)}, bf16[2,4,64,128]{3,2,1,0:T(8,128)(2,1)S(1)}, u32[]{:S(2)}, u32[]{:S(2)}) collective-permute-start(bf16[2,4,64,128]{3,2,1,0:T(8,128)(2,1)S(1)} %get-tuple-element.36), channel_id=1, source_target_pairs={{48,0},{96,48},{144,96},{192,144},{240,192},{288,240},{336,288},{3... | collective-permute-start | bytes 393224 | tf_op jit(solution)/shard_map/ppermute | solution.py:19
  68.4 29.5 %collective-permute-start.8 = (bf16[2,8,64,128]{3,2,1,0:T(8,128)(2,1)S(1)}, bf16[2,8,64,128]{3,2,1,0:T(8,128)(2,1)S(1)}, u32[]{:S(2)}, u32[]{:S(2)}) collective-permute-start(bf16[2,8,64,128]{3,2,1,0:T(8,128)(2,1)S(1)} %get-tuple-element.40), channel_id=1, source_target_pairs={{0,48},{48,96},{96,144},{144,192},{192,240},{240,288},{288,336},{3... | collective-permute-start | bytes 786440 | tf_op jit(solution)/shard_map/ppermute | solution.py:19
  70.4 27.6 %collective-permute-start.9 = (bf16[2,8,64,128]{3,2,1,0:T(8,128)(2,1)S(1)}, bf16[2,8,64,128]{3,2,1,0:T(8,128)(2,1)S(1)}, u32[]{:S(2)}, u32[]{:S(2)}) collective-permute-start(bf16[2,8,64,128]{3,2,1,0:T(8,128)(2,1)S(1)} %get-tuple-element.41), channel_id=1, source_target_pairs={{48,0},{96,48},{144,96},{192,144},{240,192},{288,240},{336,288},{3... | collective-permute-start | bytes 786440 | tf_op jit(solution)/shard_map/ppermute | solution.py:19
  80.9 26.1 %all-to-all-start.1 = ((bf16[16,32,128]{2,1,0:T(8,128)(2,1)}), bf16[16,32,128]{2,1,0:T(8,128)(2,1)S(1)}, u32[]{:S(2)}, u32[]{:S(2)}) async-start(bf16[16,32,128]{2,1,0:T(8,128)(2,1)} %coarse_solve.1), calls=%async_computation.1 | async-start | bytes 262144 | tf_op jit(solution)/shard_map/all_to_all | solution.py:422
  88.2 10.9 %collective-permute-start.10 = (bf16[4,2,64,128]{3,2,1,0:T(8,128)(2,1)S(1)}, bf16[4,2,64,128]{3,2,1,0:T(8,128)(2,1)S(1)}, u32[]{:S(2)}, u32[]{:S(2)}) collective-permute-start(bf16[4,2,64,128]{3,2,1,0:T(8,128)(2,1)S(1)} %get-tuple-element.42), channel_id=1, source_target_pairs={{0,1},{1,2},{2,3},{3,4},{4,5},{5,6},{6,7},{7,8},{8,9},{9,10},{10,1... | collective-permute-start | bytes 393224 | tf_op jit(solution)/shard_map/ppermute | solution.py:19
  96.0 11.1 %collective-permute-start.11 = (bf16[4,2,64,128]{3,2,1,0:T(8,128)(2,1)S(1)}, bf16[4,2,64,128]{3,2,1,0:T(8,128)(2,1)S(1)}, u32[]{:S(2)}, u32[]{:S(2)}) collective-permute-start(bf16[4,2,64,128]{3,2,1,0:T(8,128)(2,1)S(1)} %get-tuple-element.37), channel_id=1, source_target_pairs={{1,0},{2,1},{3,2},{4,3},{5,4},{6,5},{7,6},{8,7},{9,8},{10,9},{11,1... | collective-permute-start | bytes 393224 | tf_op jit(solution)/shard_map/ppermute | solution.py:19

commit v2 on v0

v2 whole, which is shorter than its diff:
```python
import jax
import jax.numpy as jnp
from jax import lax
from jax.experimental import pallas as pl
from jax.experimental.pallas import tpu as pltpu
from jax.sharding import PartitionSpec as P

BF16 = jnp.bfloat16
F32 = jnp.float32
MIB = 1 << 20
VMEM = pl.BlockSpec(memory_space=pltpu.VMEM)
SMEM = pl.BlockSpec(memory_space=pltpu.SMEM)


def swap_near(values, axis):
    count = lax.axis_size(axis)
    return lax.ppermute(values, axis, [(i, i ^ 1) for i in range(count) if i ^ 1 < count])


def swap_far(values, axis):
    count = lax.axis_size(axis)
    pairs = []
    for i in range(1, count - 1, 2):
        pairs += [(i, i + 1), (i + 1, i)]
    return lax.ppermute(values, axis, pairs)


def swap_bit(values, axis, bit):
    count = lax.axis_size(axis)
    return lax.ppermute(values, axis, [(i, i ^ bit) for i in range(count)])


def shaped(shape, dtype):
    return jax.ShapeDtypeStruct(shape, dtype)


def call(kernel, name, outs, ins, specs, out_specs, limit, flops=0, moved=0, scratch=()):
    return pl.pallas_call(
        kernel,
        out_shape=outs,
        in_specs=specs,
        out_specs=out_specs,
        scratch_shapes=list(scratch),
        cost_estimate=pl.CostEstimate(flops=flops, bytes_accessed=moved, transcendentals=0),
        compiler_params=pltpu.CompilerParams(vmem_limit_bytes=limit * MIB),
        name=name,
    )(*ins)


def parities(info_ref):
    return info_ref[1] % 2, info_ref[2] % 2


def mask_kernel(info_ref, residual_ref, near_ref, far_ref, cross_near, cross_far):
    rows, columns = residual_ref.shape[:2]
    half = rows // 2
    p, q = parities(info_ref)
    for out_ref, start in ((near_ref, half * (1 - p)), (far_ref, half * p)):
        for i in range(half):
            for j in range(columns):
                block = residual_ref[start + i, j]
                live = (start + i) * columns + j < info_ref[0]
                out_ref[i, j] = jnp.where(live, block, jnp.zeros_like(block))
    for out_ref, start in ((cross_near, (columns - 2) * (1 - q)), (cross_far, (columns - 2) * q)):
        for i in range(rows):
            for j in range(2):
                block = residual_ref[i, start + j]
                live = i * columns + start + j < info_ref[0]
                out_ref[i, j] = jnp.where(live, block, jnp.zeros_like(block))


def mask_blocks(info, residual):
    rows, columns, width, sides = residual.shape
    wide = shaped((rows // 2, columns, width, sides), BF16)
    tall = shaped((rows, 2, width, sides), BF16)
    return call(
        mask_kernel, "mask_blocks", (wide, wide, tall, tall), (info, residual),
        [SMEM, VMEM], (VMEM,) * 4, 4, moved=4 * residual.size,
    )


def payload_kernel(info_ref, agg_ref, near_ref, far_ref, inverse_ref, out_ref):
    unknowns, sides = near_ref.shape
    rows, columns = agg_ref.shape
    half = rows * columns * 2
    size = inverse_ref.shape[0]
    cells = unknowns // half
    p, _ = parities(info_ref)
    row = lax.broadcasted_iota(jnp.int32, (half, unknowns), 0)
    column = lax.broadcasted_iota(jnp.int32, (half, unknowns), 1)
    picks = jnp.where(column // cells == row, 1.0, 0.0).astype(BF16)
    for source, start in ((near_ref, half * (1 - p)), (far_ref, half * p)):
        sums = jnp.dot(picks, source[...], preferred_element_type=F32)
        out_ref[pl.ds(pl.multiple_of(start, half), half), :] = sums.astype(BF16)
    row = lax.broadcasted_iota(jnp.int32, (size, sides), 0)
    column = lax.broadcasted_iota(jnp.int32, (size, sides), 1)
    rest = inverse_ref[...]
    tail = jnp.zeros((size, sides), F32)
    for term in range(3):
        part = rest.astype(BF16)
        rest = rest - part.astype(F32)
        place = jnp.where(column == row + term * size, 1.0, 0.0).astype(BF16)
        tail = tail + jnp.dot(part, place, preferred_element_type=F32)
    lane = lax.broadcasted_iota(jnp.int32, (1, sides), 1) - 3 * size
    labels = jnp.zeros((1, sides), F32)
    for i in range(rows):
        for j in range(columns):
            labels = jnp.where(lane == i * columns + j, agg_ref[i, j].astype(F32), labels)
    out_ref[pl.ds(2 * half, size), :] = (tail + labels).astype(BF16)


def payload_of(info, agg, near, far, inverse):
    sides = near.shape[-1]
    rows, columns = agg.shape
    flat = (near.size // sides, sides)
    count = rows * columns * 4 + inverse.shape[0]
    return call(
        payload_kernel, "payload", shaped((1, count, sides), BF16),
        (info, agg, near.reshape(flat), far.reshape(flat), inverse),
        [SMEM, SMEM, VMEM, VMEM, VMEM], pl.BlockSpec((None, count, sides), lambda: (0, 0, 0)),
        6, flops=1 << 25, moved=4 * near.size,
    )


def join_pair_kernel(first_ref, second_ref, out_ref):
    count = first_ref.shape[0]
    out_ref[:count] = first_ref[...]
    out_ref[count:] = second_ref[...]


def join_pair(first, second):
    count = first.shape[0]
    return call(
        join_pair_kernel, "join_pair", shaped((2 * count,) + first.shape[1:], BF16),
        (first, second), [VMEM, VMEM], VMEM, 3, moved=8 * first.size,
    )


def corners_kernel(info_ref, cross_near, cross_far, near_ref, far_ref):
    half = near_ref.shape[0]
    p, _ = parities(info_ref)
    for out_ref, start in ((near_ref, half * (1 - p)), (far_ref, half * p)):
        for i in range(half):
            for j in range(2):
                out_ref[i, j] = cross_near[start + i, j]
                out_ref[i, 2 + j] = cross_far[start + i, j]


def corners(info, cross_near, cross_far):
    rows, _, width, sides = cross_near.shape
    piece = shaped((rows // 2, 4, width, sides), BF16)
    return call(
        corners_kernel, "corners", (piece, piece), (info, cross_near, cross_far),
        [SMEM, VMEM, VMEM], (VMEM, VMEM), 2, moved=8 * cross_near.size,
    )


def fix_of(pattern_ref, blocks_ref, grid_ref, n):
    picked = jnp.concatenate([grid_ref[pattern_ref[k, n]] for k in range(4)], axis=0)
    return jnp.dot(blocks_ref[n], picked, preferred_element_type=F32).astype(BF16)


def margin_kernel(
    info_ref, pattern_ref, blocks_ref,
    own_near, own_far, got_near, got_far, cross_near, cross_far, corner_near, corner_far,
    main_near, main_far, out_near, out_far, grid_ref,
):
    half, columns = own_near.shape[:2]
    rows = 2 * half
    wide = columns + 4
    p, q = parities(info_ref)
    near_row, far_row = (rows + 2) * (1 - p), (rows + 2) * p
    near_column, far_column = (columns + 2) * (1 - q), (columns + 2) * q
    for source, start in (
        (own_near, 2 + half * (1 - p)), (own_far, 2 + half * p),
        (got_near, near_row), (got_far, far_row),
    ):
        for i in range(2):
            for j in range(columns):
                grid_ref[(start + i) * wide + 2 + j] = source[i, j]
    for source, start in ((cross_near, near_column), (cross_far, far_column)):
        for i in range(rows):
            for j in range(2):
                grid_ref[(2 + i) * wide + start + j] = source[i, j]
    for source, start in ((corner_near, near_row), (corner_far, far_row)):
        for i in range(2):
            for j in range(2):
                grid_ref[(start + i) * wide + near_column + j] = source[i, j]
                grid_ref[(start + i) * wide + far_column + j] = source[i, 2 + j]
    for main, corner, start in ((main_near, out_near, near_row), (main_far, out_far, far_row)):
        for i in range(2):
            base = (start + i) * wide
            for j in range(2):
                corner[i, j] = fix_of(pattern_ref, blocks_ref, grid_ref, base + near_column + j)
                corner[i, 2 + j] = fix_of(pattern_ref, blocks_ref, grid_ref, base + far_column + j)
            for j in range(columns):
                main[i, j] = fix_of(pattern_ref, blocks_ref, grid_ref, base + 2 + j)


def margin_fixes(info, pattern, blocks, pieces):
    count, width, depth = blocks.shape
    half, columns, _, sides = pieces[0].shape
    main = shaped((2, columns, width, sides), BF16)
    corner = shaped((2, 4, width, sides), BF16)
    grid = shaped((count, width, sides), BF16)
    return call(
        margin_kernel, "margin_fixes", (main, main, corner, corner, grid),
        (info, pattern, blocks) + pieces, [SMEM, SMEM] + [VMEM] * 9, (VMEM,) * 5, 12,
        flops=blocks.size * sides, moved=2 * blocks.size,
    )


def center_kernel(info_ref, pattern_ref, blocks_ref, grid_ref, side_near, side_far, center_ref):
    rows, columns = center_ref.shape[:2]
    wide = columns + 4
    _, q = parities(info_ref)
    near_column, far_column = (columns + 2) * (1 - q), (columns + 2) * q
    for i in range(rows):
        base = (2 + i) * wide
        for j in range(2):
            side_near[i, j] = fix_of(pattern_ref, blocks_ref, grid_ref, base + near_column + j)
            side_far[i, j] = fix_of(pattern_ref, blocks_ref, grid_ref, base + far_column + j)
        for j in range(columns):
            center_ref[i, j] = fix_of(pattern_ref, blocks_ref, grid_ref, base + 2 + j)


def center_fixes(info, pattern, blocks, grid, rows, columns):
    _, width, sides = grid.shape
    side = shaped((rows, 2, width, sides), BF16)
    return call(
        center_kernel, "center_fixes",
        (side, side, shaped((rows, columns, width, sides), BF16)),
        (info, pattern, blocks, grid), [SMEM, SMEM, VMEM, VMEM], (VMEM,) * 3, 12,
        flops=blocks.size * sides, moved=2 * blocks.size,
    )


def fold_kernel(info_ref, side_near, side_far, corner_near, corner_far, out_near, out_far):
    half = corner_near.shape[0]
    p, _ = parities(info_ref)
    for source, start in ((corner_near, half * (1 - p)), (corner_far, half * p)):
        for i in range(half):
            for j in range(2):
                for side, out, at in ((side_near, out_near, j), (side_far, out_far, 2 + j)):
                    total = side[start + i, j].astype(F32) + source[i, at].astype(F32)
                    out[start + i, j] = total.astype(BF16)


def fold_sides(info, side_near, side_far, corner_near, corner_far):
    piece = shaped(side_near.shape, BF16)
    return call(
        fold_kernel, "fold_sides", (piece, piece),
        (info, side_near, side_far, corner_near, corner_far),
        [SMEM] + [VMEM] * 4, (VMEM, VMEM), 2, flops=2 * side_near.size, moved=12 * side_near.size,
    )


def split_dot(left, right):
    high = right.astype(BF16)
    low = (right - high.astype(F32)).astype(BF16)
    return jnp.dot(left, high, preferred_element_type=F32) + jnp.dot(
        left, low, preferred_element_type=F32
    )


def solve_kernel(bits, info_ref, agg_ref, first_ref, second_ref, out_ref, sums, coarse):
    count, height, sides = first_ref.shape
    rows, columns = agg_ref.shape
    fields = rows * columns * 4
    size = height - fields
    total = sums.shape[0]
    row = lax.broadcasted_iota(jnp.int32, (sides, fields), 0)
    column = lax.broadcasted_iota(jnp.int32, (sides, fields), 1)
    repeat = jnp.where(row - 3 * size == column // 4, 1.0, 0.0).astype(BF16)
    row = lax.broadcasted_iota(jnp.int32, (total, fields), 0)
    column = lax.broadcasted_iota(jnp.int32, (total, fields), 1)
    same_field = row % 4 == column % 4
    owner = (row // 4).astype(F32)
    for part, source in enumerate((first_ref, second_ref)):
        for k in range(count):
            tail = source[k, pl.ds(fields, 16), :]
            labels = jnp.dot(tail, repeat, preferred_element_type=F32)[:1]
            onehot = jnp.where(same_field & (owner == labels), 1.0, 0.0).astype(BF16)
            found = jnp.dot(
                onehot, source[k, pl.ds(0, fields), :], preferred_element_type=F32
            )
            if part == 0 and k == 0:
                sums[...] = found
            else:
                sums[...] += found
    for part, source in enumerate((first_ref, second_ref)):
        for k in range(count):
            slot, flips = part * count + k, 0
            for i, bit in enumerate(bits):
                if slot >> i & 1:
                    flips |= bit
            start = pl.multiple_of((info_ref[1] ^ flips) * size, size)
            mine = sums[pl.ds(start, size), :]
            stacked = jnp.concatenate([mine, mine, mine, jnp.zeros_like(mine)], axis=0)
            coarse[pl.ds(start, size), :] = split_dot(
                source[k, pl.ds(fields, size), :], stacked
            )
    row = lax.broadcasted_iota(jnp.int32, (fields, 1), 0)
    labels = jnp.zeros((fields, 1), jnp.int32)
    for i in range(rows):
        for j in range(columns):
            labels = jnp.where(row // 4 == i * columns + j, agg_ref[i, j], labels)
    row = lax.broadcasted_iota(jnp.int32, (fields, total), 0)
    column = lax.broadcasted_iota(jnp.int32, (fields, total), 1)
    onehot = jnp.where((column // 4 == labels) & (column % 4 == row % 4), 1.0, 0.0)
    out_ref[...] = split_dot(onehot.astype(BF16), coarse[...])


def coarse_values(bits, info, agg, first, second):
    count, height, sides = first.shape
    fields = agg.size * 4
    total = 2 * count * (height - fields)

    def kernel(*refs):
        solve_kernel(bits, *refs)

    return call(
        kernel, "coarse_values", shaped((fields, sides), F32), (info, agg, first, second),
        [SMEM, SMEM, VMEM, VMEM], VMEM, 8, flops=1 << 28, moved=4 * first.size,
        scratch=[pltpu.VMEM((total, sides), F32), pltpu.VMEM((total, sides), F32)],
    )


def join_kernel(
    info_ref, lifted_ref, center_ref, main_near, main_far, cross_near, cross_far, out_ref
):
    rows, columns, width, sides = center_ref.shape
    half = rows // 2
    cells = width // 4
    p, q = parities(info_ref)
    for i in range(rows):
        for j in range(columns):
            block = i * columns + j
            lifted = jnp.concatenate(
                [
                    jnp.broadcast_to(lifted_ref[pl.ds(block * 4 + f, 1), :], (cells, sides))
                    for f in range(4)
                ],
                axis=0,
            )
            out_ref[i, j] = center_ref[i, j].astype(F32) + lifted
    for source, start in ((main_near, half * (1 - p)), (main_far, half * p)):
        for i in range(half):
            for j in range(columns):
                out_ref[start + i, j] += source[i, j].astype(F32)
    for source, start in ((cross_near, (columns - 2) * (1 - q)), (cross_far, (columns - 2) * q)):
        for i in range(rows):
            for j in range(2):
                out_ref[i, start + j] += source[i, j].astype(F32)
    for i in range(rows):
        for j in range(columns):

            @pl.when(i * columns + j >= info_ref[0])
            def _(i=i, j=j):
                out_ref[i, j] = jnp.zeros((width, sides), F32)


def join(info, lifted, center, main_near, main_far, cross_near, cross_far):
    return call(
        join_kernel, "join", shaped(center.shape, F32),
        (info, lifted, center, main_near, main_far, cross_near, cross_far),
        [SMEM] + [VMEM] * 6, VMEM, 6, flops=8 * center.size, moved=10 * center.size,
    )


def body(residual, approx_inverse, pattern, live_blocks, block_aggregate, coarse_inverse):
    rows, columns = residual.shape[:2]
    info = jnp.stack([live_blocks[0, 0], lax.axis_index("stream"), lax.axis_index("cross")])
    own_near, own_far, edge_near, edge_far = mask_blocks(info, residual)
    bits = []
    while 2 << len(bits) <= lax.axis_size("stream"):
        bits.insert(0, 1 << len(bits))

    gathered = payload_of(info, block_aggregate, own_near, own_far, coarse_inverse)
    got_far = swap_far(own_far, "stream")
    got_near = swap_near(own_near, "stream")
    cross_far = swap_far(edge_far, "cross")
    cross_near = swap_near(edge_near, "cross")
    blocks, links = approx_inverse[0], jnp.transpose(pattern[0])
    got_far, got_near, cross_far, cross_near, blocks, gathered = lax.optimization_barrier(
        (got_far, got_near, cross_far, cross_near, blocks, gathered)
    )
    blocks = jnp.where(info[0] > 0, blocks, jnp.zeros((), BF16))
    corner_near, corner_far = corners(info, cross_near, cross_far)
    other = swap_bit(gathered, "stream", bits[0])
    corner_far = swap_far(corner_far, "stream")
    corner_near = swap_near(corner_near, "stream")
    gathered = join_pair(gathered, other)
    other = swap_bit(gathered, "stream", bits[1])
    gathered, corner_far, corner_near = lax.optimization_barrier(
        (gathered, corner_far, corner_near)
    )
    pieces = (own_near, own_far, got_near, got_far, cross_near, cross_far, corner_near, corner_far)
    main_near, main_far, corner_near, corner_far, grid = margin_fixes(info, links, blocks, pieces)
    corner_far, other = lax.optimization_barrier((corner_far, other))
    gathered = join_pair(gathered, other)
    corner_far = swap_far(corner_far, "stream")
    corner_near = swap_near(corner_near, "stream")
    other = swap_bit(gathered, "stream", bits[2])
    side_near, side_far, center = center_fixes(info, links, blocks, grid, rows, columns)
    side_near, other = lax.optimization_barrier((side_near, other))
    for bit in bits[3:]:
        gathered = join_pair(gathered, other)
        other = swap_bit(gathered, "stream", bit)
    gathered, corner_near, corner_far = lax.optimization_barrier(
        (gathered, corner_near, corner_far)
    )
    side_near, side_far = fold_sides(info, side_near, side_far, corner_near, corner_far)
    side_near, side_far, main_far, main_near = lax.optimization_barrier(
        (side_near, side_far, main_far, main_near)
    )
    main_far = swap_far(main_far, "stream")
    main_near = swap_near(main_near, "stream")
    cross_far = swap_far(side_far, "cross")
    cross_near = swap_near(side_near, "cross")
    lifted = coarse_values(bits, info, block_aggregate, gathered, other)
    return join(info, lifted, center, main_near, main_far, cross_near, cross_far)


def solution(mesh):
    placed = (
        P("stream", "cross", None, None),
        P("stream", "cross", None, None),
        P("stream", "cross", None),
        P("stream", "cross"),
        P("stream", "cross"),
        P("stream", "cross"),
    )
    return jax.shard_map(
        body,
        mesh=mesh,
        in_specs=placed,
        out_specs=P("stream", "cross", None, None),
        check_vma=False,
    )
```

time: 231 us -> 86.1 us (0.37)
  the two profiles are of different devices: /device:TPU:73 before, /device:TPU:504 now
where the time goes in v2:
time: 86.1 us; the launch traced here: 85.4 us
  starting transfers between devices  55.7 us (65%)
  waiting for transfers between devices  13.7 us (16%)
  Pallas kernels  10.5 us (12%)
  local copies, waits for them, and re-layouts  2.45 us (3%)
  other arithmetic  2.18 us (3%)
  between operations  0.96 us (1%)
    ppermute x6, starting transfers between devices, swap_far(): return lax.ppermute(values, axis, pairs)  31.1 us
    ppermute x6, starting transfers between devices, swap_near(): lax.ppermute(values, axis, [(i, i ^ 1) for i in range(count) if i ^ 1 < c...  14.5 us
    ppermute x6, waiting for transfers between devices, swap_far(): return lax.ppermute(values, axis, pairs)  11.5 us
    pallas_call x11, Pallas kernels, call(): pl.pallas_call(kernel, out_shape=outs, in_specs=specs, out_specs=out_spec...  10.5 us
    ppermute x4, starting transfers between devices, swap_bit(): return lax.ppermute(values, axis, [(i, i ^ bit) for i in range(count)])  10 us
    unnamed x10, local copies, waits for them, and re-layouts  2.45 us
    select_n x1, other arithmetic, body(): blocks = jnp.where(info[0] > 0, blocks, jnp.zeros((), BF16))  2.1 us
  transfers between devices with their start and end apart: 16, of which 5 were waited for; matrix products, arithmetic and copies ran while one was open for 2% of the time, Pallas kernels for 9%

profile of v2, /device:TPU:504, one launch (start us, length us, event | category | flops | bytes accessed | tf_op | source)
XLA Modules:
  0.0 85.4 jit_solution(12718086545467091381)
XLA Ops:
  0.7 0.1 pad_add_fusion.info_ref.refs_0_
  0.7 0.0 copy-start
  0.7 1.0 %copy-done = bf16[4,8,64,128]{3,2,1,0:T(8,128)(2,1)S(1)} copy-done((bf16[4,8,64,128]{3,2,1,0:T(8,128)(2,1)S(1)}, bf16[4,8,64,128]{3,2,1,0:T(8,128)(2,1)}, u32[]{:S(2)}) %copy-start) | copy-done | bytes 524312
  1.8 0.7 mask_blocks.1
  2.5 6.3 %collective-permute-start = (bf16[2,8,64,128]{3,2,1,0:T(8,128)(2,1)S(1)}, bf16[2,8,64,128]{3,2,1,0:T(8,128)(2,1)S(1)}, u32[]{:S(2)}, u32[]{:S(2)}) collective-permute-start(bf16[2,8,64,128]{3,2,1,0:T(8,128)(2,1)S(1)} %get-tuple-element.41.own_far), channel_id=1, source_target_pairs={{48,96},{96,48},{144,192},{192,144},{240,288},{288,240},{336,384},... | collective-permute-start | bytes 786440 | tf_op jit(solution)/shard_map/ppermute | solution.py:25
  8.9 1.9 %collective-permute-start.1 = (bf16[2,8,64,128]{3,2,1,0:T(8,128)(2,1)S(1)}, bf16[2,8,64,128]{3,2,1,0:T(8,128)(2,1)S(1)}, u32[]{:S(2)}, u32[]{:S(2)}) collective-permute-start(bf16[2,8,64,128]{3,2,1,0:T(8,128)(2,1)S(1)} %get-tuple-element.42.own_near), channel_id=1, source_target_pairs={{0,48},{48,0},{96,144},{144,96},{192,240},{240,192},{288,336},{336... | collective-permute-start | bytes 786440 | tf_op jit(solution)/shard_map/ppermute | solution.py:17
  10.8 3.0 %collective-permute-start.2 = (bf16[4,2,64,128]{3,2,1,0:T(8,128)(2,1)S(1)}, bf16[4,2,64,128]{3,2,1,0:T(8,128)(2,1)S(1)}, u32[]{:S(2)}, u32[]{:S(2)}) collective-permute-start(bf16[4,2,64,128]{3,2,1,0:T(8,128)(2,1)S(1)} %get-tuple-element.43), channel_id=1, source_target_pairs={{1,2},{2,1},{3,4},{4,3},{5,6},{6,5},{7,8},{8,7},{9,10},{10,9},{11,... | collective-permute-start | bytes 393224 | tf_op jit(solution)/shard_map/ppermute | solution.py:25
  13.9 1.9 %collective-permute-start.3 = (bf16[4,2,64,128]{3,2,1,0:T(8,128)(2,1)S(1)}, bf16[4,2,64,128]{3,2,1,0:T(8,128)(2,1)S(1)}, u32[]{:S(2)}, u32[]{:S(2)}) collective-permute-start(bf16[4,2,64,128]{3,2,1,0:T(8,128)(2,1)S(1)} %get-tuple-element.44), channel_id=1, source_target_pairs={{0,1},{1,0},{2,3},{3,2},{4,5},{5,4},{6,7},{7,6},{8,9},{9,8},{10,11... | collective-permute-start | bytes 393224 | tf_op jit(solution)/shard_map/ppermute | solution.py:17
  15.8 0.0 copy-start.1
  15.8 0.7 copy-done.1
  16.5 0.0 copy-start.3
  16.5 0.7 copy-done.3
  17.2 0.8 payload.1.first_ref
  18.0 4.7 %collective-permute-done.2.cross_far = bf16[4,2,64,128]{3,2,1,0:T(8,128)(2,1)S(1)} collective-permute-done((bf16[4,2,64,128]{3,2,1,0:T(8,128)(2,1)S(1)}, bf16[4,2,64,128]{3,2,1,0:T(8,128)(2,1)S(1)}, u32[]{:S(2)}, u32[]{:S(2)}) %collective-permute-start.2) | collective-permute-done | bytes 131104 | tf_op jit(solution)/shard_map/ppermute | solution.py:25
  22.7 1.5 %collective-permute-done.3.cross_near = bf16[4,2,64,128]{3,2,1,0:T(8,128)(2,1)S(1)} collective-permute-done((bf16[4,2,64,128]{3,2,1,0:T(8,128)(2,1)S(1)}, bf16[4,2,64,128]{3,2,1,0:T(8,128)(2,1)S(1)}, u32[]{:S(2)}, u32[]{:S(2)}) %collective-permute-start.3) | collective-permute-done | bytes 131104 | tf_op jit(solution)/shard_map/ppermute | solution.py:17
  24.2 0.0 collective-permute-done.got_far
  24.2 0.0 collective-permute-done.1.got_near
  24.2 2.3 %collective-permute-start.4 = (bf16[1,160,128]{2,1,0:T(8,128)(2,1)S(1)}, bf16[1,160,128]{2,1,0:T(8,128)(2,1)S(1)}, u32[]{:S(2)}, u32[]{:S(2)}) collective-permute-start(bf16[1,160,128]{2,1,0:T(8,128)(2,1)S(1)} %payload.1.first_ref), channel_id=1, source_target_pairs={{0,384},{48,432},{96,480},{144,528},{192,576},{240,624},{288,672},... | collective-permute-start | bytes 122888 | tf_op jit(solution)/shard_map/ppermute | solution.py:30
  26.5 0.6 corners.1
  27.0 6.1 %collective-permute-start.5 = (bf16[2,4,64,128]{3,2,1,0:T(8,128)(2,1)S(1)}, bf16[2,4,64,128]{3,2,1,0:T(8,128)(2,1)S(1)}, u32[]{:S(2)}, u32[]{:S(2)}) collective-permute-start(bf16[2,4,64,128]{3,2,1,0:T(8,128)(2,1)S(1)} %get-tuple-element.48), channel_id=1, source_target_pairs={{48,96},{96,48},{144,192},{192,144},{240,288},{288,240},{336,384},... | collective-permute-start | bytes 393224 | tf_op jit(solution)/shard_map/ppermute | solution.py:25
  33.2 1.9 %collective-permute-start.6 = (bf16[2,4,64,128]{3,2,1,0:T(8,128)(2,1)S(1)}, bf16[2,4,64,128]{3,2,1,0:T(8,128)(2,1)S(1)}, u32[]{:S(2)}, u32[]{:S(2)}) collective-permute-start(bf16[2,4,64,128]{3,2,1,0:T(8,128)(2,1)S(1)} %get-tuple-element.49), channel_id=1, source_target_pairs={{0,48},{48,0},{96,144},{144,96},{192,240},{240,192},{288,336},{336... | collective-permute-start | bytes 393224 | tf_op jit(solution)/shard_map/ppermute | solution.py:17
  35.1 0.0 collective-permute-done.4.second_ref
  35.1 3.9 %collective-permute-start.7 = (bf16[2,160,128]{2,1,0:T(8,128)(2,1)S(1)}, bf16[2,160,128]{2,1,0:T(8,128)(2,1)S(1)}, u32[]{:S(2)}, u32[]{:S(2)}) collective-permute-start(bf16[2,160,128]{2,1,0:T(8,128)(2,1)S(1)} %join_pair.3.first_ref), channel_id=1, source_target_pairs={{0,192},{48,240},{96,288},{144,336},{192,0},{240,48},{288,96},{336... | collective-permute-start | bytes 245768 | tf_op jit(solution)/shard_map/ppermute | solution.py:30
  39.1 0.0 copy-start.2
  39.1 2.1 %broadcast_select_fusion.blocks_ref = bf16[96,64,256]{2,1,0:T(8,128)(2,1)S(1)} fusion(bf16[96,64,256]{2,1,0:T(8,128)(2,1)} %bitcast.15, pred[]{:T(512)} %bitcast.8), kind=kLoop, calls=%fused_computation | loop fusion | flops 1572864 | bytes 6291457 | tf_op jit(solution)/shard_map/jit(_where)/select_n | solution.py:388
  41.2 0.0 collective-permute-done.5.corner_far
  41.2 0.0 collective-permute-done.6.corner_near
  41.2 0.0 copy-done.2
  41.2 1.5 %margin_fixes.1 = (bf16[2,8,64,128]{3,2,1,0:T(8,128)(2,1)S(1)}, bf16[2,8,64,128]{3,2,1,0:T(8,128)(2,1)S(1)}, bf16[2,4,64,128]{3,2,1,0:T(8,128)(2,1)S(1)}, bf16[2...) custom-call(s32[3]{0:T(128)S(1)} %pad_add_fusion.info_ref.refs_0_, s32[4,96]{1,0:T(4,128)S(1)} %bitcast.13, ...), custom_call_target="tpu_custom_call" | custom-call | flops 201326592 | bytes 3145728 | tf_op jit(solution)/shard_map/margin_fixes/pallas_call | solution.py:38
  42.7 0.0 copy-start.4
  42.7 0.6 collective-permute-done.7.second_ref
  43.4 1.9 %collective-permute-start.8 = (bf16[4,160,128]{2,1,0:T(8,128)(2,1)S(1)}, bf16[4,160,128]{2,1,0:T(8,128)(2,1)S(1)}, u32[]{:S(2)}, u32[]{:S(2)}) collective-permute-start(bf16[4,160,128]{2,1,0:T(8,128)(2,1)S(1)} %join_pair.4.first_ref), channel_id=1, source_target_pairs={{0,96},{48,144},{96,0},{144,48},{192,288},{240,336},{288,192},{336... | collective-permute-start | bytes 491528 | tf_op jit(solution)/shard_map/ppermute | solution.py:30
  45.3 1.9 %collective-permute-start.9 = (bf16[2,4,64,128]{3,2,1,0:T(8,128)(2,1)S(1)}, bf16[2,4,64,128]{3,2,1,0:T(8,128)(2,1)S(1)}, u32[]{:S(2)}, u32[]{:S(2)}) collective-permute-start(bf16[2,4,64,128]{3,2,1,0:T(8,128)(2,1)S(1)} %get-tuple-element.61), channel_id=1, source_target_pairs={{0,48},{48,0},{96,144},{144,96},{192,240},{240,192},{288,336},{336... | collective-permute-start | bytes 393224 | tf_op jit(solution)/shard_map/ppermute | solution.py:17
  47.2 5.5 %collective-permute-start.10 = (bf16[2,4,64,128]{3,2,1,0:T(8,128)(2,1)S(1)}, bf16[2,4,64,128]{3,2,1,0:T(8,128)(2,1)S(1)}, u32[]{:S(2)}, u32[]{:S(2)}) collective-permute-start(bf16[2,4,64,128]{3,2,1,0:T(8,128)(2,1)S(1)} %get-tuple-element.62), channel_id=1, source_target_pairs={{48,96},{96,48},{144,192},{192,144},{240,288},{288,240},{336,384},... | collective-permute-start | bytes 393224 | tf_op jit(solution)/shard_map/ppermute | solution.py:25
  52.8 1.3 %center_fixes.1 = (bf16[4,2,64,128]{3,2,1,0:T(8,128)(2,1)S(1)}, bf16[4,2,64,128]{3,2,1,0:T(8,128)(2,1)S(1)}, bf16[4,8,64,128]{3,2,1,0:T(8,128)(2,1)S(1)}) custom-call(s32[3]{0:T(128)S(1)} %pad_add_fusion.info_ref.refs_0_, s32[4,96]{1,0:T(4,128)S(1)} %bitcast.14, bf16[96,64,256]{2,1,0:T(8,128)(2,1)S(1)} %broadcast_select_fusion.blocks_ref, ...), custom_call_target="tpu_custom_call" | custom-call | flops 201326592 | bytes 3145728 | tf_op jit(solution)/shard_map/center_fixes/pallas_call | solution.py:38
  54.0 0.0 collective-permute-done.8.second_ref
  54.1 1.9 %collective-permute-start.11 = (bf16[8,160,128]{2,1,0:T(8,128)(2,1)S(1)}, bf16[8,160,128]{2,1,0:T(8,128)(2,1)S(1)}, u32[]{:S(2)}, u32[]{:S(2)}) collective-permute-start(bf16[8,160,128]{2,1,0:T(8,128)(2,1)S(1)} %join_pair.5.refs_2_), channel_id=1, source_target_pairs={{0,48},{48,0},{96,144},{144,96},{192,240},{240,192},{288,336},{336... | collective-permute-start | bytes 983048 | tf_op jit(solution)/shard_map/ppermute | solution.py:30
  56.0 0.0 collective-permute-done.9.corner_near
  56.0 3.6 %collective-permute-done.10.corner_far = bf16[2,4,64,128]{3,2,1,0:T(8,128)(2,1)S(1)} collective-permute-done((bf16[2,4,64,128]{3,2,1,0:T(8,128)(2,1)S(1)}, bf16[2,4,64,128]{3,2,1,0:T(8,128)(2,1)S(1)}, u32[]{:S(2)}, u32[]{:S(2)}) %collective-permute-start.10) | collective-permute-done | bytes 131104 | tf_op jit(solution)/shard_map/ppermute | solution.py:25
  59.6 0.6 fold_sides.1
  60.3 1.9 %collective-permute-start.12 = (bf16[2,8,64,128]{3,2,1,0:T(8,128)(2,1)S(1)}, bf16[2,8,64,128]{3,2,1,0:T(8,128)(2,1)S(1)}, u32[]{:S(2)}, u32[]{:S(2)}) collective-permute-start(bf16[2,8,64,128]{3,2,1,0:T(8,128)(2,1)S(1)} %get-tuple-element.73), channel_id=1, source_target_pairs={{0,48},{48,0},{96,144},{144,96},{192,240},{240,192},{288,336},{336... | collective-permute-start | bytes 786440 | tf_op jit(solution)/shard_map/ppermute | solution.py:17
  62.2 5.5 %collective-permute-start.13 = (bf16[2,8,64,128]{3,2,1,0:T(8,128)(2,1)S(1)}, bf16[2,8,64,128]{3,2,1,0:T(8,128)(2,1)S(1)}, u32[]{:S(2)}, u32[]{:S(2)}) collective-permute-start(bf16[2,8,64,128]{3,2,1,0:T(8,128)(2,1)S(1)} %get-tuple-element.74), channel_id=1, source_target_pairs={{48,96},{96,48},{144,192},{192,144},{240,288},{288,240},{336,384},... | collective-permute-start | bytes 786440 | tf_op jit(solution)/shard_map/ppermute | solution.py:25
  67.7 4.9 %collective-permute-start.14 = (bf16[4,2,64,128]{3,2,1,0:T(8,128)(2,1)S(1)}, bf16[4,2,64,128]{3,2,1,0:T(8,128)(2,1)S(1)}, u32[]{:S(2)}, u32[]{:S(2)}) collective-permute-start(bf16[4,2,64,128]{3,2,1,0:T(8,128)(2,1)S(1)} %get-tuple-element.75), channel_id=1, source_target_pairs={{0,1},{1,0},{2,3},{3,2},{4,5},{5,4},{6,7},{7,6},{8,9},{9,8},{10,11... | collective-permute-start | bytes 393224 | tf_op jit(solution)/shard_map/ppermute | solution.py:17
  72.7 4.5 %collective-permute-start.15 = (bf16[4,2,64,128]{3,2,1,0:T(8,128)(2,1)S(1)}, bf16[4,2,64,128]{3,2,1,0:T(8,128)(2,1)S(1)}, u32[]{:S(2)}, u32[]{:S(2)}) collective-permute-start(bf16[4,2,64,128]{3,2,1,0:T(8,128)(2,1)S(1)} %get-tuple-element.76), channel_id=1, source_target_pairs={{1,2},{2,1},{3,4},{4,3},{5,6},{6,5},{7,8},{8,7},{9,10},{10,9},{11,... | collective-permute-start | bytes 393224 | tf_op jit(solution)/shard_map/ppermute | solution.py:25
  77.2 0.0 collective-permute-done.11.refs_3_
  77.2 0.0 copy-done.4
  77.2 3.0 %coarse_values.1.lifted_ref = f32[128,128]{1,0:T(8,128)S(1)} custom-call(s32[3]{0:T(128)S(1)} %pad_add_fusion.info_ref.refs_0_, s32[4,8]{1,0:T(4,128)S(1)} %copy-done.4, bf16[8,160,128]{2,1,0:T(8,128)(2,1)S(1)} %join_pair.5.refs_2_, bf16[8,160,128]{2,1,0:T(8,128)(2,1)S(1)} %collective-permute-done.11.refs_3_), custom_call_target="tpu_custom_call" | custom-call | flops 268435456 | bytes 655360 | tf_op jit(solution)/shard_map/coarse_values/pallas_call | solution.py:38
  80.2 0.0 collective-permute-done.14.cross_near
  80.2 3.2 %collective-permute-done.15.cross_far = bf16[4,2,64,128]{3,2,1,0:T(8,128)(2,1)S(1)} collective-permute-done((bf16[4,2,64,128]{3,2,1,0:T(8,128)(2,1)S(1)}, bf16[4,2,64,128]{3,2,1,0:T(8,128)(2,1)S(1)}, u32[]{:S(2)}, u32[]{:S(2)}) %collective-permute-start.15) | collective-permute-done | bytes 131104 | tf_op jit(solution)/shard_map/ppermute | solution.py:25
  83.4 0.0 collective-permute-done.12.main_near
  83.4 0.0 collective-permute-done.13.main_far
  83.4 2.0 %join.1 = f32[4,8,64,128]{3,2,1,0:T(8,128)} custom-call(s32[3]{0:T(128)S(1)} %pad_add_fusion.info_ref.refs_0_, f32[128,128]{1,0:T(8,128)S(1)} %coarse_values.1.lifted_ref, bf16[4,8,64,128]{3,2,1,0:T(8,128)(2,1)S(1)} %get-tuple-element.64.center_ref, bf16[2,8,64,128]{3,2,1,0:T(8,128)(2,1)S(1)} %collective-permute-done.12.main_near, ...), custom_call_target="tpu_custom_call" | custom-call | flops 2097152 | bytes 2621440 | tf_op jit(solution)/shard_map/join/pallas_call | solution.py:38
  (3 shorter events, 0.0 us)
Async XLA Ops:
  0.7 1.0 %copy-start = (bf16[4,8,64,128]{3,2,1,0:T(8,128)(2,1)S(1)}, bf16[4,8,64,128]{3,2,1,0:T(8,128)(2,1)}, u32[]{:S(2)}) copy-start(bf16[4,8,64,128]{3,2,1,0:T(8,128)(2,1)} %residual_ref.1) | copy-start | bytes 1572868
  2.5 21.7 %collective-permute-start = (bf16[2,8,64,128]{3,2,1,0:T(8,128)(2,1)S(1)}, bf16[2,8,64,128]{3,2,1,0:T(8,128)(2,1)S(1)}, u32[]{:S(2)}, u32[]{:S(2)}) collective-permute-start(bf16[2,8,64,128]{3,2,1,0:T(8,128)(2,1)S(1)} %get-tuple-element.41.own_far), channel_id=1, source_target_pairs={{48,96},{96,48},{144,192},{192,144},{240,288},{288,240},{336,384},... | collective-permute-start | bytes 786440 | tf_op jit(solution)/shard_map/ppermute | solution.py:25
  8.9 15.3 %collective-permute-start.1 = (bf16[2,8,64,128]{3,2,1,0:T(8,128)(2,1)S(1)}, bf16[2,8,64,128]{3,2,1,0:T(8,128)(2,1)S(1)}, u32[]{:S(2)}, u32[]{:S(2)}) collective-permute-start(bf16[2,8,64,128]{3,2,1,0:T(8,128)(2,1)S(1)} %get-tuple-element.42.own_near), channel_id=1, source_target_pairs={{0,48},{48,0},{96,144},{144,96},{192,240},{240,192},{288,336},{336... | collective-permute-start | bytes 786440 | tf_op jit(solution)/shard_map/ppermute | solution.py:17
  10.8 11.9 %collective-permute-start.2 = (bf16[4,2,64,128]{3,2,1,0:T(8,128)(2,1)S(1)}, bf16[4,2,64,128]{3,2,1,0:T(8,128)(2,1)S(1)}, u32[]{:S(2)}, u32[]{:S(2)}) collective-permute-start(bf16[4,2,64,128]{3,2,1,0:T(8,128)(2,1)S(1)} %get-tuple-element.43), channel_id=1, source_target_pairs={{1,2},{2,1},{3,4},{4,3},{5,6},{6,5},{7,8},{8,7},{9,10},{10,9},{11,... | collective-permute-start | bytes 393224 | tf_op jit(solution)/shard_map/ppermute | solution.py:25
  13.9 10.3 %collective-permute-start.3 = (bf16[4,2,64,128]{3,2,1,0:T(8,128)(2,1)S(1)}, bf16[4,2,64,128]{3,2,1,0:T(8,128)(2,1)S(1)}, u32[]{:S(2)}, u32[]{:S(2)}) collective-permute-start(bf16[4,2,64,128]{3,2,1,0:T(8,128)(2,1)S(1)} %get-tuple-element.44), channel_id=1, source_target_pairs={{0,1},{1,0},{2,3},{3,2},{4,5},{5,4},{6,7},{7,6},{8,9},{9,8},{10,11... | collective-permute-start | bytes 393224 | tf_op jit(solution)/shard_map/ppermute | solution.py:17
  15.8 0.7 copy-start.1
  16.5 0.7 copy-start.3
  24.2 10.9 %collective-permute-start.4 = (bf16[1,160,128]{2,1,0:T(8,128)(2,1)S(1)}, bf16[1,160,128]{2,1,0:T(8,128)(2,1)S(1)}, u32[]{:S(2)}, u32[]{:S(2)}) collective-permute-start(bf16[1,160,128]{2,1,0:T(8,128)(2,1)S(1)} %payload.1.first_ref), channel_id=1, source_target_pairs={{0,384},{48,432},{96,480},{144,528},{192,576},{240,624},{288,672},... | collective-permute-start | bytes 122888 | tf_op jit(solution)/shard_map/ppermute | solution.py:30
  27.0 14.1 %collective-permute-start.5 = (bf16[2,4,64,128]{3,2,1,0:T(8,128)(2,1)S(1)}, bf16[2,4,64,128]{3,2,1,0:T(8,128)(2,1)S(1)}, u32[]{:S(2)}, u32[]{:S(2)}) collective-permute-start(bf16[2,4,64,128]{3,2,1,0:T(8,128)(2,1)S(1)} %get-tuple-element.48), channel_id=1, source_target_pairs={{48,96},{96,48},{144,192},{192,144},{240,288},{288,240},{336,384},... | collective-permute-start | bytes 393224 | tf_op jit(solution)/shard_map/ppermute | solution.py:25
  33.2 8.0 %collective-permute-start.6 = (bf16[2,4,64,128]{3,2,1,0:T(8,128)(2,1)S(1)}, bf16[2,4,64,128]{3,2,1,0:T(8,128)(2,1)S(1)}, u32[]{:S(2)}, u32[]{:S(2)}) collective-permute-start(bf16[2,4,64,128]{3,2,1,0:T(8,128)(2,1)S(1)} %get-tuple-element.49), channel_id=1, source_target_pairs={{0,48},{48,0},{96,144},{144,96},{192,240},{240,192},{288,336},{336... | collective-permute-start | bytes 393224 | tf_op jit(solution)/shard_map/ppermute | solution.py:17
  35.1 8.2 %collective-permute-start.7 = (bf16[2,160,128]{2,1,0:T(8,128)(2,1)S(1)}, bf16[2,160,128]{2,1,0:T(8,128)(2,1)S(1)}, u32[]{:S(2)}, u32[]{:S(2)}) collective-permute-start(bf16[2,160,128]{2,1,0:T(8,128)(2,1)S(1)} %join_pair.3.first_ref), channel_id=1, source_target_pairs={{0,192},{48,240},{96,288},{144,336},{192,0},{240,48},{288,96},{336... | collective-permute-start | bytes 245768 | tf_op jit(solution)/shard_map/ppermute | solution.py:30
  39.1 2.1 %copy-start.2 = (s32[1,96,4]{1,2,0:T(4,128)S(1)}, s32[1,96,4]{1,2,0:T(4,128)}, u32[]{:S(2)}) copy-start(s32[1,96,4]{1,2,0:T(4,128)} %param.8) | copy-start | bytes 4612
  42.7 34.5 %copy-start.4 = (s32[4,8]{1,0:T(4,128)S(1)}, s32[4,8]{1,0:T(4,128)}, u32[]{:S(2)}) copy-start(s32[4,8]{1,0:T(4,128)} %refs_1_.1) | copy-start | bytes 388
  43.4 10.7 %collective-permute-start.8 = (bf16[4,160,128]{2,1,0:T(8,128)(2,1)S(1)}, bf16[4,160,128]{2,1,0:T(8,128)(2,1)S(1)}, u32[]{:S(2)}, u32[]{:S(2)}) collective-permute-start(bf16[4,160,128]{2,1,0:T(8,128)(2,1)S(1)} %join_pair.4.first_ref), channel_id=1, source_target_pairs={{0,96},{48,144},{96,0},{144,48},{192,288},{240,336},{288,192},{336... | collective-permute-start | bytes 491528 | tf_op jit(solution)/shard_map/ppermute | solution.py:30
  45.3 10.7 %collective-permute-start.9 = (bf16[2,4,64,128]{3,2,1,0:T(8,128)(2,1)S(1)}, bf16[2,4,64,128]{3,2,1,0:T(8,128)(2,1)S(1)}, u32[]{:S(2)}, u32[]{:S(2)}) collective-permute-start(bf16[2,4,64,128]{3,2,1,0:T(8,128)(2,1)S(1)} %get-tuple-element.61), channel_id=1, source_target_pairs={{0,48},{48,0},{96,144},{144,96},{192,240},{240,192},{288,336},{336... | collective-permute-start | bytes 393224 | tf_op jit(solution)/shard_map/ppermute | solution.py:17
  47.2 12.4 %collective-permute-start.10 = (bf16[2,4,64,128]{3,2,1,0:T(8,128)(2,1)S(1)}, bf16[2,4,64,128]{3,2,1,0:T(8,128)(2,1)S(1)}, u32[]{:S(2)}, u32[]{:S(2)}) collective-permute-start(bf16[2,4,64,128]{3,2,1,0:T(8,128)(2,1)S(1)} %get-tuple-element.62), channel_id=1, source_target_pairs={{48,96},{96,48},{144,192},{192,144},{240,288},{288,240},{336,384},... | collective-permute-start | bytes 393224 | tf_op jit(solution)/shard_map/ppermute | solution.py:25
  54.1 23.1 %collective-permute-start.11 = (bf16[8,160,128]{2,1,0:T(8,128)(2,1)S(1)}, bf16[8,160,128]{2,1,0:T(8,128)(2,1)S(1)}, u32[]{:S(2)}, u32[]{:S(2)}) collective-permute-start(bf16[8,160,128]{2,1,0:T(8,128)(2,1)S(1)} %join_pair.5.refs_2_), channel_id=1, source_target_pairs={{0,48},{48,0},{96,144},{144,96},{192,240},{240,192},{288,336},{336... | collective-permute-start | bytes 983048 | tf_op jit(solution)/shard_map/ppermute | solution.py:30
  60.3 23.2 %collective-permute-start.12 = (bf16[2,8,64,128]{3,2,1,0:T(8,128)(2,1)S(1)}, bf16[2,8,64,128]{3,2,1,0:T(8,128)(2,1)S(1)}, u32[]{:S(2)}, u32[]{:S(2)}) collective-permute-start(bf16[2,8,64,128]{3,2,1,0:T(8,128)(2,1)S(1)} %get-tuple-element.73), channel_id=1, source_target_pairs={{0,48},{48,0},{96,144},{144,96},{192,240},{240,192},{288,336},{336... | collective-permute-start | bytes 786440 | tf_op jit(solution)/shard_map/ppermute | solution.py:17
  62.2 21.3 %collective-permute-start.13 = (bf16[2,8,64,128]{3,2,1,0:T(8,128)(2,1)S(1)}, bf16[2,8,64,128]{3,2,1,0:T(8,128)(2,1)S(1)}, u32[]{:S(2)}, u32[]{:S(2)}) collective-permute-start(bf16[2,8,64,128]{3,2,1,0:T(8,128)(2,1)S(1)} %get-tuple-element.74), channel_id=1, source_target_pairs={{48,96},{96,48},{144,192},{192,144},{240,288},{288,240},{336,384},... | collective-permute-start | bytes 786440 | tf_op jit(solution)/shard_map/ppermute | solution.py:25
  67.7 12.5 %collective-permute-start.14 = (bf16[4,2,64,128]{3,2,1,0:T(8,128)(2,1)S(1)}, bf16[4,2,64,128]{3,2,1,0:T(8,128)(2,1)S(1)}, u32[]{:S(2)}, u32[]{:S(2)}) collective-permute-start(bf16[4,2,64,128]{3,2,1,0:T(8,128)(2,1)S(1)} %get-tuple-element.75), channel_id=1, source_target_pairs={{0,1},{1,0},{2,3},{3,2},{4,5},{5,4},{6,7},{7,6},{8,9},{9,8},{10,11... | collective-permute-start | bytes 393224 | tf_op jit(solution)/shard_map/ppermute | solution.py:17
  72.7 10.8 %collective-permute-start.15 = (bf16[4,2,64,128]{3,2,1,0:T(8,128)(2,1)S(1)}, bf16[4,2,64,128]{3,2,1,0:T(8,128)(2,1)S(1)}, u32[]{:S(2)}, u32[]{:S(2)}) collective-permute-start(bf16[4,2,64,128]{3,2,1,0:T(8,128)(2,1)S(1)} %get-tuple-element.76), channel_id=1, source_target_pairs={{1,2},{2,1},{3,4},{4,3},{5,6},{6,5},{7,8},{8,7},{9,10},{10,9},{11,... | collective-permute-start | bytes 393224 | tf_op jit(solution)/shard_map/ppermute | solution.py:25

commit v3 on v2

--- a/solution.py
+++ b/solution.py
@@ -25,9 +25,15 @@
     return lax.ppermute(values, axis, pairs)
 
 
-def swap_bit(values, axis, bit):
+def swap_halves(values, axis):
     count = lax.axis_size(axis)
-    return lax.ppermute(values, axis, [(i, i ^ bit) for i in range(count)])
+    return lax.ppermute(values, axis, [(i, (i + count // 2) % count) for i in range(count)])
+
+
+def exchange_in_half(values, axis):
+    half = lax.axis_size(axis) // 2
+    groups = [list(range(half)), list(range(half, 2 * half))]
+    return lax.all_to_all(values, axis, 0, 0, axis_index_groups=groups)
 
 
 def shaped(shape, dtype):
@@ -122,36 +128,39 @@
     )
 
 
-def join_pair_kernel(first_ref, second_ref, out_ref):
-    count = first_ref.shape[0]
-    out_ref[:count] = first_ref[...]
-    out_ref[count:] = second_ref[...]
-
-
-def join_pair(first, second):
-    count = first.shape[0]
-    return call(
-        join_pair_kernel, "join_pair", shaped((2 * count,) + first.shape[1:], BF16),
-        (first, second), [VMEM, VMEM], VMEM, 3, moved=8 * first.size,
-    )
-
-
-def corners_kernel(info_ref, cross_near, cross_far, near_ref, far_ref):
-    half = near_ref.shape[0]
+def spread_kernel(first_ref, second_ref, out_ref):
+    for i in range(out_ref.shape[0]):
+        out_ref[i, 0] = first_ref[0]
+        out_ref[i, 1] = second_ref[0]
+
+
+def spread_pair(first, second, copies):
+    return call(
+        spread_kernel, "spread_pair", shaped((copies, 2) + first.shape[1:], BF16),
+        (first, second), [VMEM, VMEM], VMEM, 3, moved=4 * copies * first.size,
+    )
+
+
+def corners_kernel(info_ref, own_near, cross_near, cross_far, near_ref, far_ref):
+    half, columns = own_near.shape[:2]
     p, _ = parities(info_ref)
-    for out_ref, start in ((near_ref, half * (1 - p)), (far_ref, half * p)):
+    for i in range(half):
+        for j in range(columns):
+            near_ref[i, j] = own_near[i, j]
+    for out_ref, start, base in ((near_ref, half * (1 - p), columns), (far_ref, half * p, 0)):
         for i in range(half):
             for j in range(2):
-                out_ref[i, j] = cross_near[start + i, j]
-                out_ref[i, 2 + j] = cross_far[start + i, j]
-
-
-def corners(info, cross_near, cross_far):
-    rows, _, width, sides = cross_near.shape
-    piece = shaped((rows // 2, 4, width, sides), BF16)
-    return call(
-        corners_kernel, "corners", (piece, piece), (info, cross_near, cross_far),
-        [SMEM, VMEM, VMEM], (VMEM, VMEM), 2, moved=8 * cross_near.size,
+                out_ref[i, base + j] = cross_near[start + i, j]
+                out_ref[i, base + 2 + j] = cross_far[start + i, j]
+
+
+def corners(info, own_near, cross_near, cross_far):
+    half, columns, width, sides = own_near.shape
+    return call(
+        corners_kernel, "corners",
+        (shaped((half, columns + 4, width, sides), BF16), shaped((half, 4, width, sides), BF16)),
+        (info, own_near, cross_near, cross_far), [SMEM, VMEM, VMEM, VMEM], (VMEM, VMEM), 3,
+        moved=8 * cross_near.size,
     )
 
 
@@ -162,8 +171,8 @@
 
 def margin_kernel(
     info_ref, pattern_ref, blocks_ref,
-    own_near, own_far, got_near, got_far, cross_near, cross_far, corner_near, corner_far,
-    main_near, main_far, out_near, out_far, grid_ref,
+    own_near, own_far, got_near, got_far, cross_near, cross_far, corner_far,
+    out_near, main_far, out_far, grid_ref,
 ):
     half, columns = own_near.shape[:2]
     rows = 2 * half
@@ -182,17 +191,23 @@
         for i in range(rows):
             for j in range(2):
                 grid_ref[(2 + i) * wide + start + j] = source[i, j]
-    for source, start in ((corner_near, near_row), (corner_far, far_row)):
+    for source, start, first in ((got_near, near_row, columns), (corner_far, far_row, 0)):
         for i in range(2):
             for j in range(2):
-                grid_ref[(start + i) * wide + near_column + j] = source[i, j]
-                grid_ref[(start + i) * wide + far_column + j] = source[i, 2 + j]
-    for main, corner, start in ((main_near, out_near, near_row), (main_far, out_far, far_row)):
+                grid_ref[(start + i) * wide + near_column + j] = source[i, first + j]
+                grid_ref[(start + i) * wide + far_column + j] = source[i, first + 2 + j]
+    for main, corner, first, start in (
+        (main_far, out_far, 0, far_row), (out_near, out_near, columns, near_row)
+    ):
         for i in range(2):
             base = (start + i) * wide
             for j in range(2):
-                corner[i, j] = fix_of(pattern_ref, blocks_ref, grid_ref, base + near_column + j)
-                corner[i, 2 + j] = fix_of(pattern_ref, blocks_ref, grid_ref, base + far_column + j)
+                corner[i, first + j] = fix_of(
+                    pattern_ref, blocks_ref, grid_ref, base + near_column + j
+                )
+                corner[i, first + 2 + j] = fix_of(
+                    pattern_ref, blocks_ref, grid_ref, base + far_column + j
+                )
             for j in range(columns):
                 main[i, j] = fix_of(pattern_ref, blocks_ref, grid_ref, base + 2 + j)
 
@@ -200,12 +215,13 @@
 def margin_fixes(info, pattern, blocks, pieces):
     count, width, depth = blocks.shape
     half, columns, _, sides = pieces[0].shape
+    near = shaped((2, columns + 4, width, sides), BF16)
     main = shaped((2, columns, width, sides), BF16)
     corner = shaped((2, 4, width, sides), BF16)
     grid = shaped((count, width, sides), BF16)
     return call(
-        margin_kernel, "margin_fixes", (main, main, corner, corner, grid),
-        (info, pattern, blocks) + pieces, [SMEM, SMEM] + [VMEM] * 9, (VMEM,) * 5, 12,
+        margin_kernel, "margin_fixes", (near, main, corner, grid),
+        (info, pattern, blocks) + pieces, [SMEM, SMEM] + [VMEM] * 8, (VMEM,) * 4, 12,
         flops=blocks.size * sides, moved=2 * blocks.size,
     )
 
@@ -235,23 +251,25 @@
     )
 
 
-def fold_kernel(info_ref, side_near, side_far, corner_near, corner_far, out_near, out_far):
-    half = corner_near.shape[0]
+def fold_kernel(info_ref, side_near, side_far, got_near, corner_far, out_near, out_far):
+    half, wide = got_near.shape[:2]
     p, _ = parities(info_ref)
-    for source, start in ((corner_near, half * (1 - p)), (corner_far, half * p)):
+    for source, start, first in (
+        (got_near, half * (1 - p), wide - 4), (corner_far, half * p, 0)
+    ):
         for i in range(half):
             for j in range(2):
                 for side, out, at in ((side_near, out_near, j), (side_far, out_far, 2 + j)):
-                    total = side[start + i, j].astype(F32) + source[i, at].astype(F32)
+                    total = side[start + i, j].astype(F32) + source[i, first + at].astype(F32)
                     out[start + i, j] = total.astype(BF16)
 
 
-def fold_sides(info, side_near, side_far, corner_near, corner_far):
+def fold_sides(info, side_near, side_far, got_near, corner_far):
     piece = shaped(side_near.shape, BF16)
     return call(
         fold_kernel, "fold_sides", (piece, piece),
-        (info, side_near, side_far, corner_near, corner_far),
-        [SMEM] + [VMEM] * 4, (VMEM, VMEM), 2, flops=2 * side_near.size, moved=12 * side_near.size,
+        (info, side_near, side_far, got_near, corner_far),
+        [SMEM] + [VMEM] * 4, (VMEM, VMEM), 3, flops=2 * side_near.size, moved=12 * side_near.size,
     )
 
 
@@ -263,8 +281,8 @@
     )
 
 
-def solve_kernel(bits, info_ref, agg_ref, first_ref, second_ref, out_ref, sums, coarse):
-    count, height, sides = first_ref.shape
+def solve_kernel(info_ref, agg_ref, gathered_ref, out_ref, sums, coarse):
+    count, pair, height, sides = gathered_ref.shape
     rows, columns = agg_ref.shape
     fields = rows * columns * 4
     size = height - fields
@@ -276,30 +294,26 @@
     column = lax.broadcasted_iota(jnp.int32, (total, fields), 1)
     same_field = row % 4 == column % 4
     owner = (row // 4).astype(F32)
-    for part, source in enumerate((first_ref, second_ref)):
-        for k in range(count):
-            tail = source[k, pl.ds(fields, 16), :]
-            labels = jnp.dot(tail, repeat, preferred_element_type=F32)[:1]
-            onehot = jnp.where(same_field & (owner == labels), 1.0, 0.0).astype(BF16)
-            found = jnp.dot(
-                onehot, source[k, pl.ds(0, fields), :], preferred_element_type=F32
-            )
-            if part == 0 and k == 0:
-                sums[...] = found
-            else:
-                sums[...] += found
-    for part, source in enumerate((first_ref, second_ref)):
-        for k in range(count):
-            slot, flips = part * count + k, 0
-            for i, bit in enumerate(bits):
-                if slot >> i & 1:
-                    flips |= bit
-            start = pl.multiple_of((info_ref[1] ^ flips) * size, size)
-            mine = sums[pl.ds(start, size), :]
-            stacked = jnp.concatenate([mine, mine, mine, jnp.zeros_like(mine)], axis=0)
-            coarse[pl.ds(start, size), :] = split_dot(
-                source[k, pl.ds(fields, size), :], stacked
-            )
+    slots = [(k, i) for k in range(count) for i in range(pair)]
+    for place, (k, i) in enumerate(slots):
+        tail = gathered_ref[k, i, pl.ds(fields, 16), :]
+        labels = jnp.dot(tail, repeat, preferred_element_type=F32)[:1]
+        onehot = jnp.where(same_field & (owner == labels), 1.0, 0.0).astype(BF16)
+        found = jnp.dot(
+            onehot, gathered_ref[k, i, pl.ds(0, fields), :], preferred_element_type=F32
+        )
+        if place == 0:
+            sums[...] = found
+        else:
+            sums[...] += found
+    high = info_ref[1] // count
+    for k, i in slots:
+        start = pl.multiple_of((k + count * (high ^ i)) * size, size)
+        mine = sums[pl.ds(start, size), :]
+        stacked = jnp.concatenate([mine, mine, mine, jnp.zeros_like(mine)], axis=0)
+        coarse[pl.ds(start, size), :] = split_dot(
+            gathered_ref[k, i, pl.ds(fields, size), :], stacked
+        )
     row = lax.broadcasted_iota(jnp.int32, (fields, 1), 0)
     labels = jnp.zeros((fields, 1), jnp.int32)
     for i in range(rows):
@@ -311,17 +325,13 @@
     out_ref[...] = split_dot(onehot.astype(BF16), coarse[...])
 
 
-def coarse_values(bits, info, agg, first, second):
-    count, height, sides = first.shape
+def coarse_values(info, agg, gathered):
+    count, pair, height, sides = gathered.shape
     fields = agg.size * 4
-    total = 2 * count * (height - fields)
-
-    def kernel(*refs):
-        solve_kernel(bits, *refs)
-
-    return call(
-        kernel, "coarse_values", shaped((fields, sides), F32), (info, agg, first, second),
-        [SMEM, SMEM, VMEM, VMEM], VMEM, 8, flops=1 << 28, moved=4 * first.size,
+    total = count * pair * (height - fields)
+    return call(
+        solve_kernel, "coarse_values", shaped((fields, sides), F32), (info, agg, gathered),
+        [SMEM, SMEM, VMEM], VMEM, 8, flops=1 << 28, moved=2 * gathered.size,
         scratch=[pltpu.VMEM((total, sides), F32), pltpu.VMEM((total, sides), F32)],
     )
 
@@ -372,54 +382,33 @@
     rows, columns = residual.shape[:2]
     info = jnp.stack([live_blocks[0, 0], lax.axis_index("stream"), lax.axis_index("cross")])
     own_near, own_far, edge_near, edge_far = mask_blocks(info, residual)
-    bits = []
-    while 2 << len(bits) <= lax.axis_size("stream"):
-        bits.insert(0, 1 << len(bits))
-
     gathered = payload_of(info, block_aggregate, own_near, own_far, coarse_inverse)
     got_far = swap_far(own_far, "stream")
-    got_near = swap_near(own_near, "stream")
     cross_far = swap_far(edge_far, "cross")
     cross_near = swap_near(edge_near, "cross")
     blocks, links = approx_inverse[0], jnp.transpose(pattern[0])
-    got_far, got_near, cross_far, cross_near, blocks, gathered = lax.optimization_barrier(
-        (got_far, got_near, cross_far, cross_near, blocks, gathered)
-    )
+    blocks, gathered = lax.optimization_barrier((blocks, gathered))
     blocks = jnp.where(info[0] > 0, blocks, jnp.zeros((), BF16))
-    corner_near, corner_far = corners(info, cross_near, cross_far)
-    other = swap_bit(gathered, "stream", bits[0])
+    other = swap_halves(gathered, "stream")
+    got_far, cross_far, cross_near, blocks = lax.optimization_barrier(
+        (got_far, cross_far, cross_near, blocks)
+    )
+    got_near, corner_far = corners(info, own_near, cross_near, cross_far)
     corner_far = swap_far(corner_far, "stream")
-    corner_near = swap_near(corner_near, "stream")
-    gathered = join_pair(gathered, other)
-    other = swap_bit(gathered, "stream", bits[1])
-    gathered, corner_far, corner_near = lax.optimization_barrier(
-        (gathered, corner_far, corner_near)
-    )
-    pieces = (own_near, own_far, got_near, got_far, cross_near, cross_far, corner_near, corner_far)
-    main_near, main_far, corner_near, corner_far, grid = margin_fixes(info, links, blocks, pieces)
-    corner_far, other = lax.optimization_barrier((corner_far, other))
-    gathered = join_pair(gathered, other)
+    got_near = swap_near(got_near, "stream")
+    gathered = spread_pair(gathered, other, lax.axis_size("stream") // 2)
+    gathered = exchange_in_half(gathered, "stream")
+    pieces = (own_near, own_far, got_near, got_far, cross_near, cross_far, corner_far)
+    near, main_far, corner_far, grid = margin_fixes(info, links, blocks, pieces)
     corner_far = swap_far(corner_far, "stream")
-    corner_near = swap_near(corner_near, "stream")
-    other = swap_bit(gathered, "stream", bits[2])
+    near = swap_near(near, "stream")
     side_near, side_far, center = center_fixes(info, links, blocks, grid, rows, columns)
-    side_near, other = lax.optimization_barrier((side_near, other))
-    for bit in bits[3:]:
-        gathered = join_pair(gathered, other)
-        other = swap_bit(gathered, "stream", bit)
-    gathered, corner_near, corner_far = lax.optimization_barrier(
-        (gathered, corner_near, corner_far)
-    )
-    side_near, side_far = fold_sides(info, side_near, side_far, corner_near, corner_far)
-    side_near, side_far, main_far, main_near = lax.optimization_barrier(
-        (side_near, side_far, main_far, main_near)
-    )
+    side_near, side_far = fold_sides(info, side_near, side_far, near, corner_far)
     main_far = swap_far(main_far, "stream")
-    main_near = swap_near(main_near, "stream")
     cross_far = swap_far(side_far, "cross")
     cross_near = swap_near(side_near, "cross")
-    lifted = coarse_values(bits, info, block_aggregate, gathered, other)
-    return join(info, lifted, center, main_near, main_far, cross_near, cross_far)
+    lifted = coarse_values(info, block_aggregate, gathered)
+    return join(info, lifted, center, near, main_far, cross_near, cross_far)
 
 
 def solution(mesh):

time: 86.1 us -> 86.7 us (level)
  the two profiles are of different devices: /device:TPU:504 before, /device:TPU:248 now
where the time goes in v3:
time: 86.7 us; the launch traced here: 85.9 us
  starting transfers between devices  49.7 us (57%)
  Pallas kernels  13.1 us (15%)
  waiting for transfers between devices  12 us (14%)
  local copies, waits for them, and re-layouts  7.93 us (9%)
  other arithmetic  2.18 us (3%)
  between operations  0.94 us (1%)
    ppermute x6, starting transfers between devices, swap_far(): return lax.ppermute(values, axis, pairs)  35.4 us
    pallas_call x9, Pallas kernels, call(): pl.pallas_call(kernel, out_shape=outs, in_specs=specs, out_specs=out_spec...  13.1 us
    ppermute x1, waiting for transfers between devices, swap_halves(): lax.ppermute(values, axis, [(i, (i + count // 2) % count) for i in range(...  8.63 us
    ppermute x4, starting transfers between devices, swap_near(): lax.ppermute(values, axis, [(i, i ^ 1) for i in range(count) if i ^ 1 < c...  8.15 us
    unnamed x28, local copies, waits for them, and re-layouts  7.93 us
    all_to_all x1, starting transfers between devices, exchange_in_half(): return lax.all_to_all(values, axis, 0, 0, axis_index_groups=groups)  4.21 us
    ppermute x4, waiting for transfers between devices, swap_near(): lax.ppermute(values, axis, [(i, i ^ 1) for i in range(count) if i ^ 1 < c...  3.37 us
    select_n x1, other arithmetic, body(): blocks = jnp.where(info[0] > 0, blocks, jnp.zeros((), BF16))  2.1 us
  transfers between devices with their start and end apart: 12, of which 3 were waited for; matrix products, arithmetic and copies ran while one was open for 2% of the time, Pallas kernels for 10%

profile of v3, /device:TPU:248, one launch (start us, length us, event | category | flops | bytes accessed | tf_op | source)
XLA Modules:
  0.0 85.9 jit_solution(15565661048947773205)
XLA Ops:
  0.7 0.1 pad_add_fusion.info_ref
  0.7 0.0 copy-start.5
  0.7 1.0 %copy-done.5 = bf16[4,8,64,128]{3,2,1,0:T(8,128)(2,1)S(1)} copy-done((bf16[4,8,64,128]{3,2,1,0:T(8,128)(2,1)S(1)}, bf16[4,8,64,128]{3,2,1,0:T(8,128)(2,1)}, u32[]{:S(2)}) %copy-start.5) | copy-done | bytes 524312
  1.8 0.7 mask_blocks.1
  2.5 0.0 copy-start.1
  2.5 6.3 %collective-permute-start.1 = (bf16[2,8,64,128]{3,2,1,0:T(8,128)(2,1)S(1)}, bf16[2,8,64,128]{3,2,1,0:T(8,128)(2,1)S(1)}, u32[]{:S(2)}, u32[]{:S(2)}) collective-permute-start(bf16[2,8,64,128]{3,2,1,0:T(8,128)(2,1)S(1)} %get-tuple-element.27.own_far), channel_id=1, source_target_pairs={{48,96},{96,48},{144,192},{192,144},{240,288},{288,240},{336,384},... | collective-permute-start | bytes 786440 | tf_op jit(solution)/shard_map/ppermute | solution.py:25
  8.9 5.2 %collective-permute-start.2 = (bf16[4,2,64,128]{3,2,1,0:T(8,128)(2,1)S(1)}, bf16[4,2,64,128]{3,2,1,0:T(8,128)(2,1)S(1)}, u32[]{:S(2)}, u32[]{:S(2)}) collective-permute-start(bf16[4,2,64,128]{3,2,1,0:T(8,128)(2,1)S(1)} %get-tuple-element.29), channel_id=1, source_target_pairs={{1,2},{2,1},{3,4},{4,3},{5,6},{6,5},{7,8},{8,7},{9,10},{10,9},{11,... | collective-permute-start | bytes 393224 | tf_op jit(solution)/shard_map/ppermute | solution.py:25
  14.0 1.9 %collective-permute-start.3 = (bf16[4,2,64,128]{3,2,1,0:T(8,128)(2,1)S(1)}, bf16[4,2,64,128]{3,2,1,0:T(8,128)(2,1)S(1)}, u32[]{:S(2)}, u32[]{:S(2)}) collective-permute-start(bf16[4,2,64,128]{3,2,1,0:T(8,128)(2,1)S(1)} %get-tuple-element.30), channel_id=1, source_target_pairs={{0,1},{1,0},{2,3},{3,2},{4,5},{5,4},{6,7},{7,6},{8,9},{9,8},{10,11... | collective-permute-start | bytes 393224 | tf_op jit(solution)/shard_map/ppermute | solution.py:17
  16.0 0.0 copy-start.10
  16.0 0.7 copy-done.10
  16.7 0.0 copy-start.12
  16.7 0.7 copy-done.12
  17.4 0.8 payload.1.first_ref
  18.2 0.0 copy-start.11
  18.2 2.1 %broadcast_select_fusion.blocks_ref = bf16[96,64,256]{2,1,0:T(8,128)(2,1)S(1)} fusion(bf16[96,64,256]{2,1,0:T(8,128)(2,1)} %bitcast.15, pred[]{:T(512)} %bitcast.8), kind=kLoop, calls=%fused_computation | loop fusion | flops 1572864 | bytes 6291457 | tf_op jit(solution)/shard_map/jit(_where)/select_n | solution.py:391
  20.3 0.0 copy-done.1
  20.3 0.0 collective-permute-done.2.cross_far
  20.3 2.0 %collective-permute-done.3.cross_near = bf16[4,2,64,128]{3,2,1,0:T(8,128)(2,1)S(1)} collective-permute-done((bf16[4,2,64,128]{3,2,1,0:T(8,128)(2,1)S(1)}, bf16[4,2,64,128]{3,2,1,0:T(8,128)(2,1)S(1)}, u32[]{:S(2)}, u32[]{:S(2)}) %collective-permute-start.3) | collective-permute-done | bytes 131104 | tf_op jit(solution)/shard_map/ppermute | solution.py:17
  22.3 0.0 copy-start.3
  22.3 0.0 collective-permute-done.1.got_far
  22.3 0.0 copy-start.8
  22.3 1.4 %corners.1 = (bf16[2,12,64,128]{3,2,1,0:T(8,128)(2,1)}, bf16[2,4,64,128]{3,2,1,0:T(8,128)(2,1)}) custom-call(s32[3]{0:T(128)S(1)} %pad_add_fusion.info_ref, bf16[2,8,64,128]{3,2,1,0:T(8,128)(2,1)S(1)} %get-tuple-element.26.own_near, bf16[4,2,64,128]{3,2,1,0:T(8,128)(2,1)S(1)} %collective-permute-done.3.cross_near, ...), custom_call_target="tpu_custom_call" | custom-call | bytes 524288 | tf_op jit(solution)/shard_map/corners/pallas_call | solution.py:44
  23.7 1.9 %collective-permute-start.4 = (bf16[2,12,64,128]{3,2,1,0:T(8,128)(2,1)}, bf16[2,12,64,128]{3,2,1,0:T(8,128)(2,1)}, u32[]{:S(2)}, u32[]{:S(2)}) collective-permute-start(bf16[2,12,64,128]{3,2,1,0:T(8,128)(2,1)} %get-tuple-element.35), channel_id=1, source_target_pairs={{0,48},{48,0},{96,144},{144,96},{192,240},{240,192},{288,336},{336... | collective-permute-start | bytes 1179656 | tf_op jit(solution)/shard_map/ppermute | solution.py:17
  25.6 5.7 %collective-permute-start.5 = (bf16[2,4,64,128]{3,2,1,0:T(8,128)(2,1)}, bf16[2,4,64,128]{3,2,1,0:T(8,128)(2,1)}, u32[]{:S(2)}, u32[]{:S(2)}) collective-permute-start(bf16[2,4,64,128]{3,2,1,0:T(8,128)(2,1)} %get-tuple-element.37), channel_id=1, source_target_pairs={{48,96},{96,48},{144,192},{192,144},{240,288},{288,240},{336,384},... | collective-permute-start | bytes 393224 | tf_op jit(solution)/shard_map/ppermute | solution.py:25
  31.3 1.9 %collective-permute-start = (bf16[1,160,128]{2,1,0:T(8,128)(2,1)S(1)}, bf16[1,160,128]{2,1,0:T(8,128)(2,1)S(1)}, u32[]{:S(2)}, u32[]{:S(2)}) collective-permute-start(bf16[1,160,128]{2,1,0:T(8,128)(2,1)S(1)} %payload.1.first_ref), channel_id=1, source_target_pairs={{0,384},{48,432},{96,480},{144,528},{192,576},{240,624},{288,672},... | collective-permute-start | bytes 122888 | tf_op jit(solution)/shard_map/ppermute | solution.py:30
  33.2 0.0 copy-done.3
  33.2 8.6 %collective-permute-done.second_ref = bf16[1,160,128]{2,1,0:T(8,128)(2,1)S(1)} collective-permute-done((bf16[1,160,128]{2,1,0:T(8,128)(2,1)S(1)}, bf16[1,160,128]{2,1,0:T(8,128)(2,1)S(1)}, u32[]{:S(2)}, u32[]{:S(2)}) %collective-permute-start) | collective-permute-done | bytes 40992 | tf_op jit(solution)/shard_map/ppermute | solution.py:30
  41.9 0.0 copy-done.8
  41.9 0.1 spread_pair.1
  42.0 0.0 copy-start
  42.0 0.8 copy-done
  42.8 4.2 %all-to-all-start = ((bf16[8,2,160,128]{3,2,1,0:T(8,128)(2,1)}), bf16[8,2,160,128]{3,2,1,0:T(8,128)(2,1)}, u32[]{:S(2)}, u32[]{:S(2)}) async-start(bf16[8,2,160,128]{3,2,1,0:T(8,128)(2,1)} %copy-done), calls=%async_computation | async-start | bytes 1310720 | tf_op jit(solution)/shard_map/all_to_all | solution.py:36
  47.0 0.0 collective-permute-done.5.corner_far
  47.0 0.0 collective-permute-done.4.got_near
  47.0 0.0 copy-done.11
  47.0 0.0 copy-start.2
  47.1 0.9 %copy-done.2 = bf16[2,8,64,128]{3,2,1,0:T(8,128)(2,1)S(1)} copy-done((bf16[2,8,64,128]{3,2,1,0:T(8,128)(2,1)S(1)}, bf16[2,8,64,128]{3,2,1,0:T(8,128)(2,1)}, u32[]{:S(2)}) %copy-start.2) | copy-done | bytes 262168
  48.0 0.0 copy-start.4
  48.0 0.9 %copy-done.4 = bf16[4,2,64,128]{3,2,1,0:T(8,128)(2,1)S(1)} copy-done((bf16[4,2,64,128]{3,2,1,0:T(8,128)(2,1)S(1)}, bf16[4,2,64,128]{3,2,1,0:T(8,128)(2,1)}, u32[]{:S(2)}) %copy-start.4) | copy-done | bytes 131096
  48.9 0.0 copy-start.9
  48.9 0.9 %copy-done.9 = bf16[2,8,64,128]{3,2,1,0:T(8,128)(2,1)S(1)} copy-done((bf16[2,8,64,128]{3,2,1,0:T(8,128)(2,1)S(1)}, bf16[2,8,64,128]{3,2,1,0:T(8,128)(2,1)}, u32[]{:S(2)}) %copy-start.9) | copy-done | bytes 262168
  49.9 2.4 %margin_fixes.1 = (bf16[2,12,64,128]{3,2,1,0:T(8,128)(2,1)S(1)}, bf16[2,8,64,128]{3,2,1,0:T(8,128)(2,1)}, bf16[2,4,64,128]{3,2,1,0:T(8,128)(2,1)S(1)}, bf16[96,64,128]{2,1,0:T(8,128)(2,1)S(1)}) custom-call(s32[3]{0:T(128)S(1)} %pad_add_fusion.info_ref, s32[4,96]{1,0:T(4,128)S(1)} %bitcast.13, bf16[96,64,256]{2,1,0:T(8,128)(2,1)S(1)} %broadcast_select_fusion.blocks_ref, ...), custom_call_target="tpu_custom_call" | custom-call | flops 201326592 | bytes 3145728 | tf_op jit(solution)/shard_map/margin_fixes/pallas_call | solution.py:44
  52.3 0.0 copy-start.13
  52.3 2.4 %collective-permute-start.6 = (bf16[2,12,64,128]{3,2,1,0:T(8,128)(2,1)S(1)}, bf16[2,12,64,128]{3,2,1,0:T(8,128)(2,1)S(1)}, u32[]{:S(2)}, u32[]{:S(2)}) collective-permute-start(bf16[2,12,64,128]{3,2,1,0:T(8,128)(2,1)S(1)} %get-tuple-element.40), channel_id=1, source_target_pairs={{0,48},{48,0},{96,144},{144,96},{192,240},{240,192},{288,336},{336... | collective-permute-start | bytes 1179656 | tf_op jit(solution)/shard_map/ppermute | solution.py:17
  54.7 4.0 %collective-permute-start.8 = (bf16[2,4,64,128]{3,2,1,0:T(8,128)(2,1)S(1)}, bf16[2,4,64,128]{3,2,1,0:T(8,128)(2,1)S(1)}, u32[]{:S(2)}, u32[]{:S(2)}) collective-permute-start(bf16[2,4,64,128]{3,2,1,0:T(8,128)(2,1)S(1)} %get-tuple-element.44), channel_id=1, source_target_pairs={{48,96},{96,48},{144,192},{192,144},{240,288},{288,240},{336,384},... | collective-permute-start | bytes 393224 | tf_op jit(solution)/shard_map/ppermute | solution.py:25
  58.7 7.6 %collective-permute-start.7 = (bf16[2,8,64,128]{3,2,1,0:T(8,128)(2,1)}, bf16[2,8,64,128]{3,2,1,0:T(8,128)(2,1)}, u32[]{:S(2)}, u32[]{:S(2)}) collective-permute-start(bf16[2,8,64,128]{3,2,1,0:T(8,128)(2,1)} %get-tuple-element.41), channel_id=1, source_target_pairs={{48,96},{96,48},{144,192},{192,144},{240,288},{288,240},{336,384},... | collective-permute-start | bytes 786440 | tf_op jit(solution)/shard_map/ppermute | solution.py:25
  66.3 1.2 %center_fixes.1 = (bf16[4,2,64,128]{3,2,1,0:T(8,128)(2,1)S(1)}, bf16[4,2,64,128]{3,2,1,0:T(8,128)(2,1)S(1)}, bf16[4,8,64,128]{3,2,1,0:T(8,128)(2,1)S(1)}) custom-call(s32[3]{0:T(128)S(1)} %pad_add_fusion.info_ref, s32[4,96]{1,0:T(4,128)S(1)} %bitcast.14, bf16[96,64,256]{2,1,0:T(8,128)(2,1)S(1)} %broadcast_select_fusion.blocks_ref, ...), custom_call_target="tpu_custom_call" | custom-call | flops 201326592 | bytes 3145728 | tf_op jit(solution)/shard_map/center_fixes/pallas_call | solution.py:44
  67.5 0.0 copy-start.6
  67.5 0.8 copy-done.6
  68.3 0.0 collective-permute-done.8.corner_far
  68.3 0.0 collective-permute-done.6.got_near.main_near
  68.3 0.6 fold_sides.1
  68.9 6.7 %collective-permute-start.10 = (bf16[4,2,64,128]{3,2,1,0:T(8,128)(2,1)S(1)}, bf16[4,2,64,128]{3,2,1,0:T(8,128)(2,1)S(1)}, u32[]{:S(2)}, u32[]{:S(2)}) collective-permute-start(bf16[4,2,64,128]{3,2,1,0:T(8,128)(2,1)S(1)} %get-tuple-element.46), channel_id=1, source_target_pairs={{1,2},{2,1},{3,4},{4,3},{5,6},{6,5},{7,8},{8,7},{9,10},{10,9},{11,... | collective-permute-start | bytes 393224 | tf_op jit(solution)/shard_map/ppermute | solution.py:25
  75.6 1.9 %collective-permute-start.9 = (bf16[4,2,64,128]{3,2,1,0:T(8,128)(2,1)S(1)}, bf16[4,2,64,128]{3,2,1,0:T(8,128)(2,1)S(1)}, u32[]{:S(2)}, u32[]{:S(2)}) collective-permute-start(bf16[4,2,64,128]{3,2,1,0:T(8,128)(2,1)S(1)} %get-tuple-element.45), channel_id=1, source_target_pairs={{0,1},{1,0},{2,3},{3,2},{4,5},{5,4},{6,7},{7,6},{8,9},{9,8},{10,11... | collective-permute-start | bytes 393224 | tf_op jit(solution)/shard_map/ppermute | solution.py:17
  77.5 0.0 all-to-all-done.gathered_ref
  77.6 0.0 copy-done.13
  77.6 3.5 %coarse_values.1.lifted_ref = f32[128,128]{1,0:T(8,128)S(1)} custom-call(s32[3]{0:T(128)S(1)} %pad_add_fusion.info_ref, s32[4,8]{1,0:T(4,128)S(1)} %copy-done.13, bf16[8,2,160,128]{3,2,1,0:T(8,128)(2,1)} %all-to-all-done.gathered_ref), custom_call_target="tpu_custom_call" | custom-call | flops 268435456 | bytes 655360 | tf_op jit(solution)/shard_map/coarse_values/pallas_call | solution.py:44
  81.1 0.0 collective-permute-done.7.main_far
  81.1 0.0 collective-permute-done.10.cross_far
  81.1 1.4 %collective-permute-done.9.cross_near = bf16[4,2,64,128]{3,2,1,0:T(8,128)(2,1)S(1)} collective-permute-done((bf16[4,2,64,128]{3,2,1,0:T(8,128)(2,1)S(1)}, bf16[4,2,64,128]{3,2,1,0:T(8,128)(2,1)S(1)}, u32[]{:S(2)}, u32[]{:S(2)}) %collective-permute-start.9) | collective-permute-done | bytes 131104 | tf_op jit(solution)/shard_map/ppermute | solution.py:17
  82.5 0.0 copy-start.7
  82.5 1.0 %copy-done.7 = bf16[4,8,64,128]{3,2,1,0:T(8,128)(2,1)S(1)} copy-done((bf16[4,8,64,128]{3,2,1,0:T(8,128)(2,1)S(1)}, bf16[4,8,64,128]{3,2,1,0:T(8,128)(2,1)}, u32[]{:S(2)}) %copy-start.7) | copy-done | bytes 524312
  83.5 2.4 %join.1 = f32[4,8,64,128]{3,2,1,0:T(8,128)} custom-call(s32[3]{0:T(128)S(1)} %pad_add_fusion.info_ref, f32[128,128]{1,0:T(8,128)S(1)} %coarse_values.1.lifted_ref, bf16[4,8,64,128]{3,2,1,0:T(8,128)(2,1)S(1)} %copy-done.7, bf16[2,12,64,128]{3,2,1,0:T(8,128)(2,1)S(1)} %collective-permute-done.6.got_near.main_near, ...), custom_call_target="tpu_custom_call" | custom-call | flops 2097152 | bytes 2621440 | tf_op jit(solution)/shard_map/join/pallas_call | solution.py:44
Async XLA Ops:
  0.7 1.0 %copy-start.5 = (bf16[4,8,64,128]{3,2,1,0:T(8,128)(2,1)S(1)}, bf16[4,8,64,128]{3,2,1,0:T(8,128)(2,1)}, u32[]{:S(2)}) copy-start(bf16[4,8,64,128]{3,2,1,0:T(8,128)(2,1)} %residual_ref.1) | copy-start | bytes 1572868
  2.5 17.8 %copy-start.1 = (bf16[2,8,64,128]{3,2,1,0:T(8,128)(2,1)}, bf16[2,8,64,128]{3,2,1,0:T(8,128)(2,1)S(1)}, u32[]{:S(2)}) copy-start(bf16[2,8,64,128]{3,2,1,0:T(8,128)(2,1)S(1)} %get-tuple-element.27.own_far) | copy-start | bytes 786436
  2.5 19.8 %collective-permute-start.1 = (bf16[2,8,64,128]{3,2,1,0:T(8,128)(2,1)S(1)}, bf16[2,8,64,128]{3,2,1,0:T(8,128)(2,1)S(1)}, u32[]{:S(2)}, u32[]{:S(2)}) collective-permute-start(bf16[2,8,64,128]{3,2,1,0:T(8,128)(2,1)S(1)} %get-tuple-element.27.own_far), channel_id=1, source_target_pairs={{48,96},{96,48},{144,192},{192,144},{240,288},{288,240},{336,384},... | collective-permute-start | bytes 786440 | tf_op jit(solution)/shard_map/ppermute | solution.py:25
  8.9 11.4 %collective-permute-start.2 = (bf16[4,2,64,128]{3,2,1,0:T(8,128)(2,1)S(1)}, bf16[4,2,64,128]{3,2,1,0:T(8,128)(2,1)S(1)}, u32[]{:S(2)}, u32[]{:S(2)}) collective-permute-start(bf16[4,2,64,128]{3,2,1,0:T(8,128)(2,1)S(1)} %get-tuple-element.29), channel_id=1, source_target_pairs={{1,2},{2,1},{3,4},{4,3},{5,6},{6,5},{7,8},{8,7},{9,10},{10,9},{11,... | collective-permute-start | bytes 393224 | tf_op jit(solution)/shard_map/ppermute | solution.py:25
  14.0 8.3 %collective-permute-start.3 = (bf16[4,2,64,128]{3,2,1,0:T(8,128)(2,1)S(1)}, bf16[4,2,64,128]{3,2,1,0:T(8,128)(2,1)S(1)}, u32[]{:S(2)}, u32[]{:S(2)}) collective-permute-start(bf16[4,2,64,128]{3,2,1,0:T(8,128)(2,1)S(1)} %get-tuple-element.30), channel_id=1, source_target_pairs={{0,1},{1,0},{2,3},{3,2},{4,5},{5,4},{6,7},{7,6},{8,9},{9,8},{10,11... | collective-permute-start | bytes 393224 | tf_op jit(solution)/shard_map/ppermute | solution.py:17
  16.0 0.7 copy-start.10
  16.7 0.7 copy-start.12
  18.2 28.9 %copy-start.11 = (s32[1,96,4]{1,2,0:T(4,128)S(1)}, s32[1,96,4]{1,2,0:T(4,128)}, u32[]{:S(2)}) copy-start(s32[1,96,4]{1,2,0:T(4,128)} %param.8) | copy-start | bytes 4612
  22.3 10.9 %copy-start.3 = (bf16[4,2,64,128]{3,2,1,0:T(8,128)(2,1)}, bf16[4,2,64,128]{3,2,1,0:T(8,128)(2,1)S(1)}, u32[]{:S(2)}) copy-start(bf16[4,2,64,128]{3,2,1,0:T(8,128)(2,1)S(1)} %collective-permute-done.3.cross_near) | copy-start | bytes 393220
  22.3 19.5 %copy-start.8 = (bf16[2,8,64,128]{3,2,1,0:T(8,128)(2,1)}, bf16[2,8,64,128]{3,2,1,0:T(8,128)(2,1)S(1)}, u32[]{:S(2)}) copy-start(bf16[2,8,64,128]{3,2,1,0:T(8,128)(2,1)S(1)} %collective-permute-done.1.got_far) | copy-start | bytes 786436
  23.7 23.3 %collective-permute-start.4 = (bf16[2,12,64,128]{3,2,1,0:T(8,128)(2,1)}, bf16[2,12,64,128]{3,2,1,0:T(8,128)(2,1)}, u32[]{:S(2)}, u32[]{:S(2)}) collective-permute-start(bf16[2,12,64,128]{3,2,1,0:T(8,128)(2,1)} %get-tuple-element.35), channel_id=1, source_target_pairs={{0,48},{48,0},{96,144},{144,96},{192,240},{240,192},{288,336},{336... | collective-permute-start | bytes 1179656 | tf_op jit(solution)/shard_map/ppermute | solution.py:17
  25.6 21.4 %collective-permute-start.5 = (bf16[2,4,64,128]{3,2,1,0:T(8,128)(2,1)}, bf16[2,4,64,128]{3,2,1,0:T(8,128)(2,1)}, u32[]{:S(2)}, u32[]{:S(2)}) collective-permute-start(bf16[2,4,64,128]{3,2,1,0:T(8,128)(2,1)} %get-tuple-element.37), channel_id=1, source_target_pairs={{48,96},{96,48},{144,192},{192,144},{240,288},{288,240},{336,384},... | collective-permute-start | bytes 393224 | tf_op jit(solution)/shard_map/ppermute | solution.py:25
  31.3 10.6 %collective-permute-start = (bf16[1,160,128]{2,1,0:T(8,128)(2,1)S(1)}, bf16[1,160,128]{2,1,0:T(8,128)(2,1)S(1)}, u32[]{:S(2)}, u32[]{:S(2)}) collective-permute-start(bf16[1,160,128]{2,1,0:T(8,128)(2,1)S(1)} %payload.1.first_ref), channel_id=1, source_target_pairs={{0,384},{48,432},{96,480},{144,528},{192,576},{240,624},{288,672},... | collective-permute-start | bytes 122888 | tf_op jit(solution)/shard_map/ppermute | solution.py:30
  42.0 0.8 copy-start
  42.8 34.7 %all-to-all-start = ((bf16[8,2,160,128]{3,2,1,0:T(8,128)(2,1)}), bf16[8,2,160,128]{3,2,1,0:T(8,128)(2,1)}, u32[]{:S(2)}, u32[]{:S(2)}) async-start(bf16[8,2,160,128]{3,2,1,0:T(8,128)(2,1)} %copy-done), calls=%async_computation | async-start | bytes 1310720 | tf_op jit(solution)/shard_map/all_to_all | solution.py:36
  47.0 1.0 %copy-start.2 = (bf16[2,8,64,128]{3,2,1,0:T(8,128)(2,1)S(1)}, bf16[2,8,64,128]{3,2,1,0:T(8,128)(2,1)}, u32[]{:S(2)}) copy-start(bf16[2,8,64,128]{3,2,1,0:T(8,128)(2,1)} %copy-done.1) | copy-start | bytes 786436
  48.0 0.9 %copy-start.4 = (bf16[4,2,64,128]{3,2,1,0:T(8,128)(2,1)S(1)}, bf16[4,2,64,128]{3,2,1,0:T(8,128)(2,1)}, u32[]{:S(2)}) copy-start(bf16[4,2,64,128]{3,2,1,0:T(8,128)(2,1)} %copy-done.3) | copy-start | bytes 393220
  48.9 0.9 %copy-start.9 = (bf16[2,8,64,128]{3,2,1,0:T(8,128)(2,1)S(1)}, bf16[2,8,64,128]{3,2,1,0:T(8,128)(2,1)}, u32[]{:S(2)}) copy-start(bf16[2,8,64,128]{3,2,1,0:T(8,128)(2,1)} %copy-done.8) | copy-start | bytes 786436
  52.3 25.3 %copy-start.13 = (s32[4,8]{1,0:T(4,128)S(1)}, s32[4,8]{1,0:T(4,128)}, u32[]{:S(2)}) copy-start(s32[4,8]{1,0:T(4,128)} %agg_ref.3) | copy-start | bytes 388
  52.3 16.0 %collective-permute-start.6 = (bf16[2,12,64,128]{3,2,1,0:T(8,128)(2,1)S(1)}, bf16[2,12,64,128]{3,2,1,0:T(8,128)(2,1)S(1)}, u32[]{:S(2)}, u32[]{:S(2)}) collective-permute-start(bf16[2,12,64,128]{3,2,1,0:T(8,128)(2,1)S(1)} %get-tuple-element.40), channel_id=1, source_target_pairs={{0,48},{48,0},{96,144},{144,96},{192,240},{240,192},{288,336},{336... | collective-permute-start | bytes 1179656 | tf_op jit(solution)/shard_map/ppermute | solution.py:17
  54.7 13.6 %collective-permute-start.8 = (bf16[2,4,64,128]{3,2,1,0:T(8,128)(2,1)S(1)}, bf16[2,4,64,128]{3,2,1,0:T(8,128)(2,1)S(1)}, u32[]{:S(2)}, u32[]{:S(2)}) collective-permute-start(bf16[2,4,64,128]{3,2,1,0:T(8,128)(2,1)S(1)} %get-tuple-element.44), channel_id=1, source_target_pairs={{48,96},{96,48},{144,192},{192,144},{240,288},{288,240},{336,384},... | collective-permute-start | bytes 393224 | tf_op jit(solution)/shard_map/ppermute | solution.py:25
  58.7 22.4 %collective-permute-start.7 = (bf16[2,8,64,128]{3,2,1,0:T(8,128)(2,1)}, bf16[2,8,64,128]{3,2,1,0:T(8,128)(2,1)}, u32[]{:S(2)}, u32[]{:S(2)}) collective-permute-start(bf16[2,8,64,128]{3,2,1,0:T(8,128)(2,1)} %get-tuple-element.41), channel_id=1, source_target_pairs={{48,96},{96,48},{144,192},{192,144},{240,288},{288,240},{336,384},... | collective-permute-start | bytes 786440 | tf_op jit(solution)/shard_map/ppermute | solution.py:25
  67.5 0.8 copy-start.6
  68.9 12.2 %collective-permute-start.10 = (bf16[4,2,64,128]{3,2,1,0:T(8,128)(2,1)S(1)}, bf16[4,2,64,128]{3,2,1,0:T(8,128)(2,1)S(1)}, u32[]{:S(2)}, u32[]{:S(2)}) collective-permute-start(bf16[4,2,64,128]{3,2,1,0:T(8,128)(2,1)S(1)} %get-tuple-element.46), channel_id=1, source_target_pairs={{1,2},{2,1},{3,4},{4,3},{5,6},{6,5},{7,8},{8,7},{9,10},{10,9},{11,... | collective-permute-start | bytes 393224 | tf_op jit(solution)/shard_map/ppermute | solution.py:25
  75.6 6.9 %collective-permute-start.9 = (bf16[4,2,64,128]{3,2,1,0:T(8,128)(2,1)S(1)}, bf16[4,2,64,128]{3,2,1,0:T(8,128)(2,1)S(1)}, u32[]{:S(2)}, u32[]{:S(2)}) collective-permute-start(bf16[4,2,64,128]{3,2,1,0:T(8,128)(2,1)S(1)} %get-tuple-element.45), channel_id=1, source_target_pairs={{0,1},{1,0},{2,3},{3,2},{4,5},{5,4},{6,7},{7,6},{8,9},{9,8},{10,11... | collective-permute-start | bytes 393224 | tf_op jit(solution)/shard_map/ppermute | solution.py:17
  82.5 1.0 %copy-start.7 = (bf16[4,8,64,128]{3,2,1,0:T(8,128)(2,1)S(1)}, bf16[4,8,64,128]{3,2,1,0:T(8,128)(2,1)}, u32[]{:S(2)}) copy-start(bf16[4,8,64,128]{3,2,1,0:T(8,128)(2,1)} %copy-done.6) | copy-start | bytes 1572868

commit v4 on v3

v4 whole, which is shorter than its diff:
```python
import jax
import jax.numpy as jnp
from jax import lax
from jax.experimental import pallas as pl
from jax.experimental.pallas import tpu as pltpu
from jax.sharding import PartitionSpec as P

BF16 = jnp.bfloat16
F32 = jnp.float32
MIB = 1 << 20
VMEM = pl.BlockSpec(memory_space=pltpu.VMEM)
SMEM = pl.BlockSpec(memory_space=pltpu.SMEM)


def swap_near(values, axis):
    count = lax.axis_size(axis)
    return lax.ppermute(values, axis, [(i, i ^ 1) for i in range(count) if i ^ 1 < count])


def swap_far(values, axis):
    count = lax.axis_size(axis)
    pairs = []
    for i in range(1, count - 1, 2):
        pairs += [(i, i + 1), (i + 1, i)]
    return lax.ppermute(values, axis, pairs)


def far_of(index):
    return index + 1 if index % 2 else index - 1


def swap_diagonal(values, other):
    count, wide = lax.axis_size("stream"), lax.axis_size("cross")
    pairs = []
    for i in range(count):
        for j in range(wide):
            k, m = far_of(i), other(j)
            if 0 <= k < count and 0 <= m < wide:
                pairs.append((i * wide + j, k * wide + m))
    return lax.ppermute(values, ("stream", "cross"), pairs)


def swap_halves(values, axis):
    count = lax.axis_size(axis)
    return lax.ppermute(values, axis, [(i, (i + count // 2) % count) for i in range(count)])


def exchange_in_half(values, axis):
    half = lax.axis_size(axis) // 2
    groups = [list(range(half)), list(range(half, 2 * half))]
    return lax.all_to_all(values, axis, 0, 0, axis_index_groups=groups)


def shaped(shape, dtype):
    return jax.ShapeDtypeStruct(shape, dtype)


def call(kernel, name, outs, ins, specs, out_specs, limit, flops=0, moved=0, scratch=()):
    return pl.pallas_call(
        kernel,
        out_shape=outs,
        in_specs=specs,
        out_specs=out_specs,
        scratch_shapes=list(scratch),
        cost_estimate=pl.CostEstimate(flops=flops, bytes_accessed=moved, transcendentals=0),
        compiler_params=pltpu.CompilerParams(vmem_limit_bytes=limit * MIB),
        name=name,
    )(*ins)


def parities(info_ref):
    return info_ref[1] % 2, info_ref[2] % 2


def mask_kernel(
    info_ref, residual_ref, near_ref, far_ref, cross_near, cross_far, corner_near, corner_far
):
    rows, columns = residual_ref.shape[:2]
    half = rows // 2
    p, q = parities(info_ref)
    for out_ref, start in ((near_ref, half * (1 - p)), (far_ref, half * p)):
        for i in range(half):
            for j in range(columns):
                block = residual_ref[start + i, j]
                live = (start + i) * columns + j < info_ref[0]
                out_ref[i, j] = jnp.where(live, block, jnp.zeros_like(block))
    for out_ref, corner, start in (
        (cross_near, corner_near, (columns - 2) * (1 - q)),
        (cross_far, corner_far, (columns - 2) * q),
    ):
        for i in range(rows):
            for j in range(2):
                block = residual_ref[i, start + j]
                live = i * columns + start + j < info_ref[0]
                out_ref[i, j] = jnp.where(live, block, jnp.zeros_like(block))
        for i in range(half):
            for j in range(2):
                corner[i, j] = far_ref[i, start + j]


def mask_blocks(info, residual):
    rows, columns, width, sides = residual.shape
    wide = shaped((rows // 2, columns, width, sides), BF16)
    tall = shaped((rows, 2, width, sides), BF16)
    corner = shaped((rows // 2, 2, width, sides), BF16)
    return call(
        mask_kernel, "mask_blocks", (wide, wide, tall, tall, corner, corner), (info, residual),
        [SMEM, VMEM], (VMEM,) * 6, 4, moved=4 * residual.size,
    )


def split_dot(left, right):
    high = right.astype(BF16)
    low = (right - high.astype(F32)).astype(BF16)
    return jnp.dot(left, high, preferred_element_type=F32) + jnp.dot(
        left, low, preferred_element_type=F32
    )


def aggregate_at(index, half, size):
    per = size // 4
    slot, rest = index // (2 * size), index % (2 * size)
    return (slot + half * (rest // size)) * per + rest % size // 4


def partial_kernel(info_ref, agg_ref, near_ref, far_ref, out_ref, sums_ref):
    unknowns, sides = near_ref.shape
    rows, columns = agg_ref.shape
    fields = rows * columns * 2
    cells = unknowns // fields
    slots, height, _ = out_ref.shape
    p, _ = parities(info_ref)
    row = lax.broadcasted_iota(jnp.int32, (fields, unknowns), 0)
    column = lax.broadcasted_iota(jnp.int32, (fields, unknowns), 1)
    picks = jnp.where(column // cells == row, 1.0, 0.0).astype(BF16)
    for source, start in ((near_ref, fields * (1 - p)), (far_ref, fields * p)):
        sums_ref[pl.ds(pl.multiple_of(start, fields), fields), :] = jnp.dot(
            picks, source[...], preferred_element_type=F32
        )
    lane = lax.broadcasted_iota(jnp.int32, (1, 2 * fields), 1) // 4
    labels = jnp.zeros((1, 2 * fields), jnp.int32)
    for i in range(rows):
        for j in range(columns):
            labels = jnp.where(lane == i * columns + j, agg_ref[i, j], labels)
    shape = (slots * height, 2 * fields)
    row = lax.broadcasted_iota(jnp.int32, (shape[0], 1), 0)
    label = aggregate_at(row, slots, height // 2)
    column = lax.broadcasted_iota(jnp.int32, shape, 1)
    row = lax.broadcasted_iota(jnp.int32, shape, 0)
    onehot = jnp.where((label == labels) & (row % 4 == column % 4), 1.0, 0.0)
    found = split_dot(onehot.astype(BF16), sums_ref[...])
    out_ref[...] = found.astype(BF16).reshape(out_ref.shape)


def partial_sums(info, agg, near, far, slots, size):
    sides = near.shape[-1]
    flat = (near.size // sides, sides)
    return call(
        partial_kernel, "partial_sums", shaped((slots, 2 * size, sides), BF16),
        (info, agg, near.reshape(flat), far.reshape(flat)), [SMEM, SMEM, VMEM, VMEM], VMEM, 6,
        flops=1 << 25, moved=4 * near.size,
        scratch=[pltpu.VMEM((agg.size * 4, sides), F32)],
    )


def half_kernel(parts_ref, inverse_ref, out_ref):
    slots, height, sides = parts_ref.shape
    size = inverse_ref.shape[0]
    total = parts_ref[0].astype(F32)
    for i in range(1, slots):
        total = total + parts_ref[i].astype(F32)
    out_ref[:height] = total.astype(BF16)
    row = lax.broadcasted_iota(jnp.int32, (size, sides), 0)
    column = lax.broadcasted_iota(jnp.int32, (size, sides), 1)
    rest = inverse_ref[...]
    tail = jnp.zeros((size, sides), F32)
    for term in range(3):
        part = rest.astype(BF16)
        rest = rest - part.astype(F32)
        place = jnp.where(column == row + term * size, 1.0, 0.0).astype(BF16)
        tail = tail + jnp.dot(part, place, preferred_element_type=F32)
    out_ref[height:] = tail.astype(BF16)


def half_sums(parts, inverse):
    _, height, sides = parts.shape
    size = inverse.shape[0]
    return call(
        half_kernel, "half_sums", shaped((height + size, sides), BF16), (parts, inverse),
        [VMEM, VMEM], VMEM, 2, flops=4 * parts.size, moved=2 * parts.size,
    )


def solve_kernel(info_ref, own_ref, other_ref, out_ref):
    slots, height, sides = out_ref.shape
    size = height // 2
    high = info_ref[1] // slots
    for source, u in ((own_ref, high), (other_ref, 1 - high)):
        start = pl.multiple_of(u * size, size)
        mine = own_ref[pl.ds(start, size), :].astype(F32)
        mine = mine + other_ref[pl.ds(start, size), :].astype(F32)
        stacked = jnp.concatenate([mine, mine, mine, jnp.zeros_like(mine)], axis=0)
        coarse = split_dot(source[pl.ds(height, size), :], stacked).astype(BF16)
        for i in range(slots):
            out_ref[i, pl.ds(start, size), :] = coarse


def coarse_solve(info, own, other, slots, size):
    sides = own.shape[-1]
    return call(
        solve_kernel, "coarse_solve", shaped((slots, 2 * size, sides), BF16),
        (info, own, other), [SMEM, VMEM, VMEM], VMEM, 2, flops=1 << 22, moved=4 * own.size,
    )


def near_kernel(info_ref, own_near, cross_near, cross_far, near_ref):
    half, columns = own_near.shape[:2]
    p, _ = parities(info_ref)
    start = half * (1 - p)
    for i in range(half):
        for j in range(columns):
            near_ref[i, j] = own_near[i, j]
        for j in range(2):
            near_ref[i, columns + j] = cross_near[start + i, j]
            near_ref[i, columns + 2 + j] = cross_far[start + i, j]


def near_message(info, own_near, cross_near, cross_far):
    half, columns, width, sides = own_near.shape
    return call(
        near_kernel, "near_message", shaped((half, columns + 4, width, sides), BF16),
        (info, own_near, cross_near, cross_far), [SMEM, VMEM, VMEM, VMEM], VMEM, 3,
        moved=8 * cross_near.size,
    )


def fix_of(pattern_ref, blocks_ref, grid_ref, n):
    picked = jnp.concatenate([grid_ref[pattern_ref[k, n]] for k in range(4)], axis=0)
    return jnp.dot(blocks_ref[n], picked, preferred_element_type=F32).astype(BF16)


def margin_kernel(
    info_ref, pattern_ref, blocks_ref,
    own_near, own_far, got_near, got_far, cross_near, cross_far, got_corner_near, got_corner_far,
    out_near, out_far, corner_near, corner_far, grid_ref,
):
    half, columns = own_near.shape[:2]
    rows = 2 * half
    wide = columns + 4
    p, q = parities(info_ref)
    near_row, far_row = (rows + 2) * (1 - p), (rows + 2) * p
    near_column, far_column = (columns + 2) * (1 - q), (columns + 2) * q
    for source, start in (
        (own_near, 2 + half * (1 - p)), (own_far, 2 + half * p),
        (got_near, near_row), (got_far, far_row),
    ):
        for i in range(2):
            for j in range(columns):
                grid_ref[(start + i) * wide + 2 + j] = source[i, j]
    for source, start in ((cross_near, near_column), (cross_far, far_column)):
        for i in range(rows):
            for j in range(2):
                grid_ref[(2 + i) * wide + start + j] = source[i, j]
    for i in range(2):
        for j in range(2):
            near, far = (near_row + i) * wide + j, (far_row + i) * wide + j
            grid_ref[near + near_column] = got_near[i, columns + j]
            grid_ref[near + far_column] = got_near[i, columns + 2 + j]
            grid_ref[far + near_column] = got_corner_near[i, j]
            grid_ref[far + far_column] = got_corner_far[i, j]

    def fix(n):
        return fix_of(pattern_ref, blocks_ref, grid_ref, n)

    for i in range(2):
        near, far = (near_row + i) * wide, (far_row + i) * wide
        for j in range(columns):
            out_far[i, j] = fix(far + 2 + j)
            out_near[i, j] = fix(near + 2 + j)
        for j in range(2):
            corner_near[i, j] = fix(far + near_column + j)
            corner_far[i, j] = fix(far + far_column + j)
            out_near[i, columns + j] = fix(near + near_column + j)
            out_near[i, columns + 2 + j] = fix(near + far_column + j)


def margin_fixes(info, pattern, blocks, pieces):
    count, width, depth = blocks.shape
    half, columns, _, sides = pieces[0].shape
    near = shaped((2, columns + 4, width, sides), BF16)
    main = shaped((2, columns, width, sides), BF16)
    corner = shaped((2, 2, width, sides), BF16)
    grid = shaped((count, width, sides), BF16)
    return call(
        margin_kernel, "margin_fixes", (near, main, corner, corner, grid),
        (info, pattern, blocks) + pieces, [SMEM, SMEM] + [VMEM] * 9, (VMEM,) * 5, 12,
        flops=blocks.size * sides, moved=2 * blocks.size,
    )


def center_kernel(info_ref, pattern_ref, blocks_ref, grid_ref, side_near, side_far, center_ref):
    rows, columns = center_ref.shape[:2]
    wide = columns + 4
    _, q = parities(info_ref)
    near_column, far_column = (columns + 2) * (1 - q), (columns + 2) * q
    for i in range(rows):
        base = (2 + i) * wide
        for j in range(2):
            side_near[i, j] = fix_of(pattern_ref, blocks_ref, grid_ref, base + near_column + j)
            side_far[i, j] = fix_of(pattern_ref, blocks_ref, grid_ref, base + far_column + j)
        for j in range(columns):
            center_ref[i, j] = fix_of(pattern_ref, blocks_ref, grid_ref, base + 2 + j)


def center_fixes(info, pattern, blocks, grid, rows, columns):
    _, width, sides = grid.shape
    side = shaped((rows, 2, width, sides), BF16)
    return call(
        center_kernel, "center_fixes",
        (side, side, shaped((rows, columns, width, sides), BF16)),
        (info, pattern, blocks, grid), [SMEM, SMEM, VMEM, VMEM], (VMEM,) * 3, 12,
        flops=blocks.size * sides, moved=2 * blocks.size,
    )


def fold_kernel(info_ref, side_near, side_far, got_near, out_near, out_far):
    half, wide = got_near.shape[:2]
    p, _ = parities(info_ref)
    fold, keep = half * (1 - p), half * p
    for i in range(half):
        for j in range(2):
            for side, out, at in ((side_near, out_near, j), (side_far, out_far, 2 + j)):
                total = side[fold + i, j].astype(F32) + got_near[i, wide - 4 + at].astype(F32)
                out[fold + i, j] = total.astype(BF16)
                out[keep + i, j] = side[keep + i, j]


def fold_sides(info, side_near, side_far, got_near):
    piece = shaped(side_near.shape, BF16)
    return call(
        fold_kernel, "fold_sides", (piece, piece), (info, side_near, side_far, got_near),
        [SMEM] + [VMEM] * 3, (VMEM, VMEM), 3, flops=2 * side_near.size, moved=12 * side_near.size,
    )


def lift_kernel(agg_ref, coarse_ref, out_ref):
    slots, height, sides = coarse_ref.shape
    rows, columns = agg_ref.shape
    fields = rows * columns * 4
    shape = (fields, slots * height)
    row = lax.broadcasted_iota(jnp.int32, (fields, 1), 0) // 4
    labels = jnp.zeros((fields, 1), jnp.int32)
    for i in range(rows):
        for j in range(columns):
            labels = jnp.where(row == i * columns + j, agg_ref[i, j], labels)
    column = lax.broadcasted_iota(jnp.int32, (1, shape[1]), 1)
    label = aggregate_at(column, slots, height // 2)
    row = lax.broadcasted_iota(jnp.int32, shape, 0)
    column = lax.broadcasted_iota(jnp.int32, shape, 1)
    onehot = jnp.where((label == labels) & (column % 4 == row % 4), 1.0, 0.0)
    coarse = coarse_ref[...].reshape(shape[1], sides)
    out_ref[...] = jnp.dot(onehot.astype(BF16), coarse, preferred_element_type=F32)


def lift(agg, coarse):
    sides = coarse.shape[-1]
    return call(
        lift_kernel, "lift", shaped((agg.size * 4, sides), F32), (agg, coarse), [SMEM, VMEM],
        VMEM, 3, flops=1 << 24, moved=2 * coarse.size,
    )


def join_kernel(
    info_ref, lifted_ref, center_ref, main_near, main_far, cross_near, cross_far,
    corner_near, corner_far, out_ref,
):
    rows, columns, width, sides = center_ref.shape
    half = rows // 2
    cells = width // 4
    p, q = parities(info_ref)
    for i in range(rows):
        for j in range(columns):
            block = i * columns + j
            lifted = jnp.concatenate(
                [
                    jnp.broadcast_to(lifted_ref[pl.ds(block * 4 + f, 1), :], (cells, sides))
                    for f in range(4)
                ],
                axis=0,
            )
            out_ref[i, j] = center_ref[i, j].astype(F32) + lifted
    for source, start in ((main_near, half * (1 - p)), (main_far, half * p)):
        for i in range(half):
            for j in range(columns):
                out_ref[start + i, j] += source[i, j].astype(F32)
    for source, start in ((cross_near, (columns - 2) * (1 - q)), (cross_far, (columns - 2) * q)):
        for i in range(rows):
            for j in range(2):
                out_ref[i, start + j] += source[i, j].astype(F32)
    for source, start in (
        (corner_near, (columns - 2) * (1 - q)), (corner_far, (columns - 2) * q)
    ):
        for i in range(half):
            for j in range(2):
                out_ref[half * p + i, start + j] += source[i, j].astype(F32)
    for i in range(rows):
        for j in range(columns):

            @pl.when(i * columns + j >= info_ref[0])
            def _(i=i, j=j):
                out_ref[i, j] = jnp.zeros((width, sides), F32)


def join(info, lifted, center, pieces):
    return call(
        join_kernel, "join", shaped(center.shape, F32), (info, lifted, center) + pieces,
        [SMEM] + [VMEM] * 8, VMEM, 6, flops=8 * center.size, moved=10 * center.size,
    )


def body(residual, approx_inverse, pattern, live_blocks, block_aggregate, coarse_inverse):
    rows, columns = residual.shape[:2]
    info = jnp.stack([live_blocks[0, 0], lax.axis_index("stream"), lax.axis_index("cross")])
    own_near, own_far, edge_near, edge_far, corner_near, corner_far = mask_blocks(info, residual)
    slots, size = lax.axis_size("stream") // 2, coarse_inverse.shape[0]
    parts = partial_sums(info, block_aggregate, own_near, own_far, slots, size)
    got_far = swap_far(own_far, "stream")
    cross_far = swap_far(edge_far, "cross")
    cross_near = swap_near(edge_near, "cross")
    corner_near = swap_diagonal(corner_near, lambda j: j ^ 1)
    corner_far = swap_diagonal(corner_far, far_of)
    blocks, links = approx_inverse[0], jnp.transpose(pattern[0])
    blocks, parts = lax.optimization_barrier((blocks, parts))
    blocks = jnp.where(info[0] > 0, blocks, jnp.zeros((), BF16))
    parts = exchange_in_half(parts, "stream")
    own_sums = half_sums(parts, coarse_inverse)
    got_far, cross_far, cross_near, blocks, own_sums = lax.optimization_barrier(
        (got_far, cross_far, cross_near, blocks, own_sums)
    )
    other_sums = swap_halves(own_sums, "stream")
    got_near = swap_near(near_message(info, own_near, cross_near, cross_far), "stream")
    got_near, other_sums = lax.optimization_barrier((got_near, other_sums))
    pieces = (
        own_near, own_far, got_near, got_far, cross_near, cross_far, corner_near, corner_far
    )
    near, far, corner_near, corner_far, grid = margin_fixes(info, links, blocks, pieces)
    far, near, other_sums = lax.optimization_barrier((far, near, other_sums))
    far = swap_far(far, "stream")
    near = swap_near(near, "stream")
    side_near, side_far, center = center_fixes(info, links, blocks, grid, rows, columns)
    side_near, side_far = fold_sides(info, side_near, side_far, near)
    cross_far = swap_far(side_far, "cross")
    cross_near = swap_near(side_near, "cross")
    corner_near = swap_diagonal(corner_near, lambda j: j ^ 1)
    corner_far = swap_diagonal(corner_far, far_of)
    coarse = coarse_solve(info, own_sums, other_sums, slots, size)
    lifted = lift(block_aggregate, exchange_in_half(coarse, "stream"))
    pieces = (near, far, cross_near, cross_far, corner_near, corner_far)
    return join(info, lifted, center, pieces)


def solution(mesh):
    placed = (
        P("stream", "cross", None, None),
        P("stream", "cross", None, None),
        P("stream", "cross", None),
        P("stream", "cross"),
        P("stream", "cross"),
        P("stream", "cross"),
    )
    return jax.shard_map(
        body,
        mesh=mesh,
        in_specs=placed,
        out_specs=P("stream", "cross", None, None),
        check_vma=False,
    )
```

time: 86.7 us -> 102 us (1.18)
  the two profiles are of different devices: /device:TPU:248 before, /device:TPU:176 now
where the time goes in v4:
time: 102 us
  starting transfers between devices  61.3 us (60%)
  waiting for transfers between devices  17.2 us (17%)
  Pallas kernels  14.4 us (14%)
  local copies, waits for them, and re-layouts  5.51 us (5%)
  other arithmetic  2.18 us (2%)
    ppermute x4, starting transfers between devices, swap_diagonal(): return lax.ppermute(values, ('stream', 'cross'), pairs)  23.2 us
    ppermute x4, starting transfers between devices, swap_far(): return lax.ppermute(values, axis, pairs)  16 us
    pallas_call x10, Pallas kernels, call(): pl.pallas_call(kernel, out_shape=outs, in_specs=specs, out_specs=out_spec...  14.4 us
    ppermute x4, starting transfers between devices, swap_near(): lax.ppermute(values, axis, [(i, i ^ 1) for i in range(count) if i ^ 1 < c...  12.8 us
    ppermute x4, waiting for transfers between devices, swap_diagonal(): return lax.ppermute(values, ('stream', 'cross'), pairs)  8.19 us
    ppermute x1, waiting for transfers between devices, swap_halves(): lax.ppermute(values, axis, [(i, (i + count // 2) % count) for i in range(...  7.7 us
    all_to_all x2, starting transfers between devices, exchange_in_half(): return lax.all_to_all(values, axis, 0, 0, axis_index_groups=groups)  7.37 us
    unnamed x22, local copies, waits for them, and re-layouts  5.51 us
  transfers between devices with their start and end apart: 15, of which 3 were waited for; matrix products, arithmetic and copies ran while one was open for 2% of the time, Pallas kernels for 7%

profile of v4, /device:TPU:176, one launch (start us, length us, event | category | flops | bytes accessed | tf_op | source)
XLA Modules:
  0.0 101.5 jit_solution(13823228389031629359)
XLA Ops:
  0.7 0.1 pad_add_fusion.info_ref
  0.7 0.0 copy-start
  0.7 1.0 %copy-done = bf16[4,8,64,128]{3,2,1,0:T(8,128)(2,1)S(1)} copy-done((bf16[4,8,64,128]{3,2,1,0:T(8,128)(2,1)S(1)}, bf16[4,8,64,128]{3,2,1,0:T(8,128)(2,1)}, u32[]{:S(2)}) %copy-start) | copy-done | bytes 524312
  1.8 1.5 %mask_blocks.1 = (bf16[2,8,64,128]{3,2,1,0:T(8,128)(2,1)S(1)}, bf16[2,8,64,128]{3,2,1,0:T(8,128)(2,1)}, bf16[4,2,64,128]{3,2,1,0:T(8,128)(2,1)}, bf16[4,2,64,128...) custom-call(s32[3]{0:T(128)S(1)} %pad_add_fusion.info_ref, ...), custom_call_target="tpu_custom_call" | custom-call | bytes 1048576 | tf_op jit(solution)/shard_map/mask_blocks/pallas_call | solution.py:59
  3.3 0.0 copy-start.7
  3.3 0.6 copy-done.7
  3.9 0.0 copy-start.8
  3.9 0.6 copy-done.8
  4.5 5.4 %collective-permute-start = (bf16[2,8,64,128]{3,2,1,0:T(8,128)(2,1)}, bf16[2,8,64,128]{3,2,1,0:T(8,128)(2,1)}, u32[]{:S(2)}, u32[]{:S(2)}) collective-permute-start(bf16[2,8,64,128]{3,2,1,0:T(8,128)(2,1)} %get-tuple-element.33.own_far), channel_id=1, source_target_pairs={{48,96},{96,48},{144,192},{192,144},{240,288},{288,240},{336,384},... | collective-permute-start | bytes 786440 | tf_op jit(solution)/shard_map/ppermute | solution.py:25
  9.9 0.0 copy-start.5
  10.0 0.7 copy-done.5
  10.6 2.1 %partial_sums.1 = bf16[8,64,128]{2,1,0:T(8,128)(2,1)} custom-call(s32[3]{0:T(128)S(1)} %pad_add_fusion.info_ref, s32[4,8]{1,0:T(4,128)S(1)} %copy-done.5, bf16[1024,128]{1,0:T(8,128)(2,1)S(1)} %bitcast.11, bf16[1024,128]{1,0:T(8,128)(2,1)} %bitcast.6.far_ref), custom_call_target="tpu_custom_call" | custom-call | flops 33554432 | bytes 524288 | tf_op jit(solution)/shard_map/partial_sums/pallas_call | solution.py:59
  12.7 4.0 %all-to-all-start = ((bf16[8,64,128]{2,1,0:T(8,128)(2,1)}), bf16[8,64,128]{2,1,0:T(8,128)(2,1)}, u32[]{:S(2)}, u32[]{:S(2)}) async-start(bf16[8,64,128]{2,1,0:T(8,128)(2,1)} %partial_sums.1), calls=%async_computation | async-start | bytes 262144 | tf_op jit(solution)/shard_map/all_to_all | solution.py:51
  16.7 2.4 %collective-permute-start.1 = (bf16[4,2,64,128]{3,2,1,0:T(8,128)(2,1)}, bf16[4,2,64,128]{3,2,1,0:T(8,128)(2,1)S(1)}, u32[]{:S(2)}, u32[]{:S(2)}) collective-permute-start(bf16[4,2,64,128]{3,2,1,0:T(8,128)(2,1)} %get-tuple-element.34), channel_id=1, source_target_pairs={{1,2},{2,1},{3,4},{4,3},{5,6},{6,5},{7,8},{8,7},{9,10},{10,9},{11,... | collective-permute-start | bytes 393224 | tf_op jit(solution)/shard_map/ppermute | solution.py:25
  19.1 5.1 %collective-permute-start.2 = (bf16[4,2,64,128]{3,2,1,0:T(8,128)(2,1)}, bf16[4,2,64,128]{3,2,1,0:T(8,128)(2,1)}, u32[]{:S(2)}, u32[]{:S(2)}) collective-permute-start(bf16[4,2,64,128]{3,2,1,0:T(8,128)(2,1)} %get-tuple-element.35), channel_id=1, source_target_pairs={{0,1},{1,0},{2,3},{3,2},{4,5},{5,4},{6,7},{7,6},{8,9},{9,8},{10,11... | collective-permute-start | bytes 393224 | tf_op jit(solution)/shard_map/ppermute | solution.py:17
  24.2 0.0 copy-start.4
  24.2 2.1 %broadcast_select_fusion.blocks_ref = bf16[96,64,256]{2,1,0:T(8,128)(2,1)S(1)} fusion(bf16[96,64,256]{2,1,0:T(8,128)(2,1)} %bitcast.14, pred[]{:T(512)} %bitcast.3), kind=kLoop, calls=%fused_computation | loop fusion | flops 1572864 | bytes 6291457 | tf_op jit(solution)/shard_map/jit(_where)/select_n | solution.py:434
  26.3 0.0 all-to-all-done.parts_ref
  26.3 0.0 copy-start.3
  26.3 0.7 copy-done.3
  27.0 1.0 %half_sums.1.own_ref = bf16[96,128]{1,0:T(8,128)(2,1)S(1)} custom-call(bf16[8,64,128]{2,1,0:T(8,128)(2,1)} %all-to-all-done.parts_ref, f32[32,32]{1,0:T(8,128)S(1)} %copy-done.3), custom_call_target="tpu_custom_call" | custom-call | flops 262144 | bytes 131072 | tf_op jit(solution)/shard_map/half_sums/pallas_call | solution.py:59
  28.1 0.0 collective-permute-done.1.cross_far
  28.1 1.3 %collective-permute-done.2.cross_near = bf16[4,2,64,128]{3,2,1,0:T(8,128)(2,1)} collective-permute-done((bf16[4,2,64,128]{3,2,1,0:T(8,128)(2,1)}, bf16[4,2,64,128]{3,2,1,0:T(8,128)(2,1)}, u32[]{:S(2)}, u32[]{:S(2)}) %collective-permute-start.2) | collective-permute-done | bytes 131104 | tf_op jit(solution)/shard_map/ppermute | solution.py:17
  29.4 0.0 collective-permute-done.got_far
  29.4 0.9 near_message.1
  30.3 1.9 %collective-permute-start.3 = (bf16[2,12,64,128]{3,2,1,0:T(8,128)(2,1)S(1)}, bf16[2,12,64,128]{3,2,1,0:T(8,128)(2,1)S(1)}, u32[]{:S(2)}, u32[]{:S(2)}) collective-permute-start(bf16[2,12,64,128]{3,2,1,0:T(8,128)(2,1)S(1)} %near_message.1), channel_id=1, source_target_pairs={{0,48},{48,0},{96,144},{144,96},{192,240},{240,192},{288,336},{336... | collective-permute-start | bytes 1179656 | tf_op jit(solution)/shard_map/ppermute | solution.py:17
  32.3 7.4 %collective-permute-start.5 = (bf16[2,2,64,128]{3,2,1,0:T(8,128)(2,1)}, bf16[2,2,64,128]{3,2,1,0:T(8,128)(2,1)S(1)}, u32[]{:S(2)}, u32[]{:S(2)}) collective-permute-start(bf16[2,2,64,128]{3,2,1,0:T(8,128)(2,1)} %copy-done.8), channel_id=1, source_target_pairs={{48,97},{49,96},{50,99},{51,98},{52,101},{53,100},{54,103},{55,102... | collective-permute-start | bytes 196616 | tf_op jit(solution)/shard_map/ppermute | solution.py:40
  39.7 3.1 %collective-permute-start.6 = (bf16[2,2,64,128]{3,2,1,0:T(8,128)(2,1)}, bf16[2,2,64,128]{3,2,1,0:T(8,128)(2,1)S(1)}, u32[]{:S(2)}, u32[]{:S(2)}) collective-permute-start(bf16[2,2,64,128]{3,2,1,0:T(8,128)(2,1)} %copy-done.7), channel_id=1, source_target_pairs={{49,98},{50,97},{51,100},{52,99},{53,102},{54,101},{55,104},{56,10... | collective-permute-start | bytes 196616 | tf_op jit(solution)/shard_map/ppermute | solution.py:40
  42.8 1.9 %collective-permute-start.4 = (bf16[96,128]{1,0:T(8,128)(2,1)S(1)}, bf16[96,128]{1,0:T(8,128)(2,1)S(1)}, u32[]{:S(2)}, u32[]{:S(2)}) collective-permute-start(bf16[96,128]{1,0:T(8,128)(2,1)S(1)} %half_sums.1.own_ref), channel_id=1, source_target_pairs={{0,384},{48,432},{96,480},{144,528},{192,576},{240,624},{288,672},... | collective-permute-start | bytes 73736 | tf_op jit(solution)/shard_map/ppermute | solution.py:45
  44.7 7.7 %collective-permute-done.4.other_ref = bf16[96,128]{1,0:T(8,128)(2,1)S(1)} collective-permute-done((bf16[96,128]{1,0:T(8,128)(2,1)S(1)}, bf16[96,128]{1,0:T(8,128)(2,1)S(1)}, u32[]{:S(2)}, u32[]{:S(2)}) %collective-permute-start.4) | collective-permute-done | bytes 24608 | tf_op jit(solution)/shard_map/ppermute | solution.py:45
  52.4 0.0 collective-permute-done.3.got_near
  52.4 0.0 collective-permute-done.5.got_corner_near
  52.4 0.0 collective-permute-done.6.got_corner_far
  52.4 0.0 copy-done.4
  52.4 2.5 %margin_fixes.1 = (bf16[2,12,64,128]{3,2,1,0:T(8,128)(2,1)S(1)}, bf16[2,8,64,128]{3,2,1,0:T(8,128)(2,1)}, bf16[2,2,64,128]{3,2,1,0:T(8,128)(2,1)S(1)}, bf16[2,2,...) custom-call(s32[3]{0:T(128)S(1)} %pad_add_fusion.info_ref, s32[4,96]{1,0:T(4,128)S(1)} %bitcast.12, ...), custom_call_target="tpu_custom_call" | custom-call | flops 201326592 | bytes 3145728 | tf_op jit(solution)/shard_map/margin_fixes/pallas_call | solution.py:59
  54.9 0.0 copy-start.9
  54.9 0.0 copy-start.10
  54.9 0.0 copy-start.6
  54.9 1.9 %collective-permute-start.7 = (bf16[2,12,64,128]{3,2,1,0:T(8,128)(2,1)S(1)}, bf16[2,12,64,128]{3,2,1,0:T(8,128)(2,1)S(1)}, u32[]{:S(2)}, u32[]{:S(2)}) collective-permute-start(bf16[2,12,64,128]{3,2,1,0:T(8,128)(2,1)S(1)} %get-tuple-element.53), channel_id=1, source_target_pairs={{0,48},{48,0},{96,144},{144,96},{192,240},{240,192},{288,336},{336... | collective-permute-start | bytes 1179656 | tf_op jit(solution)/shard_map/ppermute | solution.py:17
  56.9 6.3 %collective-permute-start.8 = (bf16[2,8,64,128]{3,2,1,0:T(8,128)(2,1)}, bf16[2,8,64,128]{3,2,1,0:T(8,128)(2,1)}, u32[]{:S(2)}, u32[]{:S(2)}) collective-permute-start(bf16[2,8,64,128]{3,2,1,0:T(8,128)(2,1)} %get-tuple-element.54), channel_id=1, source_target_pairs={{48,96},{96,48},{144,192},{192,144},{240,288},{288,240},{336,384},... | collective-permute-start | bytes 786440 | tf_op jit(solution)/shard_map/ppermute | solution.py:25
  63.1 1.2 %center_fixes.1 = (bf16[4,2,64,128]{3,2,1,0:T(8,128)(2,1)S(1)}, bf16[4,2,64,128]{3,2,1,0:T(8,128)(2,1)S(1)}, bf16[4,8,64,128]{3,2,1,0:T(8,128)(2,1)S(1)}) custom-call(s32[3]{0:T(128)S(1)} %pad_add_fusion.info_ref, s32[4,96]{1,0:T(4,128)S(1)} %bitcast.13, bf16[96,64,256]{2,1,0:T(8,128)(2,1)S(1)} %broadcast_select_fusion.blocks_ref, ...), custom_call_target="tpu_custom_call" | custom-call | flops 201326592 | bytes 3145728 | tf_op jit(solution)/shard_map/center_fixes/pallas_call | solution.py:59
  64.4 0.0 copy-start.1
  64.4 0.8 copy-done.1
  65.2 0.0 collective-permute-done.7.got_near.main_near
  65.2 0.6 fold_sides.1
  65.8 3.9 %collective-permute-start.9 = (bf16[4,2,64,128]{3,2,1,0:T(8,128)(2,1)S(1)}, bf16[4,2,64,128]{3,2,1,0:T(8,128)(2,1)S(1)}, u32[]{:S(2)}, u32[]{:S(2)}) collective-permute-start(bf16[4,2,64,128]{3,2,1,0:T(8,128)(2,1)S(1)} %get-tuple-element.57), channel_id=1, source_target_pairs={{0,1},{1,0},{2,3},{3,2},{4,5},{5,4},{6,7},{7,6},{8,9},{9,8},{10,11... | collective-permute-start | bytes 393224 | tf_op jit(solution)/shard_map/ppermute | solution.py:17
  69.6 1.9 %collective-permute-start.10 = (bf16[4,2,64,128]{3,2,1,0:T(8,128)(2,1)S(1)}, bf16[4,2,64,128]{3,2,1,0:T(8,128)(2,1)S(1)}, u32[]{:S(2)}, u32[]{:S(2)}) collective-permute-start(bf16[4,2,64,128]{3,2,1,0:T(8,128)(2,1)S(1)} %get-tuple-element.58), channel_id=1, source_target_pairs={{1,2},{2,1},{3,4},{4,3},{5,6},{6,5},{7,8},{8,7},{9,10},{10,9},{11,... | collective-permute-start | bytes 393224 | tf_op jit(solution)/shard_map/ppermute | solution.py:25
  71.6 0.0 copy-done.9
  71.6 0.0 copy-done.10
  71.6 1.4 %coarse_solve.1 = bf16[8,64,128]{2,1,0:T(8,128)(2,1)} custom-call(s32[3]{0:T(128)S(1)} %pad_add_fusion.info_ref, bf16[96,128]{1,0:T(8,128)(2,1)S(1)} %half_sums.1.own_ref, bf16[96,128]{1,0:T(8,128)(2,1)S(1)} %collective-permute-done.4.other_ref), custom_call_target="tpu_custom_call" | custom-call | flops 4194304 | bytes 49152 | tf_op jit(solution)/shard_map/coarse_solve/pallas_call | solution.py:59
  73.0 3.4 %all-to-all-start.1 = ((bf16[8,64,128]{2,1,0:T(8,128)(2,1)}), bf16[8,64,128]{2,1,0:T(8,128)(2,1)S(1)}, u32[]{:S(2)}, u32[]{:S(2)}) async-start(bf16[8,64,128]{2,1,0:T(8,128)(2,1)} %coarse_solve.1), calls=%async_computation.1 | async-start | bytes 262144 | tf_op jit(solution)/shard_map/all_to_all | solution.py:51
  76.3 10.8 %collective-permute-start.11 = (bf16[2,2,64,128]{3,2,1,0:T(8,128)(2,1)}, bf16[2,2,64,128]{3,2,1,0:T(8,128)(2,1)S(1)}, u32[]{:S(2)}, u32[]{:S(2)}) collective-permute-start(bf16[2,2,64,128]{3,2,1,0:T(8,128)(2,1)} %copy-done.10), channel_id=1, source_target_pairs={{48,97},{49,96},{50,99},{51,98},{52,101},{53,100},{54,103},{55,102... | collective-permute-start | bytes 196616 | tf_op jit(solution)/shard_map/ppermute | solution.py:40
  87.1 1.9 %collective-permute-start.12 = (bf16[2,2,64,128]{3,2,1,0:T(8,128)(2,1)}, bf16[2,2,64,128]{3,2,1,0:T(8,128)(2,1)S(1)}, u32[]{:S(2)}, u32[]{:S(2)}) collective-permute-start(bf16[2,2,64,128]{3,2,1,0:T(8,128)(2,1)} %copy-done.9), channel_id=1, source_target_pairs={{49,98},{50,97},{51,100},{52,99},{53,102},{54,101},{55,104},{56,10... | collective-permute-start | bytes 196616 | tf_op jit(solution)/shard_map/ppermute | solution.py:40
  89.1 0.0 all-to-all-done.1.coarse_ref
  89.1 0.0 copy-done.6
  89.1 0.8 lift.1.lifted_ref
  89.9 0.0 collective-permute-done.11.corner_near
  89.9 8.2 %collective-permute-done.12.corner_far = bf16[2,2,64,128]{3,2,1,0:T(8,128)(2,1)S(1)} collective-permute-done((bf16[2,2,64,128]{3,2,1,0:T(8,128)(2,1)}, bf16[2,2,64,128]{3,2,1,0:T(8,128)(2,1)S(1)}, u32[]{:S(2)}, u32[]{:S(2)}) %collective-permute-start.12) | collective-permute-done | bytes 65568 | tf_op jit(solution)/shard_map/ppermute | solution.py:40
  98.1 0.0 collective-permute-done.8.main_far
  98.1 0.0 collective-permute-done.9.cross_near
  98.1 0.0 collective-permute-done.10.cross_far
  98.1 0.0 copy-start.2
  98.1 1.0 %copy-done.2 = bf16[4,8,64,128]{3,2,1,0:T(8,128)(2,1)S(1)} copy-done((bf16[4,8,64,128]{3,2,1,0:T(8,128)(2,1)S(1)}, bf16[4,8,64,128]{3,2,1,0:T(8,128)(2,1)}, u32[]{:S(2)}) %copy-start.2) | copy-done | bytes 524312
  99.1 2.4 %join.1 = f32[4,8,64,128]{3,2,1,0:T(8,128)} custom-call(s32[3]{0:T(128)S(1)} %pad_add_fusion.info_ref, f32[128,128]{1,0:T(8,128)S(1)} %lift.1.lifted_ref, bf16[4,8,64,128]{3,2,1,0:T(8,128)(2,1)S(1)} %copy-done.2, bf16[2,12,64,128]{3,2,1,0:T(8,128)(2,1)S(1)} %collective-permute-done.7.got_near.main_near, ...), custom_call_target="tpu_custom_call" | custom-call | flops 2097152 | bytes 2621440 | tf_op jit(solution)/shard_map/join/pallas_call | solution.py:59
Async XLA Ops:
  0.7 1.0 %copy-start = (bf16[4,8,64,128]{3,2,1,0:T(8,128)(2,1)S(1)}, bf16[4,8,64,128]{3,2,1,0:T(8,128)(2,1)}, u32[]{:S(2)}) copy-start(bf16[4,8,64,128]{3,2,1,0:T(8,128)(2,1)} %residual_ref.1) | copy-start | bytes 1572868
  3.3 0.6 copy-start.7
  3.9 0.6 copy-start.8
  4.5 24.9 %collective-permute-start = (bf16[2,8,64,128]{3,2,1,0:T(8,128)(2,1)}, bf16[2,8,64,128]{3,2,1,0:T(8,128)(2,1)}, u32[]{:S(2)}, u32[]{:S(2)}) collective-permute-start(bf16[2,8,64,128]{3,2,1,0:T(8,128)(2,1)} %get-tuple-element.33.own_far), channel_id=1, source_target_pairs={{48,96},{96,48},{144,192},{192,144},{240,288},{288,240},{336,384},... | collective-permute-start | bytes 786440 | tf_op jit(solution)/shard_map/ppermute | solution.py:25
  9.9 0.7 copy-start.5
  12.7 13.6 %all-to-all-start = ((bf16[8,64,128]{2,1,0:T(8,128)(2,1)}), bf16[8,64,128]{2,1,0:T(8,128)(2,1)}, u32[]{:S(2)}, u32[]{:S(2)}) async-start(bf16[8,64,128]{2,1,0:T(8,128)(2,1)} %partial_sums.1), calls=%async_computation | async-start | bytes 262144 | tf_op jit(solution)/shard_map/all_to_all | solution.py:51
  16.7 11.4 %collective-permute-start.1 = (bf16[4,2,64,128]{3,2,1,0:T(8,128)(2,1)}, bf16[4,2,64,128]{3,2,1,0:T(8,128)(2,1)S(1)}, u32[]{:S(2)}, u32[]{:S(2)}) collective-permute-start(bf16[4,2,64,128]{3,2,1,0:T(8,128)(2,1)} %get-tuple-element.34), channel_id=1, source_target_pairs={{1,2},{2,1},{3,4},{4,3},{5,6},{6,5},{7,8},{8,7},{9,10},{10,9},{11,... | collective-permute-start | bytes 393224 | tf_op jit(solution)/shard_map/ppermute | solution.py:25
  19.1 10.3 %collective-permute-start.2 = (bf16[4,2,64,128]{3,2,1,0:T(8,128)(2,1)}, bf16[4,2,64,128]{3,2,1,0:T(8,128)(2,1)}, u32[]{:S(2)}, u32[]{:S(2)}) collective-permute-start(bf16[4,2,64,128]{3,2,1,0:T(8,128)(2,1)} %get-tuple-element.35), channel_id=1, source_target_pairs={{0,1},{1,0},{2,3},{3,2},{4,5},{5,4},{6,7},{7,6},{8,9},{9,8},{10,11... | collective-permute-start | bytes 393224 | tf_op jit(solution)/shard_map/ppermute | solution.py:17
  24.2 28.2 %copy-start.4 = (s32[1,96,4]{1,2,0:T(4,128)S(1)}, s32[1,96,4]{1,2,0:T(4,128)}, u32[]{:S(2)}) copy-start(s32[1,96,4]{1,2,0:T(4,128)} %param.8) | copy-start | bytes 4612
  26.3 0.7 copy-start.3
  30.3 22.1 %collective-permute-start.3 = (bf16[2,12,64,128]{3,2,1,0:T(8,128)(2,1)S(1)}, bf16[2,12,64,128]{3,2,1,0:T(8,128)(2,1)S(1)}, u32[]{:S(2)}, u32[]{:S(2)}) collective-permute-start(bf16[2,12,64,128]{3,2,1,0:T(8,128)(2,1)S(1)} %near_message.1), channel_id=1, source_target_pairs={{0,48},{48,0},{96,144},{144,96},{192,240},{240,192},{288,336},{336... | collective-permute-start | bytes 1179656 | tf_op jit(solution)/shard_map/ppermute | solution.py:17
  32.3 20.1 %collective-permute-start.5 = (bf16[2,2,64,128]{3,2,1,0:T(8,128)(2,1)}, bf16[2,2,64,128]{3,2,1,0:T(8,128)(2,1)S(1)}, u32[]{:S(2)}, u32[]{:S(2)}) collective-permute-start(bf16[2,2,64,128]{3,2,1,0:T(8,128)(2,1)} %copy-done.8), channel_id=1, source_target_pairs={{48,97},{49,96},{50,99},{51,98},{52,101},{53,100},{54,103},{55,102... | collective-permute-start | bytes 196616 | tf_op jit(solution)/shard_map/ppermute | solution.py:40
  39.7 12.7 %collective-permute-start.6 = (bf16[2,2,64,128]{3,2,1,0:T(8,128)(2,1)}, bf16[2,2,64,128]{3,2,1,0:T(8,128)(2,1)S(1)}, u32[]{:S(2)}, u32[]{:S(2)}) collective-permute-start(bf16[2,2,64,128]{3,2,1,0:T(8,128)(2,1)} %copy-done.7), channel_id=1, source_target_pairs={{49,98},{50,97},{51,100},{52,99},{53,102},{54,101},{55,104},{56,10... | collective-permute-start | bytes 196616 | tf_op jit(solution)/shard_map/ppermute | solution.py:40
  42.8 9.6 %collective-permute-start.4 = (bf16[96,128]{1,0:T(8,128)(2,1)S(1)}, bf16[96,128]{1,0:T(8,128)(2,1)S(1)}, u32[]{:S(2)}, u32[]{:S(2)}) collective-permute-start(bf16[96,128]{1,0:T(8,128)(2,1)S(1)} %half_sums.1.own_ref), channel_id=1, source_target_pairs={{0,384},{48,432},{96,480},{144,528},{192,576},{240,624},{288,672},... | collective-permute-start | bytes 73736 | tf_op jit(solution)/shard_map/ppermute | solution.py:45
  54.9 16.7 %copy-start.9 = (bf16[2,2,64,128]{3,2,1,0:T(8,128)(2,1)}, bf16[2,2,64,128]{3,2,1,0:T(8,128)(2,1)S(1)}, u32[]{:S(2)}) copy-start(bf16[2,2,64,128]{3,2,1,0:T(8,128)(2,1)S(1)} %get-tuple-element.60) | copy-start | bytes 196612
  54.9 16.7 %copy-start.10 = (bf16[2,2,64,128]{3,2,1,0:T(8,128)(2,1)}, bf16[2,2,64,128]{3,2,1,0:T(8,128)(2,1)S(1)}, u32[]{:S(2)}) copy-start(bf16[2,2,64,128]{3,2,1,0:T(8,128)(2,1)S(1)} %get-tuple-element.59) | copy-start | bytes 196612
  54.9 34.2 %copy-start.6 = (s32[4,8]{1,0:T(4,128)S(1)}, s32[4,8]{1,0:T(4,128)}, u32[]{:S(2)}) copy-start(s32[4,8]{1,0:T(4,128)} %agg_ref.3) | copy-start | bytes 388
  54.9 10.2 %collective-permute-start.7 = (bf16[2,12,64,128]{3,2,1,0:T(8,128)(2,1)S(1)}, bf16[2,12,64,128]{3,2,1,0:T(8,128)(2,1)S(1)}, u32[]{:S(2)}, u32[]{:S(2)}) collective-permute-start(bf16[2,12,64,128]{3,2,1,0:T(8,128)(2,1)S(1)} %get-tuple-element.53), channel_id=1, source_target_pairs={{0,48},{48,0},{96,144},{144,96},{192,240},{240,192},{288,336},{336... | collective-permute-start | bytes 1179656 | tf_op jit(solution)/shard_map/ppermute | solution.py:17
  56.9 41.2 %collective-permute-start.8 = (bf16[2,8,64,128]{3,2,1,0:T(8,128)(2,1)}, bf16[2,8,64,128]{3,2,1,0:T(8,128)(2,1)}, u32[]{:S(2)}, u32[]{:S(2)}) collective-permute-start(bf16[2,8,64,128]{3,2,1,0:T(8,128)(2,1)} %get-tuple-element.54), channel_id=1, source_target_pairs={{48,96},{96,48},{144,192},{192,144},{240,288},{288,240},{336,384},... | collective-permute-start | bytes 786440 | tf_op jit(solution)/shard_map/ppermute | solution.py:25
  64.4 0.8 copy-start.1
  65.8 32.3 %collective-permute-start.9 = (bf16[4,2,64,128]{3,2,1,0:T(8,128)(2,1)S(1)}, bf16[4,2,64,128]{3,2,1,0:T(8,128)(2,1)S(1)}, u32[]{:S(2)}, u32[]{:S(2)}) collective-permute-start(bf16[4,2,64,128]{3,2,1,0:T(8,128)(2,1)S(1)} %get-tuple-element.57), channel_id=1, source_target_pairs={{0,1},{1,0},{2,3},{3,2},{4,5},{5,4},{6,7},{7,6},{8,9},{9,8},{10,11... | collective-permute-start | bytes 393224 | tf_op jit(solution)/shard_map/ppermute | solution.py:17
  69.6 28.4 %collective-permute-start.10 = (bf16[4,2,64,128]{3,2,1,0:T(8,128)(2,1)S(1)}, bf16[4,2,64,128]{3,2,1,0:T(8,128)(2,1)S(1)}, u32[]{:S(2)}, u32[]{:S(2)}) collective-permute-start(bf16[4,2,64,128]{3,2,1,0:T(8,128)(2,1)S(1)} %get-tuple-element.58), channel_id=1, source_target_pairs={{1,2},{2,1},{3,4},{4,3},{5,6},{6,5},{7,8},{8,7},{9,10},{10,9},{11,... | collective-permute-start | bytes 393224 | tf_op jit(solution)/shard_map/ppermute | solution.py:25
  73.0 16.1 %all-to-all-start.1 = ((bf16[8,64,128]{2,1,0:T(8,128)(2,1)}), bf16[8,64,128]{2,1,0:T(8,128)(2,1)S(1)}, u32[]{:S(2)}, u32[]{:S(2)}) async-start(bf16[8,64,128]{2,1,0:T(8,128)(2,1)} %coarse_solve.1), calls=%async_computation.1 | async-start | bytes 262144 | tf_op jit(solution)/shard_map/all_to_all | solution.py:51
  76.3 13.5 %collective-permute-start.11 = (bf16[2,2,64,128]{3,2,1,0:T(8,128)(2,1)}, bf16[2,2,64,128]{3,2,1,0:T(8,128)(2,1)S(1)}, u32[]{:S(2)}, u32[]{:S(2)}) collective-permute-start(bf16[2,2,64,128]{3,2,1,0:T(8,128)(2,1)} %copy-done.10), channel_id=1, source_target_pairs={{48,97},{49,96},{50,99},{51,98},{52,101},{53,100},{54,103},{55,102... | collective-permute-start | bytes 196616 | tf_op jit(solution)/shard_map/ppermute | solution.py:40
  87.1 10.9 %collective-permute-start.12 = (bf16[2,2,64,128]{3,2,1,0:T(8,128)(2,1)}, bf16[2,2,64,128]{3,2,1,0:T(8,128)(2,1)S(1)}, u32[]{:S(2)}, u32[]{:S(2)}) collective-permute-start(bf16[2,2,64,128]{3,2,1,0:T(8,128)(2,1)} %copy-done.9), channel_id=1, source_target_pairs={{49,98},{50,97},{51,100},{52,99},{53,102},{54,101},{55,104},{56,10... | collective-permute-start | bytes 196616 | tf_op jit(solution)/shard_map/ppermute | solution.py:40
  98.1 1.0 %copy-start.2 = (bf16[4,8,64,128]{3,2,1,0:T(8,128)(2,1)S(1)}, bf16[4,8,64,128]{3,2,1,0:T(8,128)(2,1)}, u32[]{:S(2)}) copy-start(bf16[4,8,64,128]{3,2,1,0:T(8,128)(2,1)} %copy-done.1) | copy-start | bytes 1572868

commit v5 on v2

--- a/solution.py
+++ b/solution.py
@@ -8,6 +8,7 @@
 BF16 = jnp.bfloat16
 F32 = jnp.float32
 MIB = 1 << 20
+HOLD = 1 << 34
 VMEM = pl.BlockSpec(memory_space=pltpu.VMEM)
 SMEM = pl.BlockSpec(memory_space=pltpu.SMEM)
 
@@ -34,14 +35,14 @@
     return jax.ShapeDtypeStruct(shape, dtype)
 
 
-def call(kernel, name, outs, ins, specs, out_specs, limit, flops=0, moved=0, scratch=()):
+def call(kernel, name, outs, ins, specs, out_specs, limit, flops=HOLD, scratch=()):
     return pl.pallas_call(
         kernel,
         out_shape=outs,
         in_specs=specs,
         out_specs=out_specs,
         scratch_shapes=list(scratch),
-        cost_estimate=pl.CostEstimate(flops=flops, bytes_accessed=moved, transcendentals=0),
+        cost_estimate=pl.CostEstimate(flops=flops, bytes_accessed=1024, transcendentals=0),
         compiler_params=pltpu.CompilerParams(vmem_limit_bytes=limit * MIB),
         name=name,
     )(*ins)
@@ -75,7 +76,7 @@
     tall = shaped((rows, 2, width, sides), BF16)
     return call(
         mask_kernel, "mask_blocks", (wide, wide, tall, tall), (info, residual),
-        [SMEM, VMEM], (VMEM,) * 4, 4, moved=4 * residual.size,
+        [SMEM, VMEM], (VMEM,) * 4, 4,
     )
 
 
@@ -118,7 +119,7 @@
         payload_kernel, "payload", shaped((1, count, sides), BF16),
         (info, agg, near.reshape(flat), far.reshape(flat), inverse),
         [SMEM, SMEM, VMEM, VMEM, VMEM], pl.BlockSpec((None, count, sides), lambda: (0, 0, 0)),
-        6, flops=1 << 25, moved=4 * near.size,
+        6,
     )
 
 
@@ -132,26 +133,29 @@
     count = first.shape[0]
     return call(
         join_pair_kernel, "join_pair", shaped((2 * count,) + first.shape[1:], BF16),
-        (first, second), [VMEM, VMEM], VMEM, 3, moved=8 * first.size,
-    )
-
-
-def corners_kernel(info_ref, cross_near, cross_far, near_ref, far_ref):
-    half = near_ref.shape[0]
+        (first, second), [VMEM, VMEM], VMEM, 3,
+    )
+
+
+def corners_kernel(info_ref, own_near, cross_near, cross_far, near_ref, far_ref):
+    half, columns = own_near.shape[:2]
     p, _ = parities(info_ref)
-    for out_ref, start in ((near_ref, half * (1 - p)), (far_ref, half * p)):
+    for i in range(half):
+        for j in range(columns):
+            near_ref[i, j] = own_near[i, j]
+    for out_ref, start, base in ((near_ref, half * (1 - p), columns), (far_ref, half * p, 0)):
         for i in range(half):
             for j in range(2):
-                out_ref[i, j] = cross_near[start + i, j]
-                out_ref[i, 2 + j] = cross_far[start + i, j]
-
-
-def corners(info, cross_near, cross_far):
-    rows, _, width, sides = cross_near.shape
-    piece = shaped((rows // 2, 4, width, sides), BF16)
-    return call(
-        corners_kernel, "corners", (piece, piece), (info, cross_near, cross_far),
-        [SMEM, VMEM, VMEM], (VMEM, VMEM), 2, moved=8 * cross_near.size,
+                out_ref[i, base + j] = cross_near[start + i, j]
+                out_ref[i, base + 2 + j] = cross_far[start + i, j]
+
+
+def corners(info, own_near, cross_near, cross_far):
+    half, columns, width, sides = own_near.shape
+    return call(
+        corners_kernel, "corners",
+        (shaped((half, columns + 4, width, sides), BF16), shaped((half, 4, width, sides), BF16)),
+        (info, own_near, cross_near, cross_far), [SMEM, VMEM, VMEM, VMEM], (VMEM, VMEM), 3,
     )
 
 
@@ -162,8 +166,8 @@
 
 def margin_kernel(
     info_ref, pattern_ref, blocks_ref,
-    own_near, own_far, got_near, got_far, cross_near, cross_far, corner_near, corner_far,
-    main_near, main_far, out_near, out_far, grid_ref,
+    own_near, own_far, got_near, got_far, cross_near, cross_far, corner_far,
+    out_near, main_far, out_far, grid_ref,
 ):
     half, columns = own_near.shape[:2]
     rows = 2 * half
@@ -182,17 +186,23 @@
         for i in range(rows):
             for j in range(2):
                 grid_ref[(2 + i) * wide + start + j] = source[i, j]
-    for source, start in ((corner_near, near_row), (corner_far, far_row)):
+    for source, start, first in ((got_near, near_row, columns), (corner_far, far_row, 0)):
         for i in range(2):
             for j in range(2):
-                grid_ref[(start + i) * wide + near_column + j] = source[i, j]
-                grid_ref[(start + i) * wide + far_column + j] = source[i, 2 + j]
-    for main, corner, start in ((main_near, out_near, near_row), (main_far, out_far, far_row)):
+                grid_ref[(start + i) * wide + near_column + j] = source[i, first + j]
+                grid_ref[(start + i) * wide + far_column + j] = source[i, first + 2 + j]
+    for main, corner, first, start in (
+        (main_far, out_far, 0, far_row), (out_near, out_near, columns, near_row)
+    ):
         for i in range(2):
             base = (start + i) * wide
             for j in range(2):
-                corner[i, j] = fix_of(pattern_ref, blocks_ref, grid_ref, base + near_column + j)
-                corner[i, 2 + j] = fix_of(pattern_ref, blocks_ref, grid_ref, base + far_column + j)
+                corner[i, first + j] = fix_of(
+                    pattern_ref, blocks_ref, grid_ref, base + near_column + j
+                )
+                corner[i, first + 2 + j] = fix_of(
+                    pattern_ref, blocks_ref, grid_ref, base + far_column + j
+                )
             for j in range(columns):
                 main[i, j] = fix_of(pattern_ref, blocks_ref, grid_ref, base + 2 + j)
 
@@ -200,13 +210,13 @@
 def margin_fixes(info, pattern, blocks, pieces):
     count, width, depth = blocks.shape
     half, columns, _, sides = pieces[0].shape
+    near = shaped((2, columns + 4, width, sides), BF16)
     main = shaped((2, columns, width, sides), BF16)
     corner = shaped((2, 4, width, sides), BF16)
     grid = shaped((count, width, sides), BF16)
     return call(
-        margin_kernel, "margin_fixes", (main, main, corner, corner, grid),
-        (info, pattern, blocks) + pieces, [SMEM, SMEM] + [VMEM] * 9, (VMEM,) * 5, 12,
-        flops=blocks.size * sides, moved=2 * blocks.size,
+        margin_kernel, "margin_fixes", (near, main, corner, grid),
+        (info, pattern, blocks) + pieces, [SMEM, SMEM] + [VMEM] * 8, (VMEM,) * 4, 12,
     )
 
 
@@ -230,28 +240,29 @@
     return call(
         center_kernel, "center_fixes",
         (side, side, shaped((rows, columns, width, sides), BF16)),
-        (info, pattern, blocks, grid), [SMEM, SMEM, VMEM, VMEM], (VMEM,) * 3, 12,
-        flops=blocks.size * sides, moved=2 * blocks.size,
-    )
-
-
-def fold_kernel(info_ref, side_near, side_far, corner_near, corner_far, out_near, out_far):
-    half = corner_near.shape[0]
+        (info, pattern, blocks, grid), [SMEM, SMEM, VMEM, VMEM], (VMEM,) * 3, 12, flops=0,
+    )
+
+
+def fold_kernel(info_ref, side_near, side_far, got_near, corner_far, out_near, out_far):
+    half, wide = got_near.shape[:2]
     p, _ = parities(info_ref)
-    for source, start in ((corner_near, half * (1 - p)), (corner_far, half * p)):
+    for source, start, first in (
+        (got_near, half * (1 - p), wide - 4), (corner_far, half * p, 0)
+    ):
         for i in range(half):
             for j in range(2):
                 for side, out, at in ((side_near, out_near, j), (side_far, out_far, 2 + j)):
-                    total = side[start + i, j].astype(F32) + source[i, at].astype(F32)
+                    total = side[start + i, j].astype(F32) + source[i, first + at].astype(F32)
                     out[start + i, j] = total.astype(BF16)
 
 
-def fold_sides(info, side_near, side_far, corner_near, corner_far):
+def fold_sides(info, side_near, side_far, got_near, corner_far):
     piece = shaped(side_near.shape, BF16)
     return call(
         fold_kernel, "fold_sides", (piece, piece),
-        (info, side_near, side_far, corner_near, corner_far),
-        [SMEM] + [VMEM] * 4, (VMEM, VMEM), 2, flops=2 * side_near.size, moved=12 * side_near.size,
+        (info, side_near, side_far, got_near, corner_far),
+        [SMEM] + [VMEM] * 4, (VMEM, VMEM), 3,
     )
 
 
@@ -321,7 +332,7 @@
 
     return call(
         kernel, "coarse_values", shaped((fields, sides), F32), (info, agg, first, second),
-        [SMEM, SMEM, VMEM, VMEM], VMEM, 8, flops=1 << 28, moved=4 * first.size,
+        [SMEM, SMEM, VMEM, VMEM], VMEM, 8,
         scratch=[pltpu.VMEM((total, sides), F32), pltpu.VMEM((total, sides), F32)],
     )
 
@@ -364,7 +375,7 @@
     return call(
         join_kernel, "join", shaped(center.shape, F32),
         (info, lifted, center, main_near, main_far, cross_near, cross_far),
-        [SMEM] + [VMEM] * 6, VMEM, 6, flops=8 * center.size, moved=10 * center.size,
+        [SMEM] + [VMEM] * 6, VMEM, 6,
     )
 
 
@@ -375,51 +386,42 @@
     bits = []
     while 2 << len(bits) <= lax.axis_size("stream"):
         bits.insert(0, 1 << len(bits))
-
     gathered = payload_of(info, block_aggregate, own_near, own_far, coarse_inverse)
     got_far = swap_far(own_far, "stream")
-    got_near = swap_near(own_near, "stream")
     cross_far = swap_far(edge_far, "cross")
     cross_near = swap_near(edge_near, "cross")
     blocks, links = approx_inverse[0], jnp.transpose(pattern[0])
-    got_far, got_near, cross_far, cross_near, blocks, gathered = lax.optimization_barrier(
-        (got_far, got_near, cross_far, cross_near, blocks, gathered)
-    )
-    blocks = jnp.where(info[0] > 0, blocks, jnp.zeros((), BF16))
-    corner_near, corner_far = corners(info, cross_near, cross_far)
+    got_far, cross_far, cross_near, gathered = lax.optimization_barrier(
+        (got_far, cross_far, cross_near, gathered)
+    )
     other = swap_bit(gathered, "stream", bits[0])
+    got_near, corner_far = corners(info, own_near, cross_near, cross_far)
     corner_far = swap_far(corner_far, "stream")
-    corner_near = swap_near(corner_near, "stream")
+    got_near = swap_near(got_near, "stream")
     gathered = join_pair(gathered, other)
     other = swap_bit(gathered, "stream", bits[1])
-    gathered, corner_far, corner_near = lax.optimization_barrier(
-        (gathered, corner_far, corner_near)
-    )
-    pieces = (own_near, own_far, got_near, got_far, cross_near, cross_far, corner_near, corner_far)
-    main_near, main_far, corner_near, corner_far, grid = margin_fixes(info, links, blocks, pieces)
+    gathered, corner_far, got_near = lax.optimization_barrier((gathered, corner_far, got_near))
+    pieces = (own_near, own_far, got_near, got_far, cross_near, cross_far, corner_far)
+    near, far, corner_far, grid = margin_fixes(info, links, blocks, pieces)
     corner_far, other = lax.optimization_barrier((corner_far, other))
-    gathered = join_pair(gathered, other)
     corner_far = swap_far(corner_far, "stream")
-    corner_near = swap_near(corner_near, "stream")
-    other = swap_bit(gathered, "stream", bits[2])
+    near = swap_near(near, "stream")
+    far = swap_far(far, "stream")
+    if bits[2:]:
+        gathered = join_pair(gathered, other)
+        other = swap_bit(gathered, "stream", bits[2])
+    near, grid = lax.optimization_barrier((near, grid))
     side_near, side_far, center = center_fixes(info, links, blocks, grid, rows, columns)
     side_near, other = lax.optimization_barrier((side_near, other))
     for bit in bits[3:]:
         gathered = join_pair(gathered, other)
         other = swap_bit(gathered, "stream", bit)
-    gathered, corner_near, corner_far = lax.optimization_barrier(
-        (gathered, corner_near, corner_far)
-    )
-    side_near, side_far = fold_sides(info, side_near, side_far, corner_near, corner_far)
-    side_near, side_far, main_far, main_near = lax.optimization_barrier(
-        (side_near, side_far, main_far, main_near)
-    )
-    main_far = swap_far(main_far, "stream")
-    main_near = swap_near(main_near, "stream")
+    gathered, near, corner_far = lax.optimization_barrier((gathered, near, corner_far))
+    side_near, side_far = fold_sides(info, side_near, side_far, near, corner_far)
     cross_far = swap_far(side_far, "cross")
     cross_near = swap_near(side_near, "cross")
     lifted = coarse_values(bits, info, block_aggregate, gathered, other)
-    return join(info, lifted, center, main_near, main_far, cross_near, cross_far)
+    return join(info, lifted, center, near, far, cross_near, cross_far)
 
 
 def solution(mesh):

time: 86.1 us -> 79.4 us (0.922)
  the two profiles are of different devices: /device:TPU:504 before, /device:TPU:519 now
where the time goes in v5:
time: 79.4 us; the launch traced here: 77.9 us
  starting transfers between devices  54.7 us (69%)
  waiting for transfers between devices  10.8 us (14%)
  Pallas kernels  10.4 us (13%)
  local copies, waits for them, and re-layouts  1.06 us (1%)
  between operations  0.93 us (1%)
    ppermute x6, starting transfers between devices, swap_far(): return lax.ppermute(values, axis, pairs)  32.7 us
    ppermute x4, starting transfers between devices, swap_near(): lax.ppermute(values, axis, [(i, i ^ 1) for i in range(count) if i ^ 1 < c...  12.7 us
    pallas_call x11, Pallas kernels, call(): pl.pallas_call(kernel, out_shape=outs, in_specs=specs, out_specs=out_spec...  10.4 us
    ppermute x4, starting transfers between devices, swap_bit(): return lax.ppermute(values, axis, [(i, i ^ bit) for i in range(count)])  9.27 us
    ppermute x6, waiting for transfers between devices, swap_far(): return lax.ppermute(values, axis, pairs)  7.37 us
    ppermute x4, waiting for transfers between devices, swap_near(): lax.ppermute(values, axis, [(i, i ^ 1) for i in range(count) if i ^ 1 < c...  2.84 us
  transfers between devices with their start and end apart: 14, of which 5 were waited for; matrix products, arithmetic and copies ran while one was open for 0% of the time, Pallas kernels for 10%

profile of v5, /device:TPU:519, one launch (start us, length us, event | category | flops | bytes accessed | tf_op | source)
XLA Modules:
  0.0 77.9 jit_solution(4683969683541982804)
XLA Ops:
  0.7 0.1 pad_add_fusion.info_ref.refs_0_
  0.7 0.0 copy-start.2
  0.7 1.0 %copy-done.2 = bf16[4,8,64,128]{3,2,1,0:T(8,128)(2,1)S(1)} copy-done((bf16[4,8,64,128]{3,2,1,0:T(8,128)(2,1)S(1)}, bf16[4,8,64,128]{3,2,1,0:T(8,128)(2,1)}, u32[]{:S(2)}) %copy-start.2) | copy-done | bytes 524312
  1.8 0.0 copy-start.3
  1.8 0.0 copy-start.4
  1.8 0.7 mask_blocks.1
  2.5 7.9 %collective-permute-start = (bf16[2,8,64,128]{3,2,1,0:T(8,128)(2,1)S(1)}, bf16[2,8,64,128]{3,2,1,0:T(8,128)(2,1)S(1)}, u32[]{:S(2)}, u32[]{:S(2)}) collective-permute-start(bf16[2,8,64,128]{3,2,1,0:T(8,128)(2,1)S(1)} %get-tuple-element.36.own_far), channel_id=1, source_target_pairs={{48,96},{96,48},{144,192},{192,144},{240,288},{288,240},{336,384},... | collective-permute-start | bytes 786440 | tf_op jit(solution)/shard_map/ppermute | solution.py:26
  10.5 3.7 %collective-permute-start.1 = (bf16[4,2,64,128]{3,2,1,0:T(8,128)(2,1)S(1)}, bf16[4,2,64,128]{3,2,1,0:T(8,128)(2,1)S(1)}, u32[]{:S(2)}, u32[]{:S(2)}) collective-permute-start(bf16[4,2,64,128]{3,2,1,0:T(8,128)(2,1)S(1)} %get-tuple-element.37), channel_id=1, source_target_pairs={{1,2},{2,1},{3,4},{4,3},{5,6},{6,5},{7,8},{8,7},{9,10},{10,9},{11,... | collective-permute-start | bytes 393224 | tf_op jit(solution)/shard_map/ppermute | solution.py:26
  14.2 1.9 %collective-permute-start.2 = (bf16[4,2,64,128]{3,2,1,0:T(8,128)(2,1)S(1)}, bf16[4,2,64,128]{3,2,1,0:T(8,128)(2,1)S(1)}, u32[]{:S(2)}, u32[]{:S(2)}) collective-permute-start(bf16[4,2,64,128]{3,2,1,0:T(8,128)(2,1)S(1)} %get-tuple-element.38), channel_id=1, source_target_pairs={{0,1},{1,0},{2,3},{3,2},{4,5},{5,4},{6,7},{7,6},{8,9},{9,8},{10,11... | collective-permute-start | bytes 393224 | tf_op jit(solution)/shard_map/ppermute | solution.py:18
  16.1 0.0 copy-done.3
  16.1 0.0 copy-done.4
  16.2 0.8 %payload.1.first_ref = bf16[1,160,128]{2,1,0:T(8,128)(2,1)S(1)} custom-call(s32[3]{0:T(128)S(1)} %pad_add_fusion.info_ref.refs_0_, s32[4,8]{1,0:T(4,128)S(1)} %copy-done.4, bf16[1024,128]{1,0:T(8,128)(2,1)S(1)} %bitcast.15, bf16[1024,128]{1,0:T(8,128)(2,1)S(1)} %bitcast.14, f32[32,32]{1,0:T(8,128)S(1)} %copy-done.3), custom_call_target="tpu_custom_call" | custom-call | flops 17179869184 | bytes 1024 | tf_op jit(solution)/shard_map/payload/pallas_call | solution.py:39
  17.0 3.2 %collective-permute-done.1.cross_far = bf16[4,2,64,128]{3,2,1,0:T(8,128)(2,1)S(1)} collective-permute-done((bf16[4,2,64,128]{3,2,1,0:T(8,128)(2,1)S(1)}, bf16[4,2,64,128]{3,2,1,0:T(8,128)(2,1)S(1)}, u32[]{:S(2)}, u32[]{:S(2)}) %collective-permute-start.1) | collective-permute-done | bytes 131104 | tf_op jit(solution)/shard_map/ppermute | solution.py:26
  20.2 2.8 %collective-permute-done.2.cross_near = bf16[4,2,64,128]{3,2,1,0:T(8,128)(2,1)S(1)} collective-permute-done((bf16[4,2,64,128]{3,2,1,0:T(8,128)(2,1)S(1)}, bf16[4,2,64,128]{3,2,1,0:T(8,128)(2,1)S(1)}, u32[]{:S(2)}, u32[]{:S(2)}) %collective-permute-start.2) | collective-permute-done | bytes 131104 | tf_op jit(solution)/shard_map/ppermute | solution.py:18
  23.0 0.0 collective-permute-done.got_far
  23.0 1.9 %collective-permute-start.3 = (bf16[1,160,128]{2,1,0:T(8,128)(2,1)S(1)}, bf16[1,160,128]{2,1,0:T(8,128)(2,1)S(1)}, u32[]{:S(2)}, u32[]{:S(2)}) collective-permute-start(bf16[1,160,128]{2,1,0:T(8,128)(2,1)S(1)} %payload.1.first_ref), channel_id=1, source_target_pairs={{0,384},{48,432},{96,480},{144,528},{192,576},{240,624},{288,672},... | collective-permute-start | bytes 122888 | tf_op jit(solution)/shard_map/ppermute | solution.py:31
  24.9 0.6 corners.1
  25.5 5.4 %collective-permute-start.4 = (bf16[2,4,64,128]{3,2,1,0:T(8,128)(2,1)S(1)}, bf16[2,4,64,128]{3,2,1,0:T(8,128)(2,1)S(1)}, u32[]{:S(2)}, u32[]{:S(2)}) collective-permute-start(bf16[2,4,64,128]{3,2,1,0:T(8,128)(2,1)S(1)} %get-tuple-element.43), channel_id=1, source_target_pairs={{48,96},{96,48},{144,192},{192,144},{240,288},{288,240},{336,384},... | collective-permute-start | bytes 393224 | tf_op jit(solution)/shard_map/ppermute | solution.py:26
  31.0 0.0 copy-start
  31.0 0.0 copy-start.1
  31.0 2.2 %collective-permute-start.5 = (bf16[2,12,64,128]{3,2,1,0:T(8,128)(2,1)S(1)}, bf16[2,12,64,128]{3,2,1,0:T(8,128)(2,1)S(1)}, u32[]{:S(2)}, u32[]{:S(2)}) collective-permute-start(bf16[2,12,64,128]{3,2,1,0:T(8,128)(2,1)S(1)} %get-tuple-element.44), channel_id=1, source_target_pairs={{0,48},{48,0},{96,144},{144,96},{192,240},{240,192},{288,336},{336... | collective-permute-start | bytes 1179656 | tf_op jit(solution)/shard_map/ppermute | solution.py:18
  33.2 0.0 collective-permute-done.3.second_ref
  33.2 3.5 %collective-permute-start.6 = (bf16[2,160,128]{2,1,0:T(8,128)(2,1)S(1)}, bf16[2,160,128]{2,1,0:T(8,128)(2,1)S(1)}, u32[]{:S(2)}, u32[]{:S(2)}) collective-permute-start(bf16[2,160,128]{2,1,0:T(8,128)(2,1)S(1)} %join_pair.3.first_ref), channel_id=1, source_target_pairs={{0,192},{48,240},{96,288},{144,336},{192,0},{240,48},{288,96},{336... | collective-permute-start | bytes 245768 | tf_op jit(solution)/shard_map/ppermute | solution.py:31
  36.7 1.2 %collective-permute-done.4.corner_far = bf16[2,4,64,128]{3,2,1,0:T(8,128)(2,1)S(1)} collective-permute-done((bf16[2,4,64,128]{3,2,1,0:T(8,128)(2,1)S(1)}, bf16[2,4,64,128]{3,2,1,0:T(8,128)(2,1)S(1)}, u32[]{:S(2)}, u32[]{:S(2)}) %collective-permute-start.4) | collective-permute-done | bytes 131104 | tf_op jit(solution)/shard_map/ppermute | solution.py:26
  37.9 0.0 collective-permute-done.5.got_near
  37.9 0.0 copy-done
  37.9 0.0 copy-done.1
  37.9 1.4 %margin_fixes.1 = (bf16[2,12,64,128]{3,2,1,0:T(8,128)(2,1)S(1)}, bf16[2,8,64,128]{3,2,1,0:T(8,128)(2,1)S(1)}, bf16[2,4,64,128]{3,2,1,0:T(8,128)(2,1)S(1)}, bf16[96,64,128]{2,1,0:T(8,128)(2,1)S(1)}) custom-call(s32[3]{0:T(128)S(1)} %pad_add_fusion.info_ref.refs_0_, s32[4,96]{1,0:T(4,128)S(1)} %bitcast.12, bf16[96,64,256]{2,1,0:T(8,128)(2,1)S(1)} %bitcast.10, ...), custom_call_target="tpu_custom_call" | custom-call | flops 17179869184 | bytes 1024 | tf_op jit(solution)/shard_map/margin_fixes/pallas_call | solution.py:39
  39.4 0.5 collective-permute-done.6.second_ref
  39.9 3.5 %collective-permute-start.7 = (bf16[2,12,64,128]{3,2,1,0:T(8,128)(2,1)S(1)}, bf16[2,12,64,128]{3,2,1,0:T(8,128)(2,1)S(1)}, u32[]{:S(2)}, u32[]{:S(2)}) collective-permute-start(bf16[2,12,64,128]{3,2,1,0:T(8,128)(2,1)S(1)} %get-tuple-element.51), channel_id=1, source_target_pairs={{0,48},{48,0},{96,144},{144,96},{192,240},{240,192},{288,336},{336... | collective-permute-start | bytes 1179656 | tf_op jit(solution)/shard_map/ppermute | solution.py:18
  43.5 1.9 %collective-permute-start.8 = (bf16[4,160,128]{2,1,0:T(8,128)(2,1)S(1)}, bf16[4,160,128]{2,1,0:T(8,128)(2,1)S(1)}, u32[]{:S(2)}, u32[]{:S(2)}) collective-permute-start(bf16[4,160,128]{2,1,0:T(8,128)(2,1)S(1)} %join_pair.4.first_ref), channel_id=1, source_target_pairs={{0,96},{48,144},{96,0},{144,48},{192,288},{240,336},{288,192},{336... | collective-permute-start | bytes 491528 | tf_op jit(solution)/shard_map/ppermute | solution.py:31
  45.4 6.1 %collective-permute-start.9 = (bf16[2,4,64,128]{3,2,1,0:T(8,128)(2,1)S(1)}, bf16[2,4,64,128]{3,2,1,0:T(8,128)(2,1)S(1)}, u32[]{:S(2)}, u32[]{:S(2)}) collective-permute-start(bf16[2,4,64,128]{3,2,1,0:T(8,128)(2,1)S(1)} %get-tuple-element.57), channel_id=1, source_target_pairs={{48,96},{96,48},{144,192},{192,144},{240,288},{288,240},{336,384},... | collective-permute-start | bytes 393224 | tf_op jit(solution)/shard_map/ppermute | solution.py:26
  51.5 5.5 %collective-permute-start.11 = (bf16[2,8,64,128]{3,2,1,0:T(8,128)(2,1)S(1)}, bf16[2,8,64,128]{3,2,1,0:T(8,128)(2,1)S(1)}, u32[]{:S(2)}, u32[]{:S(2)}) collective-permute-start(bf16[2,8,64,128]{3,2,1,0:T(8,128)(2,1)S(1)} %get-tuple-element.61), channel_id=1, source_target_pairs={{48,96},{96,48},{144,192},{192,144},{240,288},{288,240},{336,384},... | collective-permute-start | bytes 786440 | tf_op jit(solution)/shard_map/ppermute | solution.py:26
  57.0 0.0 collective-permute-done.7.got_near.main_near
  57.0 1.2 %center_fixes.1 = (bf16[4,2,64,128]{3,2,1,0:T(8,128)(2,1)S(1)}, bf16[4,2,64,128]{3,2,1,0:T(8,128)(2,1)S(1)}, bf16[4,8,64,128]{3,2,1,0:T(8,128)(2,1)S(1)}) custom-call(s32[3]{0:T(128)S(1)} %pad_add_fusion.info_ref.refs_0_, s32[4,96]{1,0:T(4,128)S(1)} %bitcast.13, bf16[96,64,256]{2,1,0:T(8,128)(2,1)S(1)} %bitcast.11, ...), custom_call_target="tpu_custom_call" | custom-call | bytes 1024 | tf_op jit(solution)/shard_map/center_fixes/pallas_call | solution.py:39
  58.2 0.0 collective-permute-done.8.second_ref
  58.3 1.9 %collective-permute-start.10 = (bf16[8,160,128]{2,1,0:T(8,128)(2,1)S(1)}, bf16[8,160,128]{2,1,0:T(8,128)(2,1)S(1)}, u32[]{:S(2)}, u32[]{:S(2)}) collective-permute-start(bf16[8,160,128]{2,1,0:T(8,128)(2,1)S(1)} %join_pair.5.refs_2_), channel_id=1, source_target_pairs={{0,48},{48,0},{96,144},{144,96},{192,240},{240,192},{288,336},{336... | collective-permute-start | bytes 983048 | tf_op jit(solution)/shard_map/ppermute | solution.py:31
  60.2 0.0 collective-permute-done.9.corner_far
  60.2 0.6 fold_sides.1
  60.8 5.0 %collective-permute-start.12 = (bf16[4,2,64,128]{3,2,1,0:T(8,128)(2,1)S(1)}, bf16[4,2,64,128]{3,2,1,0:T(8,128)(2,1)S(1)}, u32[]{:S(2)}, u32[]{:S(2)}) collective-permute-start(bf16[4,2,64,128]{3,2,1,0:T(8,128)(2,1)S(1)} %get-tuple-element.65), channel_id=1, source_target_pairs={{0,1},{1,0},{2,3},{3,2},{4,5},{5,4},{6,7},{7,6},{8,9},{9,8},{10,11... | collective-permute-start | bytes 393224 | tf_op jit(solution)/shard_map/ppermute | solution.py:18
  65.9 4.1 %collective-permute-start.13 = (bf16[4,2,64,128]{3,2,1,0:T(8,128)(2,1)S(1)}, bf16[4,2,64,128]{3,2,1,0:T(8,128)(2,1)S(1)}, u32[]{:S(2)}, u32[]{:S(2)}) collective-permute-start(bf16[4,2,64,128]{3,2,1,0:T(8,128)(2,1)S(1)} %get-tuple-element.66), channel_id=1, source_target_pairs={{1,2},{2,1},{3,4},{4,3},{5,6},{6,5},{7,8},{8,7},{9,10},{10,9},{11,... | collective-permute-start | bytes 393224 | tf_op jit(solution)/shard_map/ppermute | solution.py:26
  69.9 0.0 collective-permute-done.10.refs_3_
  70.0 3.0 %coarse_values.1.lifted_ref = f32[128,128]{1,0:T(8,128)S(1)} custom-call(s32[3]{0:T(128)S(1)} %pad_add_fusion.info_ref.refs_0_, s32[4,8]{1,0:T(4,128)S(1)} %copy-done.4, bf16[8,160,128]{2,1,0:T(8,128)(2,1)S(1)} %join_pair.5.refs_2_, bf16[8,160,128]{2,1,0:T(8,128)(2,1)S(1)} %collective-permute-done.10.refs_3_), custom_call_target="tpu_custom_call" | custom-call | flops 17179869184 | bytes 1024 | tf_op jit(solution)/shard_map/coarse_values/pallas_call | solution.py:39
  73.0 0.0 collective-permute-done.11.main_far
  73.0 0.0 collective-permute-done.12.cross_near
  73.0 2.9 %collective-permute-done.13.cross_far = bf16[4,2,64,128]{3,2,1,0:T(8,128)(2,1)S(1)} collective-permute-done((bf16[4,2,64,128]{3,2,1,0:T(8,128)(2,1)S(1)}, bf16[4,2,64,128]{3,2,1,0:T(8,128)(2,1)S(1)}, u32[]{:S(2)}, u32[]{:S(2)}) %collective-permute-start.13) | collective-permute-done | bytes 131104 | tf_op jit(solution)/shard_map/ppermute | solution.py:26
  75.9 2.0 %join.1 = f32[4,8,64,128]{3,2,1,0:T(8,128)} custom-call(s32[3]{0:T(128)S(1)} %pad_add_fusion.info_ref.refs_0_, f32[128,128]{1,0:T(8,128)S(1)} %coarse_values.1.lifted_ref, bf16[4,8,64,128]{3,2,1,0:T(8,128)(2,1)S(1)} %get-tuple-element.59.center_ref, bf16[2,12,64,128]{3,2,1,0:T(8,128)(2,1)S(1)} %collective-permute-done.7.got_near.main_near, ...), custom_call_target="tpu_custom_call" | custom-call | flops 17179869184 | bytes 1024 | tf_op jit(solution)/shard_map/join/pallas_call | solution.py:39
  (3 shorter events, 0.0 us)
Async XLA Ops:
  0.7 1.0 %copy-start.2 = (bf16[4,8,64,128]{3,2,1,0:T(8,128)(2,1)S(1)}, bf16[4,8,64,128]{3,2,1,0:T(8,128)(2,1)}, u32[]{:S(2)}) copy-start(bf16[4,8,64,128]{3,2,1,0:T(8,128)(2,1)} %residual_ref.1) | copy-start | bytes 1572868
  1.8 14.4 %copy-start.3 = (f32[32,32]{1,0:T(8,128)S(1)}, f32[32,32]{1,0:T(8,128)}, u32[]{:S(2)}) copy-start(f32[32,32]{1,0:T(8,128)} %inverse_ref.1) | copy-start | bytes 12292
  1.8 14.4 %copy-start.4 = (s32[4,8]{1,0:T(4,128)S(1)}, s32[4,8]{1,0:T(4,128)}, u32[]{:S(2)}) copy-start(s32[4,8]{1,0:T(4,128)} %refs_1_.1) | copy-start | bytes 388
  2.5 20.5 %collective-permute-start = (bf16[2,8,64,128]{3,2,1,0:T(8,128)(2,1)S(1)}, bf16[2,8,64,128]{3,2,1,0:T(8,128)(2,1)S(1)}, u32[]{:S(2)}, u32[]{:S(2)}) collective-permute-start(bf16[2,8,64,128]{3,2,1,0:T(8,128)(2,1)S(1)} %get-tuple-element.36.own_far), channel_id=1, source_target_pairs={{48,96},{96,48},{144,192},{192,144},{240,288},{288,240},{336,384},... | collective-permute-start | bytes 786440 | tf_op jit(solution)/shard_map/ppermute | solution.py:26
  10.5 9.7 %collective-permute-start.1 = (bf16[4,2,64,128]{3,2,1,0:T(8,128)(2,1)S(1)}, bf16[4,2,64,128]{3,2,1,0:T(8,128)(2,1)S(1)}, u32[]{:S(2)}, u32[]{:S(2)}) collective-permute-start(bf16[4,2,64,128]{3,2,1,0:T(8,128)(2,1)S(1)} %get-tuple-element.37), channel_id=1, source_target_pairs={{1,2},{2,1},{3,4},{4,3},{5,6},{6,5},{7,8},{8,7},{9,10},{10,9},{11,... | collective-permute-start | bytes 393224 | tf_op jit(solution)/shard_map/ppermute | solution.py:26
  14.2 8.8 %collective-permute-start.2 = (bf16[4,2,64,128]{3,2,1,0:T(8,128)(2,1)S(1)}, bf16[4,2,64,128]{3,2,1,0:T(8,128)(2,1)S(1)}, u32[]{:S(2)}, u32[]{:S(2)}) collective-permute-start(bf16[4,2,64,128]{3,2,1,0:T(8,128)(2,1)S(1)} %get-tuple-element.38), channel_id=1, source_target_pairs={{0,1},{1,0},{2,3},{3,2},{4,5},{5,4},{6,7},{7,6},{8,9},{9,8},{10,11... | collective-permute-start | bytes 393224 | tf_op jit(solution)/shard_map/ppermute | solution.py:18
  23.0 10.1 %collective-permute-start.3 = (bf16[1,160,128]{2,1,0:T(8,128)(2,1)S(1)}, bf16[1,160,128]{2,1,0:T(8,128)(2,1)S(1)}, u32[]{:S(2)}, u32[]{:S(2)}) collective-permute-start(bf16[1,160,128]{2,1,0:T(8,128)(2,1)S(1)} %payload.1.first_ref), channel_id=1, source_target_pairs={{0,384},{48,432},{96,480},{144,528},{192,576},{240,624},{288,672},... | collective-permute-start | bytes 122888 | tf_op jit(solution)/shard_map/ppermute | solution.py:31
  25.5 12.4 %collective-permute-start.4 = (bf16[2,4,64,128]{3,2,1,0:T(8,128)(2,1)S(1)}, bf16[2,4,64,128]{3,2,1,0:T(8,128)(2,1)S(1)}, u32[]{:S(2)}, u32[]{:S(2)}) collective-permute-start(bf16[2,4,64,128]{3,2,1,0:T(8,128)(2,1)S(1)} %get-tuple-element.43), channel_id=1, source_target_pairs={{48,96},{96,48},{144,192},{192,144},{240,288},{288,240},{336,384},... | collective-permute-start | bytes 393224 | tf_op jit(solution)/shard_map/ppermute | solution.py:26
  31.0 7.0 %copy-start = (bf16[1,96,64,256]{3,2,1,0:T(8,128)(2,1)S(1)}, bf16[1,96,64,256]{3,2,1,0:T(8,128)(2,1)}, u32[]{:S(2)}) copy-start(bf16[1,96,64,256]{3,2,1,0:T(8,128)(2,1)} %param.7) | copy-start | bytes 9437188
  31.0 7.0 %copy-start.1 = (s32[1,96,4]{1,2,0:T(4,128)S(1)}, s32[1,96,4]{1,2,0:T(4,128)}, u32[]{:S(2)}) copy-start(s32[1,96,4]{1,2,0:T(4,128)} %param.8) | copy-start | bytes 4612
  31.0 7.0 %collective-permute-start.5 = (bf16[2,12,64,128]{3,2,1,0:T(8,128)(2,1)S(1)}, bf16[2,12,64,128]{3,2,1,0:T(8,128)(2,1)S(1)}, u32[]{:S(2)}, u32[]{:S(2)}) collective-permute-start(bf16[2,12,64,128]{3,2,1,0:T(8,128)(2,1)S(1)} %get-tuple-element.44), channel_id=1, source_target_pairs={{0,48},{48,0},{96,144},{144,96},{192,240},{240,192},{288,336},{336... | collective-permute-start | bytes 1179656 | tf_op jit(solution)/shard_map/ppermute | solution.py:18
  33.2 6.7 %collective-permute-start.6 = (bf16[2,160,128]{2,1,0:T(8,128)(2,1)S(1)}, bf16[2,160,128]{2,1,0:T(8,128)(2,1)S(1)}, u32[]{:S(2)}, u32[]{:S(2)}) collective-permute-start(bf16[2,160,128]{2,1,0:T(8,128)(2,1)S(1)} %join_pair.3.first_ref), channel_id=1, source_target_pairs={{0,192},{48,240},{96,288},{144,336},{192,0},{240,48},{288,96},{336... | collective-permute-start | bytes 245768 | tf_op jit(solution)/shard_map/ppermute | solution.py:31
  39.9 17.1 %collective-permute-start.7 = (bf16[2,12,64,128]{3,2,1,0:T(8,128)(2,1)S(1)}, bf16[2,12,64,128]{3,2,1,0:T(8,128)(2,1)S(1)}, u32[]{:S(2)}, u32[]{:S(2)}) collective-permute-start(bf16[2,12,64,128]{3,2,1,0:T(8,128)(2,1)S(1)} %get-tuple-element.51), channel_id=1, source_target_pairs={{0,48},{48,0},{96,144},{144,96},{192,240},{240,192},{288,336},{336... | collective-permute-start | bytes 1179656 | tf_op jit(solution)/shard_map/ppermute | solution.py:18
  43.5 14.8 %collective-permute-start.8 = (bf16[4,160,128]{2,1,0:T(8,128)(2,1)S(1)}, bf16[4,160,128]{2,1,0:T(8,128)(2,1)S(1)}, u32[]{:S(2)}, u32[]{:S(2)}) collective-permute-start(bf16[4,160,128]{2,1,0:T(8,128)(2,1)S(1)} %join_pair.4.first_ref), channel_id=1, source_target_pairs={{0,96},{48,144},{96,0},{144,48},{192,288},{240,336},{288,192},{336... | collective-permute-start | bytes 491528 | tf_op jit(solution)/shard_map/ppermute | solution.py:31
  45.4 14.8 %collective-permute-start.9 = (bf16[2,4,64,128]{3,2,1,0:T(8,128)(2,1)S(1)}, bf16[2,4,64,128]{3,2,1,0:T(8,128)(2,1)S(1)}, u32[]{:S(2)}, u32[]{:S(2)}) collective-permute-start(bf16[2,4,64,128]{3,2,1,0:T(8,128)(2,1)S(1)} %get-tuple-element.57), channel_id=1, source_target_pairs={{48,96},{96,48},{144,192},{192,144},{240,288},{288,240},{336,384},... | collective-permute-start | bytes 393224 | tf_op jit(solution)/shard_map/ppermute | solution.py:26
  51.5 21.5 %collective-permute-start.11 = (bf16[2,8,64,128]{3,2,1,0:T(8,128)(2,1)S(1)}, bf16[2,8,64,128]{3,2,1,0:T(8,128)(2,1)S(1)}, u32[]{:S(2)}, u32[]{:S(2)}) collective-permute-start(bf16[2,8,64,128]{3,2,1,0:T(8,128)(2,1)S(1)} %get-tuple-element.61), channel_id=1, source_target_pairs={{48,96},{96,48},{144,192},{192,144},{240,288},{288,240},{336,384},... | collective-permute-start | bytes 786440 | tf_op jit(solution)/shard_map/ppermute | solution.py:26
  58.3 11.7 %collective-permute-start.10 = (bf16[8,160,128]{2,1,0:T(8,128)(2,1)S(1)}, bf16[8,160,128]{2,1,0:T(8,128)(2,1)S(1)}, u32[]{:S(2)}, u32[]{:S(2)}) collective-permute-start(bf16[8,160,128]{2,1,0:T(8,128)(2,1)S(1)} %join_pair.5.refs_2_), channel_id=1, source_target_pairs={{0,48},{48,0},{96,144},{144,96},{192,240},{240,192},{288,336},{336... | collective-permute-start | bytes 983048 | tf_op jit(solution)/shard_map/ppermute | solution.py:31
  60.8 12.2 %collective-permute-start.12 = (bf16[4,2,64,128]{3,2,1,0:T(8,128)(2,1)S(1)}, bf16[4,2,64,128]{3,2,1,0:T(8,128)(2,1)S(1)}, u32[]{:S(2)}, u32[]{:S(2)}) collective-permute-start(bf16[4,2,64,128]{3,2,1,0:T(8,128)(2,1)S(1)} %get-tuple-element.65), channel_id=1, source_target_pairs={{0,1},{1,0},{2,3},{3,2},{4,5},{5,4},{6,7},{7,6},{8,9},{9,8},{10,11... | collective-permute-start | bytes 393224 | tf_op jit(solution)/shard_map/ppermute | solution.py:18
  65.9 10.0 %collective-permute-start.13 = (bf16[4,2,64,128]{3,2,1,0:T(8,128)(2,1)S(1)}, bf16[4,2,64,128]{3,2,1,0:T(8,128)(2,1)S(1)}, u32[]{:S(2)}, u32[]{:S(2)}) collective-permute-start(bf16[4,2,64,128]{3,2,1,0:T(8,128)(2,1)S(1)} %get-tuple-element.66), channel_id=1, source_target_pairs={{1,2},{2,1},{3,4},{4,3},{5,6},{6,5},{7,8},{8,7},{9,10},{10,9},{11,... | collective-permute-start | bytes 393224 | tf_op jit(solution)/shard_map/ppermute | solution.py:26

commit v6 on v5

--- a/solution.py
+++ b/solution.py
@@ -137,25 +137,40 @@
     )
 
 
-def corners_kernel(info_ref, own_near, cross_near, cross_far, near_ref, far_ref):
+def far_corner_kernel(info_ref, cross_near, cross_far, far_ref):
+    half = far_ref.shape[0]
+    p, _ = parities(info_ref)
+    for i in range(half):
+        for j in range(2):
+            far_ref[i, j] = cross_near[half * p + i, j]
+            far_ref[i, 2 + j] = cross_far[half * p + i, j]
+
+
+def far_corners(info, cross_near, cross_far):
+    rows, _, width, sides = cross_near.shape
+    return call(
+        far_corner_kernel, "far_corners", shaped((rows // 2, 4, width, sides), BF16),
+        (info, cross_near, cross_far), [SMEM, VMEM, VMEM], VMEM, 2,
+    )
+
+
+def near_kernel(info_ref, own_near, cross_near, cross_far, near_ref):
     half, columns = own_near.shape[:2]
     p, _ = parities(info_ref)
+    start = half * (1 - p)
     for i in range(half):
         for j in range(columns):
             near_ref[i, j] = own_near[i, j]
-    for out_ref, start, base in ((near_ref, half * (1 - p), columns), (far_ref, half * p, 0)):
-        for i in range(half):
-            for j in range(2):
-                out_ref[i, base + j] = cross_near[start + i, j]
-                out_ref[i, base + 2 + j] = cross_far[start + i, j]
-
-
-def corners(info, own_near, cross_near, cross_far):
+        for j in range(2):
+            near_ref[i, columns + j] = cross_near[start + i, j]
+            near_ref[i, columns + 2 + j] = cross_far[start + i, j]
+
+
+def near_message(info, own_near, cross_near, cross_far):
     half, columns, width, sides = own_near.shape
     return call(
-        corners_kernel, "corners",
-        (shaped((half, columns + 4, width, sides), BF16), shaped((half, 4, width, sides), BF16)),
-        (info, own_near, cross_near, cross_far), [SMEM, VMEM, VMEM, VMEM], (VMEM, VMEM), 3,
+        near_kernel, "near_message", shaped((half, columns + 4, width, sides), BF16),
+        (info, own_near, cross_near, cross_far), [SMEM, VMEM, VMEM, VMEM], VMEM, 3,
     )
 
 
@@ -164,10 +179,10 @@
     return jnp.dot(blocks_ref[n], picked, preferred_element_type=F32).astype(BF16)
 
 
-def margin_kernel(
+def far_margin_kernel(
     info_ref, pattern_ref, blocks_ref,
     own_near, own_far, got_near, got_far, cross_near, cross_far, corner_far,
-    out_near, main_far, out_far, grid_ref,
+    main_far, out_far, grid_ref,
 ):
     half, columns = own_near.shape[:2]
     rows = 2 * half
@@ -191,32 +206,52 @@
             for j in range(2):
                 grid_ref[(start + i) * wide + near_column + j] = source[i, first + j]
                 grid_ref[(start + i) * wide + far_column + j] = source[i, first + 2 + j]
-    for main, corner, first, start in (
-        (main_far, out_far, 0, far_row), (out_near, out_near, columns, near_row)
-    ):
-        for i in range(2):
-            base = (start + i) * wide
-            for j in range(2):
-                corner[i, first + j] = fix_of(
-                    pattern_ref, blocks_ref, grid_ref, base + near_column + j
-                )
-                corner[i, first + 2 + j] = fix_of(
-                    pattern_ref, blocks_ref, grid_ref, base + far_column + j
-                )
-            for j in range(columns):
-                main[i, j] = fix_of(pattern_ref, blocks_ref, grid_ref, base + 2 + j)
-
-
-def margin_fixes(info, pattern, blocks, pieces):
+    for i in range(2):
+        base = (far_row + i) * wide
+        for j in range(2):
+            out_far[i, j] = fix_of(pattern_ref, blocks_ref, grid_ref, base + near_column + j)
+            out_far[i, 2 + j] = fix_of(pattern_ref, blocks_ref, grid_ref, base + far_column + j)
+        for j in range(columns):
+            main_far[i, j] = fix_of(pattern_ref, blocks_ref, grid_ref, base + 2 + j)
+
+
+def far_margin(info, pattern, blocks, pieces):
     count, width, depth = blocks.shape
     half, columns, _, sides = pieces[0].shape
-    near = shaped((2, columns + 4, width, sides), BF16)
     main = shaped((2, columns, width, sides), BF16)
     corner = shaped((2, 4, width, sides), BF16)
     grid = shaped((count, width, sides), BF16)
     return call(
-        margin_kernel, "margin_fixes", (near, main, corner, grid),
-        (info, pattern, blocks) + pieces, [SMEM, SMEM] + [VMEM] * 8, (VMEM,) * 4, 12,
+        far_margin_kernel, "far_margin", (main, corner, grid),
+        (info, pattern, blocks) + pieces, [SMEM, SMEM] + [VMEM] * 8, (VMEM,) * 3, 12,
+    )
+
+
+def near_margin_kernel(info_ref, pattern_ref, blocks_ref, grid_ref, out_near):
+    wide = out_near.shape[1]
+    columns = wide - 4
+    rows = grid_ref.shape[0] // wide - 4
+    p, q = parities(info_ref)
+    near_row = (rows + 2) * (1 - p)
+    near_column, far_column = (columns + 2) * (1 - q), (columns + 2) * q
+    for i in range(2):
+        base = (near_row + i) * wide
+        for j in range(2):
+            out_near[i, columns + j] = fix_of(
+                pattern_ref, blocks_ref, grid_ref, base + near_column + j
+            )
+            out_near[i, columns + 2 + j] = fix_of(
+                pattern_ref, blocks_ref, grid_ref, base + far_column + j
+            )
+        for j in range(columns):
+            out_near[i, j] = fix_of(pattern_ref, blocks_ref, grid_ref, base + 2 + j)
+
+
+def near_margin(info, pattern, blocks, grid, columns):
+    _, width, sides = grid.shape
+    return call(
+        near_margin_kernel, "near_margin", shaped((2, columns + 4, width, sides), BF16),
+        (info, pattern, blocks, grid), [SMEM, SMEM, VMEM, VMEM], VMEM, 12,
     )
 
 
@@ -244,25 +279,24 @@
     )
 
 
-def fold_kernel(info_ref, side_near, side_far, got_near, corner_far, out_near, out_far):
+def fold_kernel(first, info_ref, side_ref, corner_far, got_near, out_ref):
     half, wide = got_near.shape[:2]
     p, _ = parities(info_ref)
-    for source, start, first in (
-        (got_near, half * (1 - p), wide - 4), (corner_far, half * p, 0)
-    ):
+    for source, start, base in ((got_near, half * (1 - p), wide - 4), (corner_far, half * p, 0)):
         for i in range(half):
             for j in range(2):
-                for side, out, at in ((side_near, out_near, j), (side_far, out_far, 2 + j)):
-                    total = side[start + i, j].astype(F32) + source[i, first + at].astype(F32)
-                    out[start + i, j] = total.astype(BF16)
-
-
-def fold_sides(info, side_near, side_far, got_near, corner_far):
-    piece = shaped(side_near.shape, BF16)
-    return call(
-        fold_kernel, "fold_sides", (piece, piece),
-        (info, side_near, side_far, got_near, corner_far),
-        [SMEM] + [VMEM] * 4, (VMEM, VMEM), 3,
+                total = side_ref[start + i, j].astype(F32)
+                total = total + source[i, base + first + j].astype(F32)
+                out_ref[start + i, j] = total.astype(BF16)
+
+
+def fold_side(first, info, side, corner_far, got_near):
+    def kernel(*refs):
+        fold_kernel(first, *refs)
+
+    return call(
+        kernel, "fold_side", shaped(side.shape, BF16), (info, side, corner_far, got_near),
+        [SMEM] + [VMEM] * 3, VMEM, 3,
     )
 
 
@@ -274,12 +308,11 @@
     )
 
 
-def solve_kernel(bits, info_ref, agg_ref, first_ref, second_ref, out_ref, sums, coarse):
+def solve_kernel(bits, info_ref, first_ref, second_ref, coarse, sums):
     count, height, sides = first_ref.shape
-    rows, columns = agg_ref.shape
-    fields = rows * columns * 4
-    size = height - fields
     total = sums.shape[0]
+    size = total // (2 * count)
+    fields = height - size
     row = lax.broadcasted_iota(jnp.int32, (sides, fields), 0)
     column = lax.broadcasted_iota(jnp.int32, (sides, fields), 1)
     repeat = jnp.where(row - 3 * size == column // 4, 1.0, 0.0).astype(BF16)
@@ -311,6 +344,12 @@
             coarse[pl.ds(start, size), :] = split_dot(
                 source[k, pl.ds(fields, size), :], stacked
             )
+
+
+def lift_kernel(agg_ref, coarse_ref, out_ref):
+    total = coarse_ref.shape[0]
+    rows, columns = agg_ref.shape
+    fields = rows * columns * 4
     row = lax.broadcasted_iota(jnp.int32, (fields, 1), 0)
     labels = jnp.zeros((fields, 1), jnp.int32)
     for i in range(rows):
@@ -319,26 +358,31 @@
     row = lax.broadcasted_iota(jnp.int32, (fields, total), 0)
     column = lax.broadcasted_iota(jnp.int32, (fields, total), 1)
     onehot = jnp.where((column // 4 == labels) & (column % 4 == row % 4), 1.0, 0.0)
-    out_ref[...] = split_dot(onehot.astype(BF16), coarse[...])
-
-
-def coarse_values(bits, info, agg, first, second):
+    out_ref[...] = split_dot(onehot.astype(BF16), coarse_ref[...])
+
+
+def coarse_values(bits, info, size, first, second):
     count, height, sides = first.shape
-    fields = agg.size * 4
-    total = 2 * count * (height - fields)
+    total = 2 * count * size
 
     def kernel(*refs):
         solve_kernel(bits, *refs)
 
     return call(
-        kernel, "coarse_values", shaped((fields, sides), F32), (info, agg, first, second),
-        [SMEM, SMEM, VMEM, VMEM], VMEM, 8,
-        scratch=[pltpu.VMEM((total, sides), F32), pltpu.VMEM((total, sides), F32)],
+        kernel, "coarse_values", shaped((total, sides), F32), (info, first, second),
+        [SMEM, VMEM, VMEM], VMEM, 8, scratch=[pltpu.VMEM((total, sides), F32)],
+    )
+
+
+def lift(agg, coarse):
+    return call(
+        lift_kernel, "lift", shaped((agg.size * 4, coarse.shape[1]), F32), (agg, coarse),
+        [SMEM, VMEM], VMEM, 3,
     )
 
 
 def join_kernel(
-    info_ref, lifted_ref, center_ref, main_near, main_far, cross_near, cross_far, out_ref
+    info_ref, lifted_ref, center_ref, main_near, main_far, cross_far, cross_near, out_ref
 ):
     rows, columns, width, sides = center_ref.shape
     half = rows // 2
@@ -371,10 +415,10 @@
                 out_ref[i, j] = jnp.zeros((width, sides), F32)
 
 
-def join(info, lifted, center, main_near, main_far, cross_near, cross_far):
+def join(info, lifted, center, main_near, main_far, cross_far, cross_near):
     return call(
         join_kernel, "join", shaped(center.shape, F32),
-        (info, lifted, center, main_near, main_far, cross_near, cross_far),
+        (info, lifted, center, main_near, main_far, cross_far, cross_near),
         [SMEM] + [VMEM] * 6, VMEM, 6,
     )
 
@@ -395,33 +439,36 @@
         (got_far, cross_far, cross_near, gathered)
     )
     other = swap_bit(gathered, "stream", bits[0])
-    got_near, corner_far = corners(info, own_near, cross_near, cross_far)
+    corner_far = far_corners(info, cross_near, cross_far)
+    corner_far, own_near = lax.optimization_barrier((corner_far, own_near))
+    got_near = near_message(info, own_near, cross_near, cross_far)
     corner_far = swap_far(corner_far, "stream")
     got_near = swap_near(got_near, "stream")
     gathered = join_pair(gathered, other)
     other = swap_bit(gathered, "stream", bits[1])
     gathered, corner_far, got_near = lax.optimization_barrier((gathered, corner_far, got_near))
     pieces = (own_near, own_far, got_near, got_far, cross_near, cross_far, corner_far)
-    near, far, corner_far, grid = margin_fixes(info, links, blocks, pieces)
-    corner_far, other = lax.optimization_barrier((corner_far, other))
+    far, corner_far, grid = far_margin(info, links, blocks, pieces)
+    near = near_margin(info, links, blocks, grid, columns)
     corner_far = swap_far(corner_far, "stream")
     near = swap_near(near, "stream")
     far = swap_far(far, "stream")
+    side_near, side_far, center = center_fixes(info, links, blocks, grid, rows, columns)
     if bits[2:]:
         gathered = join_pair(gathered, other)
         other = swap_bit(gathered, "stream", bits[2])
-    near, grid = lax.optimization_barrier((near, grid))
-    side_near, side_far, center = center_fixes(info, links, blocks, grid, rows, columns)
-    side_near, other = lax.optimization_barrier((side_near, other))
+    corner_far, other = lax.optimization_barrier((corner_far, other))
     for bit in bits[3:]:
         gathered = join_pair(gathered, other)
         other = swap_bit(gathered, "stream", bit)
-    gathered, near, corner_far = lax.optimization_barrier((gathered, near, corner_far))
-    side_near, side_far = fold_sides(info, side_near, side_far, near, corner_far)
+    side_near = fold_side(0, info, side_near, corner_far, near)
+    side_far, side_near = lax.optimization_barrier((side_far, side_near))
+    side_far = fold_side(2, info, side_far, corner_far, near)
     cross_far = swap_far(side_far, "cross")
     cross_near = swap_near(side_near, "cross")
-    lifted = coarse_values(bits, info, block_aggregate, gathered, other)
-    return join(info, lifted, center, near, far, cross_near, cross_far)
+    coarse = coarse_values(bits, info, coarse_inverse.shape[0], gathered, other)
+    lifted = lift(block_aggregate, coarse)
+    return join(info, lifted, center, near, far, cross_far, cross_near)
 
 
 def solution(mesh):

time: 79.4 us -> 80.9 us (1.019); the launches traced: 77.9 us -> 80.4 us
  starting transfers between devices: 54.7 us -> 50.9 us
  waiting for transfers between devices: 10.8 us -> 14.6 us
  Pallas kernels: 10.4 us -> 12.8 us
    ppermute x4, starting transfers between devices: 12.7 us -> 9.14 us  [swap_near(): lax.ppermute(values, axis, [(i, i ^ 1) for i in range(count) if i ^ 1 < c...]
    ppermute x4, waiting for transfers between devices: 2.84 us -> 6.36 us  [swap_near(): lax.ppermute(values, axis, [(i, i ^ 1) for i in range(count) if i ^ 1 < c...]
    pallas_call x11 -> x15, Pallas kernels: 10.4 us -> 12.8 us  [call(): pl.pallas_call(kernel, out_shape=outs, in_specs=specs, out_specs=out_spec...]
    ppermute x6, waiting for transfers between devices: 7.37 us -> 8.24 us  [swap_far(): return lax.ppermute(values, axis, pairs)]
  transfers between devices with their start and end apart: 14 -> 14, of which waited for: 5 -> 4; matrix products, arithmetic and copies ran while one was open for 0% -> 0% of each run, Pallas kernels for 10% -> 12%
where the time goes in v6:
time: 80.9 us; the launch traced here: 80.4 us
  starting transfers between devices  50.9 us (63%)
  waiting for transfers between devices  14.6 us (18%)
  Pallas kernels  12.8 us (16%)
  local copies, waits for them, and re-layouts  1.07 us (1%)
  between operations  0.97 us (1%)
    ppermute x6, starting transfers between devices, swap_far(): return lax.ppermute(values, axis, pairs)  32.4 us
    pallas_call x15, Pallas kernels, call(): pl.pallas_call(kernel, out_shape=outs, in_specs=specs, out_specs=out_spec...  12.8 us
    ppermute x4, starting transfers between devices, swap_bit(): return lax.ppermute(values, axis, [(i, i ^ bit) for i in range(count)])  9.28 us
    ppermute x4, starting transfers between devices, swap_near(): lax.ppermute(values, axis, [(i, i ^ 1) for i in range(count) if i ^ 1 < c...  9.14 us
    ppermute x6, waiting for transfers between devices, swap_far(): return lax.ppermute(values, axis, pairs)  8.24 us
    ppermute x4, waiting for transfers between devices, swap_near(): lax.ppermute(values, axis, [(i, i ^ 1) for i in range(count) if i ^ 1 < c...  6.36 us
  transfers between devices with their start and end apart: 14, of which 4 were waited for; matrix products, arithmetic and copies ran while one was open for 0% of the time, Pallas kernels for 12%

profile of v6, /device:TPU:519, one launch (start us, length us, event | category | flops | bytes accessed | tf_op | source)
XLA Modules:
  0.0 80.4 jit_solution(10060811202236538049)
XLA Ops:
  0.7 0.1 pad_add_fusion.info_ref.refs_0_
  0.7 0.0 copy-start.2
  0.7 1.0 %copy-done.2 = bf16[4,8,64,128]{3,2,1,0:T(8,128)(2,1)S(1)} copy-done((bf16[4,8,64,128]{3,2,1,0:T(8,128)(2,1)S(1)}, bf16[4,8,64,128]{3,2,1,0:T(8,128)(2,1)}, u32[]{:S(2)}) %copy-start.2) | copy-done | bytes 524312
  1.8 0.0 copy-start.3
  1.8 0.0 copy-start.4
  1.8 0.7 mask_blocks.1
  2.5 7.9 %collective-permute-start = (bf16[2,8,64,128]{3,2,1,0:T(8,128)(2,1)S(1)}, bf16[2,8,64,128]{3,2,1,0:T(8,128)(2,1)S(1)}, u32[]{:S(2)}, u32[]{:S(2)}) collective-permute-start(bf16[2,8,64,128]{3,2,1,0:T(8,128)(2,1)S(1)} %get-tuple-element.28.own_far), channel_id=1, source_target_pairs={{48,96},{96,48},{144,192},{192,144},{240,288},{288,240},{336,384},... | collective-permute-start | bytes 786440 | tf_op jit(solution)/shard_map/ppermute | solution.py:26
  10.5 3.7 %collective-permute-start.1 = (bf16[4,2,64,128]{3,2,1,0:T(8,128)(2,1)S(1)}, bf16[4,2,64,128]{3,2,1,0:T(8,128)(2,1)S(1)}, u32[]{:S(2)}, u32[]{:S(2)}) collective-permute-start(bf16[4,2,64,128]{3,2,1,0:T(8,128)(2,1)S(1)} %get-tuple-element.29), channel_id=1, source_target_pairs={{1,2},{2,1},{3,4},{4,3},{5,6},{6,5},{7,8},{8,7},{9,10},{10,9},{11,... | collective-permute-start | bytes 393224 | tf_op jit(solution)/shard_map/ppermute | solution.py:26
  14.2 1.9 %collective-permute-start.2 = (bf16[4,2,64,128]{3,2,1,0:T(8,128)(2,1)S(1)}, bf16[4,2,64,128]{3,2,1,0:T(8,128)(2,1)S(1)}, u32[]{:S(2)}, u32[]{:S(2)}) collective-permute-start(bf16[4,2,64,128]{3,2,1,0:T(8,128)(2,1)S(1)} %get-tuple-element.30), channel_id=1, source_target_pairs={{0,1},{1,0},{2,3},{3,2},{4,5},{5,4},{6,7},{7,6},{8,9},{9,8},{10,11... | collective-permute-start | bytes 393224 | tf_op jit(solution)/shard_map/ppermute | solution.py:18
  16.1 0.0 copy-done.3
  16.1 0.0 copy-done.4
  16.2 0.8 payload.1.first_ref
  17.0 3.2 %collective-permute-done.1.cross_far = bf16[4,2,64,128]{3,2,1,0:T(8,128)(2,1)S(1)} collective-permute-done((bf16[4,2,64,128]{3,2,1,0:T(8,128)(2,1)S(1)}, bf16[4,2,64,128]{3,2,1,0:T(8,128)(2,1)S(1)}, u32[]{:S(2)}, u32[]{:S(2)}) %collective-permute-start.1) | collective-permute-done | bytes 131104 | tf_op jit(solution)/shard_map/ppermute | solution.py:26
  20.2 2.8 %collective-permute-done.2.cross_near = bf16[4,2,64,128]{3,2,1,0:T(8,128)(2,1)S(1)} collective-permute-done((bf16[4,2,64,128]{3,2,1,0:T(8,128)(2,1)S(1)}, bf16[4,2,64,128]{3,2,1,0:T(8,128)(2,1)S(1)}, u32[]{:S(2)}, u32[]{:S(2)}) %collective-permute-start.2) | collective-permute-done | bytes 131104 | tf_op jit(solution)/shard_map/ppermute | solution.py:18
  23.0 0.0 collective-permute-done.got_far
  23.0 0.6 far_corners.1
  23.6 1.9 %collective-permute-start.3 = (bf16[1,160,128]{2,1,0:T(8,128)(2,1)S(1)}, bf16[1,160,128]{2,1,0:T(8,128)(2,1)S(1)}, u32[]{:S(2)}, u32[]{:S(2)}) collective-permute-start(bf16[1,160,128]{2,1,0:T(8,128)(2,1)S(1)} %payload.1.first_ref), channel_id=1, source_target_pairs={{0,384},{48,432},{96,480},{144,528},{192,576},{240,624},{288,672},... | collective-permute-start | bytes 122888 | tf_op jit(solution)/shard_map/ppermute | solution.py:31
  25.5 0.6 near_message.1
  26.1 0.0 copy-start
  26.1 0.0 copy-start.1
  26.1 2.6 %collective-permute-start.5 = (bf16[2,12,64,128]{3,2,1,0:T(8,128)(2,1)S(1)}, bf16[2,12,64,128]{3,2,1,0:T(8,128)(2,1)S(1)}, u32[]{:S(2)}, u32[]{:S(2)}) collective-permute-start(bf16[2,12,64,128]{3,2,1,0:T(8,128)(2,1)S(1)} %near_message.1), channel_id=1, source_target_pairs={{0,48},{48,0},{96,144},{144,96},{192,240},{240,192},{288,336},{336... | collective-permute-start | bytes 1179656 | tf_op jit(solution)/shard_map/ppermute | solution.py:18
  28.8 5.0 %collective-permute-start.4 = (bf16[2,4,64,128]{3,2,1,0:T(8,128)(2,1)S(1)}, bf16[2,4,64,128]{3,2,1,0:T(8,128)(2,1)S(1)}, u32[]{:S(2)}, u32[]{:S(2)}) collective-permute-start(bf16[2,4,64,128]{3,2,1,0:T(8,128)(2,1)S(1)} %far_corners.1), channel_id=1, source_target_pairs={{48,96},{96,48},{144,192},{192,144},{240,288},{288,240},{336,384},... | collective-permute-start | bytes 393224 | tf_op jit(solution)/shard_map/ppermute | solution.py:26
  33.7 0.0 collective-permute-done.3.second_ref
  33.8 3.5 %collective-permute-start.6 = (bf16[2,160,128]{2,1,0:T(8,128)(2,1)S(1)}, bf16[2,160,128]{2,1,0:T(8,128)(2,1)S(1)}, u32[]{:S(2)}, u32[]{:S(2)}) collective-permute-start(bf16[2,160,128]{2,1,0:T(8,128)(2,1)S(1)} %join_pair.3.first_ref), channel_id=1, source_target_pairs={{0,192},{48,240},{96,288},{144,336},{192,0},{240,48},{288,96},{336... | collective-permute-start | bytes 245768 | tf_op jit(solution)/shard_map/ppermute | solution.py:31
  37.3 5.0 %collective-permute-done.4.corner_far = bf16[2,4,64,128]{3,2,1,0:T(8,128)(2,1)S(1)} collective-permute-done((bf16[2,4,64,128]{3,2,1,0:T(8,128)(2,1)S(1)}, bf16[2,4,64,128]{3,2,1,0:T(8,128)(2,1)S(1)}, u32[]{:S(2)}, u32[]{:S(2)}) %collective-permute-start.4) | collective-permute-done | bytes 131104 | tf_op jit(solution)/shard_map/ppermute | solution.py:26
  42.3 0.0 collective-permute-done.5.got_near
  42.3 0.0 copy-done
  42.3 0.0 copy-done.1
  42.3 1.1 %far_margin.1 = (bf16[2,8,64,128]{3,2,1,0:T(8,128)(2,1)S(1)}, bf16[2,4,64,128]{3,2,1,0:T(8,128)(2,1)S(1)}, bf16[96,64,128]{2,1,0:T(8,128)(2,1)S(1)}) custom-call(s32[3]{0:T(128)S(1)} %pad_add_fusion.info_ref.refs_0_, s32[4,96]{1,0:T(4,128)S(1)} %bitcast.13, bf16[96,64,256]{2,1,0:T(8,128)(2,1)S(1)} %bitcast.10, ...), custom_call_target="tpu_custom_call" | custom-call | flops 17179869184 | bytes 1024 | tf_op jit(solution)/shard_map/far_margin/pallas_call | solution.py:39
  43.4 4.6 %collective-permute-start.7 = (bf16[2,4,64,128]{3,2,1,0:T(8,128)(2,1)S(1)}, bf16[2,4,64,128]{3,2,1,0:T(8,128)(2,1)S(1)}, u32[]{:S(2)}, u32[]{:S(2)}) collective-permute-start(bf16[2,4,64,128]{3,2,1,0:T(8,128)(2,1)S(1)} %get-tuple-element.41), channel_id=1, source_target_pairs={{48,96},{96,48},{144,192},{192,144},{240,288},{288,240},{336,384},... | collective-permute-start | bytes 393224 | tf_op jit(solution)/shard_map/ppermute | solution.py:26
  48.0 0.0 collective-permute-done.6.second_ref
  48.1 1.9 %collective-permute-start.8 = (bf16[4,160,128]{2,1,0:T(8,128)(2,1)S(1)}, bf16[4,160,128]{2,1,0:T(8,128)(2,1)S(1)}, u32[]{:S(2)}, u32[]{:S(2)}) collective-permute-start(bf16[4,160,128]{2,1,0:T(8,128)(2,1)S(1)} %join_pair.4.first_ref), channel_id=1, source_target_pairs={{0,96},{48,144},{96,0},{144,48},{192,288},{240,336},{288,192},{336... | collective-permute-start | bytes 491528 | tf_op jit(solution)/shard_map/ppermute | solution.py:31
  50.0 1.0 %near_margin.1 = bf16[2,12,64,128]{3,2,1,0:T(8,128)(2,1)S(1)} custom-call(s32[3]{0:T(128)S(1)} %pad_add_fusion.info_ref.refs_0_, s32[4,96]{1,0:T(4,128)S(1)} %bitcast.14, bf16[96,64,256]{2,1,0:T(8,128)(2,1)S(1)} %bitcast.11, bf16[96,64,128]{2,1,0:T(8,128)(2,1)S(1)} %get-tuple-element.43.grid_ref), custom_call_target="tpu_custom_call" | custom-call | flops 17179869184 | bytes 1024 | tf_op jit(solution)/shard_map/near_margin/pallas_call | solution.py:39
  51.0 1.2 %center_fixes.1 = (bf16[4,2,64,128]{3,2,1,0:T(8,128)(2,1)S(1)}, bf16[4,2,64,128]{3,2,1,0:T(8,128)(2,1)S(1)}, bf16[4,8,64,128]{3,2,1,0:T(8,128)(2,1)S(1)}) custom-call(s32[3]{0:T(128)S(1)} %pad_add_fusion.info_ref.refs_0_, s32[4,96]{1,0:T(4,128)S(1)} %bitcast.15, bf16[96,64,256]{2,1,0:T(8,128)(2,1)S(1)} %bitcast.12, ...), custom_call_target="tpu_custom_call" | custom-call | bytes 1024 | tf_op jit(solution)/shard_map/center_fixes/pallas_call | solution.py:39
  52.2 1.9 %collective-permute-start.10 = (bf16[2,12,64,128]{3,2,1,0:T(8,128)(2,1)S(1)}, bf16[2,12,64,128]{3,2,1,0:T(8,128)(2,1)S(1)}, u32[]{:S(2)}, u32[]{:S(2)}) collective-permute-start(bf16[2,12,64,128]{3,2,1,0:T(8,128)(2,1)S(1)} %near_margin.1), channel_id=1, source_target_pairs={{0,48},{48,0},{96,144},{144,96},{192,240},{240,192},{288,336},{336... | collective-permute-start | bytes 1179656 | tf_op jit(solution)/shard_map/ppermute | solution.py:18
  54.1 7.0 %collective-permute-start.11 = (bf16[2,8,64,128]{3,2,1,0:T(8,128)(2,1)S(1)}, bf16[2,8,64,128]{3,2,1,0:T(8,128)(2,1)S(1)}, u32[]{:S(2)}, u32[]{:S(2)}) collective-permute-start(bf16[2,8,64,128]{3,2,1,0:T(8,128)(2,1)S(1)} %get-tuple-element.45), channel_id=1, source_target_pairs={{48,96},{96,48},{144,192},{192,144},{240,288},{288,240},{336,384},... | collective-permute-start | bytes 786440 | tf_op jit(solution)/shard_map/ppermute | solution.py:26
  61.1 0.0 collective-permute-done.7.refs_2_
  61.1 0.0 collective-permute-done.8.second_ref
  61.1 1.9 %collective-permute-start.9 = (bf16[8,160,128]{2,1,0:T(8,128)(2,1)S(1)}, bf16[8,160,128]{2,1,0:T(8,128)(2,1)S(1)}, u32[]{:S(2)}, u32[]{:S(2)}) collective-permute-start(bf16[8,160,128]{2,1,0:T(8,128)(2,1)S(1)} %join_pair.5.refs_1_), channel_id=1, source_target_pairs={{0,48},{48,0},{96,144},{144,96},{192,240},{240,192},{288,336},{336... | collective-permute-start | bytes 983048 | tf_op jit(solution)/shard_map/ppermute | solution.py:31
  63.1 0.0 collective-permute-done.10.refs_3_.main_near
  63.1 0.6 fold_side.2
  63.7 0.6 fold_side.3
  64.3 0.0 copy-start.5
  64.3 4.2 %collective-permute-start.12 = (bf16[4,2,64,128]{3,2,1,0:T(8,128)(2,1)S(1)}, bf16[4,2,64,128]{3,2,1,0:T(8,128)(2,1)S(1)}, u32[]{:S(2)}, u32[]{:S(2)}) collective-permute-start(bf16[4,2,64,128]{3,2,1,0:T(8,128)(2,1)S(1)} %fold_side.3), channel_id=1, source_target_pairs={{1,2},{2,1},{3,4},{4,3},{5,6},{6,5},{7,8},{8,7},{9,10},{10,9},{11,... | collective-permute-start | bytes 393224 | tf_op jit(solution)/shard_map/ppermute | solution.py:26
  68.5 2.7 %collective-permute-start.13 = (bf16[4,2,64,128]{3,2,1,0:T(8,128)(2,1)S(1)}, bf16[4,2,64,128]{3,2,1,0:T(8,128)(2,1)S(1)}, u32[]{:S(2)}, u32[]{:S(2)}) collective-permute-start(bf16[4,2,64,128]{3,2,1,0:T(8,128)(2,1)S(1)} %fold_side.2), channel_id=1, source_target_pairs={{0,1},{1,0},{2,3},{3,2},{4,5},{5,4},{6,7},{7,6},{8,9},{9,8},{10,11... | collective-permute-start | bytes 393224 | tf_op jit(solution)/shard_map/ppermute | solution.py:18
  71.2 0.0 collective-permute-done.9.refs_2_
  71.2 2.8 %coarse_values.1.coarse_ref = f32[512,128]{1,0:T(8,128)S(1)} custom-call(s32[3]{0:T(128)S(1)} %pad_add_fusion.info_ref.refs_0_, bf16[8,160,128]{2,1,0:T(8,128)(2,1)S(1)} %join_pair.5.refs_1_, bf16[8,160,128]{2,1,0:T(8,128)(2,1)S(1)} %collective-permute-done.9.refs_2_), custom_call_target="tpu_custom_call" | custom-call | flops 17179869184 | bytes 1024 | tf_op jit(solution)/shard_map/coarse_values/pallas_call | solution.py:39
  74.0 0.0 copy-done.5
  74.0 0.8 %lift.1.lifted_ref = f32[128,128]{1,0:T(8,128)S(1)} custom-call(s32[4,8]{1,0:T(4,128)S(1)} %copy-done.5, f32[512,128]{1,0:T(8,128)S(1)} %coarse_values.1.coarse_ref), custom_call_target="tpu_custom_call" | custom-call | flops 17179869184 | bytes 1024 | tf_op jit(solution)/shard_map/lift/pallas_call | solution.py:39
  74.9 0.0 collective-permute-done.11.main_far
  74.9 0.0 collective-permute-done.12.cross_far
  74.9 3.5 %collective-permute-done.13.cross_near = bf16[4,2,64,128]{3,2,1,0:T(8,128)(2,1)S(1)} collective-permute-done((bf16[4,2,64,128]{3,2,1,0:T(8,128)(2,1)S(1)}, bf16[4,2,64,128]{3,2,1,0:T(8,128)(2,1)S(1)}, u32[]{:S(2)}, u32[]{:S(2)}) %collective-permute-start.13) | collective-permute-done | bytes 131104 | tf_op jit(solution)/shard_map/ppermute | solution.py:18
  78.4 2.0 %join.1 = f32[4,8,64,128]{3,2,1,0:T(8,128)} custom-call(s32[3]{0:T(128)S(1)} %pad_add_fusion.info_ref.refs_0_, f32[128,128]{1,0:T(8,128)S(1)} %lift.1.lifted_ref, bf16[4,8,64,128]{3,2,1,0:T(8,128)(2,1)S(1)} %get-tuple-element.44.center_ref, bf16[2,12,64,128]{3,2,1,0:T(8,128)(2,1)S(1)} %collective-permute-done.10.refs_3_.main_near, ...), custom_call_target="tpu_custom_call" | custom-call | flops 17179869184 | bytes 1024 | tf_op jit(solution)/shard_map/join/pallas_call | solution.py:39
  (3 shorter events, 0.0 us)
Async XLA Ops:
  0.7 1.0 %copy-start.2 = (bf16[4,8,64,128]{3,2,1,0:T(8,128)(2,1)S(1)}, bf16[4,8,64,128]{3,2,1,0:T(8,128)(2,1)}, u32[]{:S(2)}) copy-start(bf16[4,8,64,128]{3,2,1,0:T(8,128)(2,1)} %residual_ref.1) | copy-start | bytes 1572868
  1.8 14.4 %copy-start.3 = (f32[32,32]{1,0:T(8,128)S(1)}, f32[32,32]{1,0:T(8,128)}, u32[]{:S(2)}) copy-start(f32[32,32]{1,0:T(8,128)} %inverse_ref.1) | copy-start | bytes 12292
  1.8 14.4 %copy-start.4 = (s32[4,8]{1,0:T(4,128)S(1)}, s32[4,8]{1,0:T(4,128)}, u32[]{:S(2)}) copy-start(s32[4,8]{1,0:T(4,128)} %agg_ref.3) | copy-start | bytes 388
  2.5 20.5 %collective-permute-start = (bf16[2,8,64,128]{3,2,1,0:T(8,128)(2,1)S(1)}, bf16[2,8,64,128]{3,2,1,0:T(8,128)(2,1)S(1)}, u32[]{:S(2)}, u32[]{:S(2)}) collective-permute-start(bf16[2,8,64,128]{3,2,1,0:T(8,128)(2,1)S(1)} %get-tuple-element.28.own_far), channel_id=1, source_target_pairs={{48,96},{96,48},{144,192},{192,144},{240,288},{288,240},{336,384},... | collective-permute-start | bytes 786440 | tf_op jit(solution)/shard_map/ppermute | solution.py:26
  10.5 9.7 %collective-permute-start.1 = (bf16[4,2,64,128]{3,2,1,0:T(8,128)(2,1)S(1)}, bf16[4,2,64,128]{3,2,1,0:T(8,128)(2,1)S(1)}, u32[]{:S(2)}, u32[]{:S(2)}) collective-permute-start(bf16[4,2,64,128]{3,2,1,0:T(8,128)(2,1)S(1)} %get-tuple-element.29), channel_id=1, source_target_pairs={{1,2},{2,1},{3,4},{4,3},{5,6},{6,5},{7,8},{8,7},{9,10},{10,9},{11,... | collective-permute-start | bytes 393224 | tf_op jit(solution)/shard_map/ppermute | solution.py:26
  14.2 8.8 %collective-permute-start.2 = (bf16[4,2,64,128]{3,2,1,0:T(8,128)(2,1)S(1)}, bf16[4,2,64,128]{3,2,1,0:T(8,128)(2,1)S(1)}, u32[]{:S(2)}, u32[]{:S(2)}) collective-permute-start(bf16[4,2,64,128]{3,2,1,0:T(8,128)(2,1)S(1)} %get-tuple-element.30), channel_id=1, source_target_pairs={{0,1},{1,0},{2,3},{3,2},{4,5},{5,4},{6,7},{7,6},{8,9},{9,8},{10,11... | collective-permute-start | bytes 393224 | tf_op jit(solution)/shard_map/ppermute | solution.py:18
  23.6 10.2 %collective-permute-start.3 = (bf16[1,160,128]{2,1,0:T(8,128)(2,1)S(1)}, bf16[1,160,128]{2,1,0:T(8,128)(2,1)S(1)}, u32[]{:S(2)}, u32[]{:S(2)}) collective-permute-start(bf16[1,160,128]{2,1,0:T(8,128)(2,1)S(1)} %payload.1.first_ref), channel_id=1, source_target_pairs={{0,384},{48,432},{96,480},{144,528},{192,576},{240,624},{288,672},... | collective-permute-start | bytes 122888 | tf_op jit(solution)/shard_map/ppermute | solution.py:31
  26.1 16.2 %copy-start = (bf16[1,96,64,256]{3,2,1,0:T(8,128)(2,1)S(1)}, bf16[1,96,64,256]{3,2,1,0:T(8,128)(2,1)}, u32[]{:S(2)}) copy-start(bf16[1,96,64,256]{3,2,1,0:T(8,128)(2,1)} %param.7) | copy-start | bytes 9437188
  26.1 16.2 %copy-start.1 = (s32[1,96,4]{1,2,0:T(4,128)S(1)}, s32[1,96,4]{1,2,0:T(4,128)}, u32[]{:S(2)}) copy-start(s32[1,96,4]{1,2,0:T(4,128)} %param.8) | copy-start | bytes 4612
  26.1 16.2 %collective-permute-start.5 = (bf16[2,12,64,128]{3,2,1,0:T(8,128)(2,1)S(1)}, bf16[2,12,64,128]{3,2,1,0:T(8,128)(2,1)S(1)}, u32[]{:S(2)}, u32[]{:S(2)}) collective-permute-start(bf16[2,12,64,128]{3,2,1,0:T(8,128)(2,1)S(1)} %near_message.1), channel_id=1, source_target_pairs={{0,48},{48,0},{96,144},{144,96},{192,240},{240,192},{288,336},{336... | collective-permute-start | bytes 1179656 | tf_op jit(solution)/shard_map/ppermute | solution.py:18
  28.8 13.5 %collective-permute-start.4 = (bf16[2,4,64,128]{3,2,1,0:T(8,128)(2,1)S(1)}, bf16[2,4,64,128]{3,2,1,0:T(8,128)(2,1)S(1)}, u32[]{:S(2)}, u32[]{:S(2)}) collective-permute-start(bf16[2,4,64,128]{3,2,1,0:T(8,128)(2,1)S(1)} %far_corners.1), channel_id=1, source_target_pairs={{48,96},{96,48},{144,192},{192,144},{240,288},{288,240},{336,384},... | collective-permute-start | bytes 393224 | tf_op jit(solution)/shard_map/ppermute | solution.py:26
  33.8 14.3 %collective-permute-start.6 = (bf16[2,160,128]{2,1,0:T(8,128)(2,1)S(1)}, bf16[2,160,128]{2,1,0:T(8,128)(2,1)S(1)}, u32[]{:S(2)}, u32[]{:S(2)}) collective-permute-start(bf16[2,160,128]{2,1,0:T(8,128)(2,1)S(1)} %join_pair.3.first_ref), channel_id=1, source_target_pairs={{0,192},{48,240},{96,288},{144,336},{192,0},{240,48},{288,96},{336... | collective-permute-start | bytes 245768 | tf_op jit(solution)/shard_map/ppermute | solution.py:31
  43.4 17.7 %collective-permute-start.7 = (bf16[2,4,64,128]{3,2,1,0:T(8,128)(2,1)S(1)}, bf16[2,4,64,128]{3,2,1,0:T(8,128)(2,1)S(1)}, u32[]{:S(2)}, u32[]{:S(2)}) collective-permute-start(bf16[2,4,64,128]{3,2,1,0:T(8,128)(2,1)S(1)} %get-tuple-element.41), channel_id=1, source_target_pairs={{48,96},{96,48},{144,192},{192,144},{240,288},{288,240},{336,384},... | collective-permute-start | bytes 393224 | tf_op jit(solution)/shard_map/ppermute | solution.py:26
  48.1 13.0 %collective-permute-start.8 = (bf16[4,160,128]{2,1,0:T(8,128)(2,1)S(1)}, bf16[4,160,128]{2,1,0:T(8,128)(2,1)S(1)}, u32[]{:S(2)}, u32[]{:S(2)}) collective-permute-start(bf16[4,160,128]{2,1,0:T(8,128)(2,1)S(1)} %join_pair.4.first_ref), channel_id=1, source_target_pairs={{0,96},{48,144},{96,0},{144,48},{192,288},{240,336},{288,192},{336... | collective-permute-start | bytes 491528 | tf_op jit(solution)/shard_map/ppermute | solution.py:31
  52.2 10.9 %collective-permute-start.10 = (bf16[2,12,64,128]{3,2,1,0:T(8,128)(2,1)S(1)}, bf16[2,12,64,128]{3,2,1,0:T(8,128)(2,1)S(1)}, u32[]{:S(2)}, u32[]{:S(2)}) collective-permute-start(bf16[2,12,64,128]{3,2,1,0:T(8,128)(2,1)S(1)} %near_margin.1), channel_id=1, source_target_pairs={{0,48},{48,0},{96,144},{144,96},{192,240},{240,192},{288,336},{336... | collective-permute-start | bytes 1179656 | tf_op jit(solution)/shard_map/ppermute | solution.py:18
  54.1 20.7 %collective-permute-start.11 = (bf16[2,8,64,128]{3,2,1,0:T(8,128)(2,1)S(1)}, bf16[2,8,64,128]{3,2,1,0:T(8,128)(2,1)S(1)}, u32[]{:S(2)}, u32[]{:S(2)}) collective-permute-start(bf16[2,8,64,128]{3,2,1,0:T(8,128)(2,1)S(1)} %get-tuple-element.45), channel_id=1, source_target_pairs={{48,96},{96,48},{144,192},{192,144},{240,288},{288,240},{336,384},... | collective-permute-start | bytes 786440 | tf_op jit(solution)/shard_map/ppermute | solution.py:26
  61.1 10.0 %collective-permute-start.9 = (bf16[8,160,128]{2,1,0:T(8,128)(2,1)S(1)}, bf16[8,160,128]{2,1,0:T(8,128)(2,1)S(1)}, u32[]{:S(2)}, u32[]{:S(2)}) collective-permute-start(bf16[8,160,128]{2,1,0:T(8,128)(2,1)S(1)} %join_pair.5.refs_1_), channel_id=1, source_target_pairs={{0,48},{48,0},{96,144},{144,96},{192,240},{240,192},{288,336},{336... | collective-permute-start | bytes 983048 | tf_op jit(solution)/shard_map/ppermute | solution.py:31
  64.3 9.8 %copy-start.5 = (s32[4,8]{1,0:T(4,128)S(1)}, s32[4,8]{1,0:T(4,128)}, u32[]{:S(2)}) copy-start(s32[4,8]{1,0:T(4,128)} %agg_ref.3) | copy-start | bytes 388
  64.3 10.6 %collective-permute-start.12 = (bf16[4,2,64,128]{3,2,1,0:T(8,128)(2,1)S(1)}, bf16[4,2,64,128]{3,2,1,0:T(8,128)(2,1)S(1)}, u32[]{:S(2)}, u32[]{:S(2)}) collective-permute-start(bf16[4,2,64,128]{3,2,1,0:T(8,128)(2,1)S(1)} %fold_side.3), channel_id=1, source_target_pairs={{1,2},{2,1},{3,4},{4,3},{5,6},{6,5},{7,8},{8,7},{9,10},{10,9},{11,... | collective-permute-start | bytes 393224 | tf_op jit(solution)/shard_map/ppermute | solution.py:26
  68.5 9.9 %collective-permute-start.13 = (bf16[4,2,64,128]{3,2,1,0:T(8,128)(2,1)S(1)}, bf16[4,2,64,128]{3,2,1,0:T(8,128)(2,1)S(1)}, u32[]{:S(2)}, u32[]{:S(2)}) collective-permute-start(bf16[4,2,64,128]{3,2,1,0:T(8,128)(2,1)S(1)} %fold_side.2), channel_id=1, source_target_pairs={{0,1},{1,0},{2,3},{3,2},{4,5},{5,4},{6,7},{7,6},{8,9},{9,8},{10,11... | collective-permute-start | bytes 393224 | tf_op jit(solution)/shard_map/ppermute | solution.py:18

commit v7 on v5

--- a/solution.py
+++ b/solution.py
@@ -244,25 +244,24 @@
     )
 
 
-def fold_kernel(info_ref, side_near, side_far, got_near, corner_far, out_near, out_far):
+def fold_kernel(first, info_ref, side_ref, corner_far, got_near, out_ref):
     half, wide = got_near.shape[:2]
     p, _ = parities(info_ref)
-    for source, start, first in (
-        (got_near, half * (1 - p), wide - 4), (corner_far, half * p, 0)
-    ):
+    for source, start, base in ((got_near, half * (1 - p), wide - 4), (corner_far, half * p, 0)):
         for i in range(half):
             for j in range(2):
-                for side, out, at in ((side_near, out_near, j), (side_far, out_far, 2 + j)):
-                    total = side[start + i, j].astype(F32) + source[i, first + at].astype(F32)
-                    out[start + i, j] = total.astype(BF16)
-
-
-def fold_sides(info, side_near, side_far, got_near, corner_far):
-    piece = shaped(side_near.shape, BF16)
-    return call(
-        fold_kernel, "fold_sides", (piece, piece),
-        (info, side_near, side_far, got_near, corner_far),
-        [SMEM] + [VMEM] * 4, (VMEM, VMEM), 3,
+                total = side_ref[start + i, j].astype(F32)
+                total = total + source[i, base + first + j].astype(F32)
+                out_ref[start + i, j] = total.astype(BF16)
+
+
+def fold_side(first, info, side, corner_far, got_near):
+    def kernel(*refs):
+        fold_kernel(first, *refs)
+
+    return call(
+        kernel, "fold_side", shaped(side.shape, BF16), (info, side, corner_far, got_near),
+        [SMEM] + [VMEM] * 3, VMEM, 3,
     )
 
 
@@ -417,7 +416,9 @@
         gathered = join_pair(gathered, other)
         other = swap_bit(gathered, "stream", bit)
     gathered, near, corner_far = lax.optimization_barrier((gathered, near, corner_far))
-    side_near, side_far = fold_sides(info, side_near, side_far, near, corner_far)
+    side_far = fold_side(2, info, side_far, corner_far, near)
+    side_far, side_near = lax.optimization_barrier((side_far, side_near))
+    side_near = fold_side(0, info, side_near, corner_far, near)
     cross_far = swap_far(side_far, "cross")
     cross_near = swap_near(side_near, "cross")
     lifted = coarse_values(bits, info, block_aggregate, gathered, other)

time: 79.4 us -> 79.9 us (level)
    pallas_call x11 -> x12, Pallas kernels: 10.4 us -> 10.9 us  [call(): pl.pallas_call(kernel, out_shape=outs, in_specs=specs, out_specs=out_spec...]
where the time goes in v7:
time: 79.9 us; the launch traced here: 78.4 us
  starting transfers between devices  54.7 us (68%)
  Pallas kernels  10.9 us (14%)
  waiting for transfers between devices  10.8 us (14%)
  local copies, waits for them, and re-layouts  1.06 us (1%)
  between operations  0.94 us (1%)
    ppermute x6, starting transfers between devices, swap_far(): return lax.ppermute(values, axis, pairs)  32.7 us
    ppermute x4, starting transfers between devices, swap_near(): lax.ppermute(values, axis, [(i, i ^ 1) for i in range(count) if i ^ 1 < c...  12.7 us
    pallas_call x12, Pallas kernels, call(): pl.pallas_call(kernel, out_shape=outs, in_specs=specs, out_specs=out_spec...  10.9 us
    ppermute x4, starting transfers between devices, swap_bit(): return lax.ppermute(values, axis, [(i, i ^ bit) for i in range(count)])  9.27 us
    ppermute x6, waiting for transfers between devices, swap_far(): return lax.ppermute(values, axis, pairs)  7.37 us
    ppermute x4, waiting for transfers between devices, swap_near(): lax.ppermute(values, axis, [(i, i ^ 1) for i in range(count) if i ^ 1 < c...  2.84 us
  transfers between devices with their start and end apart: 14, of which 5 were waited for; matrix products, arithmetic and copies ran while one was open for 0% of the time, Pallas kernels for 10%

profile of v7, /device:TPU:519, one launch (start us, length us, event | category | flops | bytes accessed | tf_op | source)
XLA Modules:
  0.0 78.4 jit_solution(11590421206606267384)
XLA Ops:
  0.7 0.1 pad_add_fusion.info_ref.refs_0_
  0.7 0.0 copy-start.2
  0.7 1.0 %copy-done.2 = bf16[4,8,64,128]{3,2,1,0:T(8,128)(2,1)S(1)} copy-done((bf16[4,8,64,128]{3,2,1,0:T(8,128)(2,1)S(1)}, bf16[4,8,64,128]{3,2,1,0:T(8,128)(2,1)}, u32[]{:S(2)}) %copy-start.2) | copy-done | bytes 524312
  1.8 0.0 copy-start.3
  1.8 0.0 copy-start.4
  1.8 0.7 mask_blocks.1
  2.5 7.9 %collective-permute-start = (bf16[2,8,64,128]{3,2,1,0:T(8,128)(2,1)S(1)}, bf16[2,8,64,128]{3,2,1,0:T(8,128)(2,1)S(1)}, u32[]{:S(2)}, u32[]{:S(2)}) collective-permute-start(bf16[2,8,64,128]{3,2,1,0:T(8,128)(2,1)S(1)} %get-tuple-element.36.own_far), channel_id=1, source_target_pairs={{48,96},{96,48},{144,192},{192,144},{240,288},{288,240},{336,384},... | collective-permute-start | bytes 786440 | tf_op jit(solution)/shard_map/ppermute | solution.py:26
  10.5 3.7 %collective-permute-start.1 = (bf16[4,2,64,128]{3,2,1,0:T(8,128)(2,1)S(1)}, bf16[4,2,64,128]{3,2,1,0:T(8,128)(2,1)S(1)}, u32[]{:S(2)}, u32[]{:S(2)}) collective-permute-start(bf16[4,2,64,128]{3,2,1,0:T(8,128)(2,1)S(1)} %get-tuple-element.37), channel_id=1, source_target_pairs={{1,2},{2,1},{3,4},{4,3},{5,6},{6,5},{7,8},{8,7},{9,10},{10,9},{11,... | collective-permute-start | bytes 393224 | tf_op jit(solution)/shard_map/ppermute | solution.py:26
  14.2 1.9 %collective-permute-start.2 = (bf16[4,2,64,128]{3,2,1,0:T(8,128)(2,1)S(1)}, bf16[4,2,64,128]{3,2,1,0:T(8,128)(2,1)S(1)}, u32[]{:S(2)}, u32[]{:S(2)}) collective-permute-start(bf16[4,2,64,128]{3,2,1,0:T(8,128)(2,1)S(1)} %get-tuple-element.38), channel_id=1, source_target_pairs={{0,1},{1,0},{2,3},{3,2},{4,5},{5,4},{6,7},{7,6},{8,9},{9,8},{10,11... | collective-permute-start | bytes 393224 | tf_op jit(solution)/shard_map/ppermute | solution.py:18
  16.1 0.0 copy-done.3
  16.1 0.0 copy-done.4
  16.2 0.8 %payload.1.first_ref = bf16[1,160,128]{2,1,0:T(8,128)(2,1)S(1)} custom-call(s32[3]{0:T(128)S(1)} %pad_add_fusion.info_ref.refs_0_, s32[4,8]{1,0:T(4,128)S(1)} %copy-done.4, bf16[1024,128]{1,0:T(8,128)(2,1)S(1)} %bitcast.15, bf16[1024,128]{1,0:T(8,128)(2,1)S(1)} %bitcast.14, f32[32,32]{1,0:T(8,128)S(1)} %copy-done.3), custom_call_target="tpu_custom_call" | custom-call | flops 17179869184 | bytes 1024 | tf_op jit(solution)/shard_map/payload/pallas_call | solution.py:39
  17.0 3.2 %collective-permute-done.1.cross_far = bf16[4,2,64,128]{3,2,1,0:T(8,128)(2,1)S(1)} collective-permute-done((bf16[4,2,64,128]{3,2,1,0:T(8,128)(2,1)S(1)}, bf16[4,2,64,128]{3,2,1,0:T(8,128)(2,1)S(1)}, u32[]{:S(2)}, u32[]{:S(2)}) %collective-permute-start.1) | collective-permute-done | bytes 131104 | tf_op jit(solution)/shard_map/ppermute | solution.py:26
  20.2 2.8 %collective-permute-done.2.cross_near = bf16[4,2,64,128]{3,2,1,0:T(8,128)(2,1)S(1)} collective-permute-done((bf16[4,2,64,128]{3,2,1,0:T(8,128)(2,1)S(1)}, bf16[4,2,64,128]{3,2,1,0:T(8,128)(2,1)S(1)}, u32[]{:S(2)}, u32[]{:S(2)}) %collective-permute-start.2) | collective-permute-done | bytes 131104 | tf_op jit(solution)/shard_map/ppermute | solution.py:18
  23.0 0.0 collective-permute-done.got_far
  23.0 1.9 %collective-permute-start.3 = (bf16[1,160,128]{2,1,0:T(8,128)(2,1)S(1)}, bf16[1,160,128]{2,1,0:T(8,128)(2,1)S(1)}, u32[]{:S(2)}, u32[]{:S(2)}) collective-permute-start(bf16[1,160,128]{2,1,0:T(8,128)(2,1)S(1)} %payload.1.first_ref), channel_id=1, source_target_pairs={{0,384},{48,432},{96,480},{144,528},{192,576},{240,624},{288,672},... | collective-permute-start | bytes 122888 | tf_op jit(solution)/shard_map/ppermute | solution.py:31
  24.9 0.6 corners.1
  25.5 5.4 %collective-permute-start.4 = (bf16[2,4,64,128]{3,2,1,0:T(8,128)(2,1)S(1)}, bf16[2,4,64,128]{3,2,1,0:T(8,128)(2,1)S(1)}, u32[]{:S(2)}, u32[]{:S(2)}) collective-permute-start(bf16[2,4,64,128]{3,2,1,0:T(8,128)(2,1)S(1)} %get-tuple-element.43), channel_id=1, source_target_pairs={{48,96},{96,48},{144,192},{192,144},{240,288},{288,240},{336,384},... | collective-permute-start | bytes 393224 | tf_op jit(solution)/shard_map/ppermute | solution.py:26
  31.0 0.0 copy-start
  31.0 0.0 copy-start.1
  31.0 2.2 %collective-permute-start.5 = (bf16[2,12,64,128]{3,2,1,0:T(8,128)(2,1)S(1)}, bf16[2,12,64,128]{3,2,1,0:T(8,128)(2,1)S(1)}, u32[]{:S(2)}, u32[]{:S(2)}) collective-permute-start(bf16[2,12,64,128]{3,2,1,0:T(8,128)(2,1)S(1)} %get-tuple-element.44), channel_id=1, source_target_pairs={{0,48},{48,0},{96,144},{144,96},{192,240},{240,192},{288,336},{336... | collective-permute-start | bytes 1179656 | tf_op jit(solution)/shard_map/ppermute | solution.py:18
  33.2 0.0 collective-permute-done.3.second_ref
  33.2 3.5 %collective-permute-start.6 = (bf16[2,160,128]{2,1,0:T(8,128)(2,1)S(1)}, bf16[2,160,128]{2,1,0:T(8,128)(2,1)S(1)}, u32[]{:S(2)}, u32[]{:S(2)}) collective-permute-start(bf16[2,160,128]{2,1,0:T(8,128)(2,1)S(1)} %join_pair.3.first_ref), channel_id=1, source_target_pairs={{0,192},{48,240},{96,288},{144,336},{192,0},{240,48},{288,96},{336... | collective-permute-start | bytes 245768 | tf_op jit(solution)/shard_map/ppermute | solution.py:31
  36.7 1.2 %collective-permute-done.4.corner_far = bf16[2,4,64,128]{3,2,1,0:T(8,128)(2,1)S(1)} collective-permute-done((bf16[2,4,64,128]{3,2,1,0:T(8,128)(2,1)S(1)}, bf16[2,4,64,128]{3,2,1,0:T(8,128)(2,1)S(1)}, u32[]{:S(2)}, u32[]{:S(2)}) %collective-permute-start.4) | collective-permute-done | bytes 131104 | tf_op jit(solution)/shard_map/ppermute | solution.py:26
  37.9 0.0 collective-permute-done.5.got_near
  37.9 0.0 copy-done
  37.9 0.0 copy-done.1
  37.9 1.4 %margin_fixes.1 = (bf16[2,12,64,128]{3,2,1,0:T(8,128)(2,1)S(1)}, bf16[2,8,64,128]{3,2,1,0:T(8,128)(2,1)S(1)}, bf16[2,4,64,128]{3,2,1,0:T(8,128)(2,1)S(1)}, bf16[96,64,128]{2,1,0:T(8,128)(2,1)S(1)}) custom-call(s32[3]{0:T(128)S(1)} %pad_add_fusion.info_ref.refs_0_, s32[4,96]{1,0:T(4,128)S(1)} %bitcast.12, bf16[96,64,256]{2,1,0:T(8,128)(2,1)S(1)} %bitcast.10, ...), custom_call_target="tpu_custom_call" | custom-call | flops 17179869184 | bytes 1024 | tf_op jit(solution)/shard_map/margin_fixes/pallas_call | solution.py:39
  39.4 0.5 collective-permute-done.6.second_ref
  39.9 3.5 %collective-permute-start.7 = (bf16[2,12,64,128]{3,2,1,0:T(8,128)(2,1)S(1)}, bf16[2,12,64,128]{3,2,1,0:T(8,128)(2,1)S(1)}, u32[]{:S(2)}, u32[]{:S(2)}) collective-permute-start(bf16[2,12,64,128]{3,2,1,0:T(8,128)(2,1)S(1)} %get-tuple-element.51), channel_id=1, source_target_pairs={{0,48},{48,0},{96,144},{144,96},{192,240},{240,192},{288,336},{336... | collective-permute-start | bytes 1179656 | tf_op jit(solution)/shard_map/ppermute | solution.py:18
  43.5 1.9 %collective-permute-start.8 = (bf16[4,160,128]{2,1,0:T(8,128)(2,1)S(1)}, bf16[4,160,128]{2,1,0:T(8,128)(2,1)S(1)}, u32[]{:S(2)}, u32[]{:S(2)}) collective-permute-start(bf16[4,160,128]{2,1,0:T(8,128)(2,1)S(1)} %join_pair.4.first_ref), channel_id=1, source_target_pairs={{0,96},{48,144},{96,0},{144,48},{192,288},{240,336},{288,192},{336... | collective-permute-start | bytes 491528 | tf_op jit(solution)/shard_map/ppermute | solution.py:31
  45.4 6.1 %collective-permute-start.9 = (bf16[2,4,64,128]{3,2,1,0:T(8,128)(2,1)S(1)}, bf16[2,4,64,128]{3,2,1,0:T(8,128)(2,1)S(1)}, u32[]{:S(2)}, u32[]{:S(2)}) collective-permute-start(bf16[2,4,64,128]{3,2,1,0:T(8,128)(2,1)S(1)} %get-tuple-element.57), channel_id=1, source_target_pairs={{48,96},{96,48},{144,192},{192,144},{240,288},{288,240},{336,384},... | collective-permute-start | bytes 393224 | tf_op jit(solution)/shard_map/ppermute | solution.py:26
  51.5 5.5 %collective-permute-start.11 = (bf16[2,8,64,128]{3,2,1,0:T(8,128)(2,1)S(1)}, bf16[2,8,64,128]{3,2,1,0:T(8,128)(2,1)S(1)}, u32[]{:S(2)}, u32[]{:S(2)}) collective-permute-start(bf16[2,8,64,128]{3,2,1,0:T(8,128)(2,1)S(1)} %get-tuple-element.61), channel_id=1, source_target_pairs={{48,96},{96,48},{144,192},{192,144},{240,288},{288,240},{336,384},... | collective-permute-start | bytes 786440 | tf_op jit(solution)/shard_map/ppermute | solution.py:26
  57.0 0.0 collective-permute-done.7.refs_3_.main_near
  57.0 1.2 %center_fixes.1 = (bf16[4,2,64,128]{3,2,1,0:T(8,128)(2,1)S(1)}, bf16[4,2,64,128]{3,2,1,0:T(8,128)(2,1)S(1)}, bf16[4,8,64,128]{3,2,1,0:T(8,128)(2,1)S(1)}) custom-call(s32[3]{0:T(128)S(1)} %pad_add_fusion.info_ref.refs_0_, s32[4,96]{1,0:T(4,128)S(1)} %bitcast.13, bf16[96,64,256]{2,1,0:T(8,128)(2,1)S(1)} %bitcast.11, ...), custom_call_target="tpu_custom_call" | custom-call | bytes 1024 | tf_op jit(solution)/shard_map/center_fixes/pallas_call | solution.py:39
  58.2 0.0 collective-permute-done.8.second_ref
  58.3 1.9 %collective-permute-start.10 = (bf16[8,160,128]{2,1,0:T(8,128)(2,1)S(1)}, bf16[8,160,128]{2,1,0:T(8,128)(2,1)S(1)}, u32[]{:S(2)}, u32[]{:S(2)}) collective-permute-start(bf16[8,160,128]{2,1,0:T(8,128)(2,1)S(1)} %join_pair.5.refs_2_), channel_id=1, source_target_pairs={{0,48},{48,0},{96,144},{144,96},{192,240},{240,192},{288,336},{336... | collective-permute-start | bytes 983048 | tf_op jit(solution)/shard_map/ppermute | solution.py:31
  60.2 0.0 collective-permute-done.9.refs_2_
  60.2 0.6 fold_side.2
  60.8 0.6 fold_side.3
  61.4 5.0 %collective-permute-start.12 = (bf16[4,2,64,128]{3,2,1,0:T(8,128)(2,1)S(1)}, bf16[4,2,64,128]{3,2,1,0:T(8,128)(2,1)S(1)}, u32[]{:S(2)}, u32[]{:S(2)}) collective-permute-start(bf16[4,2,64,128]{3,2,1,0:T(8,128)(2,1)S(1)} %fold_side.3), channel_id=1, source_target_pairs={{0,1},{1,0},{2,3},{3,2},{4,5},{5,4},{6,7},{7,6},{8,9},{9,8},{10,11... | collective-permute-start | bytes 393224 | tf_op jit(solution)/shard_map/ppermute | solution.py:18
  66.4 4.1 %collective-permute-start.13 = (bf16[4,2,64,128]{3,2,1,0:T(8,128)(2,1)S(1)}, bf16[4,2,64,128]{3,2,1,0:T(8,128)(2,1)S(1)}, u32[]{:S(2)}, u32[]{:S(2)}) collective-permute-start(bf16[4,2,64,128]{3,2,1,0:T(8,128)(2,1)S(1)} %fold_side.2), channel_id=1, source_target_pairs={{1,2},{2,1},{3,4},{4,3},{5,6},{6,5},{7,8},{8,7},{9,10},{10,9},{11,... | collective-permute-start | bytes 393224 | tf_op jit(solution)/shard_map/ppermute | solution.py:26
  70.5 0.0 collective-permute-done.10.refs_3_
  70.5 3.0 %coarse_values.1.lifted_ref = f32[128,128]{1,0:T(8,128)S(1)} custom-call(s32[3]{0:T(128)S(1)} %pad_add_fusion.info_ref.refs_0_, s32[4,8]{1,0:T(4,128)S(1)} %copy-done.4, bf16[8,160,128]{2,1,0:T(8,128)(2,1)S(1)} %join_pair.5.refs_2_, bf16[8,160,128]{2,1,0:T(8,128)(2,1)S(1)} %collective-permute-done.10.refs_3_), custom_call_target="tpu_custom_call" | custom-call | flops 17179869184 | bytes 1024 | tf_op jit(solution)/shard_map/coarse_values/pallas_call | solution.py:39
  73.5 0.0 collective-permute-done.11.main_far
  73.5 0.0 collective-permute-done.12.cross_near
  73.6 2.9 %collective-permute-done.13.cross_far = bf16[4,2,64,128]{3,2,1,0:T(8,128)(2,1)S(1)} collective-permute-done((bf16[4,2,64,128]{3,2,1,0:T(8,128)(2,1)S(1)}, bf16[4,2,64,128]{3,2,1,0:T(8,128)(2,1)S(1)}, u32[]{:S(2)}, u32[]{:S(2)}) %collective-permute-start.13) | collective-permute-done | bytes 131104 | tf_op jit(solution)/shard_map/ppermute | solution.py:26
  76.5 2.0 %join.1 = f32[4,8,64,128]{3,2,1,0:T(8,128)} custom-call(s32[3]{0:T(128)S(1)} %pad_add_fusion.info_ref.refs_0_, f32[128,128]{1,0:T(8,128)S(1)} %coarse_values.1.lifted_ref, bf16[4,8,64,128]{3,2,1,0:T(8,128)(2,1)S(1)} %get-tuple-element.59.center_ref, bf16[2,12,64,128]{3,2,1,0:T(8,128)(2,1)S(1)} %collective-permute-done.7.refs_3_.main_near, ...), custom_call_target="tpu_custom_call" | custom-call | flops 17179869184 | bytes 1024 | tf_op jit(solution)/shard_map/join/pallas_call | solution.py:39
  (3 shorter events, 0.0 us)
Async XLA Ops:
  0.7 1.0 %copy-start.2 = (bf16[4,8,64,128]{3,2,1,0:T(8,128)(2,1)S(1)}, bf16[4,8,64,128]{3,2,1,0:T(8,128)(2,1)}, u32[]{:S(2)}) copy-start(bf16[4,8,64,128]{3,2,1,0:T(8,128)(2,1)} %residual_ref.1) | copy-start | bytes 1572868
  1.8 14.4 %copy-start.3 = (f32[32,32]{1,0:T(8,128)S(1)}, f32[32,32]{1,0:T(8,128)}, u32[]{:S(2)}) copy-start(f32[32,32]{1,0:T(8,128)} %inverse_ref.1) | copy-start | bytes 12292
  1.8 14.4 %copy-start.4 = (s32[4,8]{1,0:T(4,128)S(1)}, s32[4,8]{1,0:T(4,128)}, u32[]{:S(2)}) copy-start(s32[4,8]{1,0:T(4,128)} %refs_1_.1) | copy-start | bytes 388
  2.5 20.5 %collective-permute-start = (bf16[2,8,64,128]{3,2,1,0:T(8,128)(2,1)S(1)}, bf16[2,8,64,128]{3,2,1,0:T(8,128)(2,1)S(1)}, u32[]{:S(2)}, u32[]{:S(2)}) collective-permute-start(bf16[2,8,64,128]{3,2,1,0:T(8,128)(2,1)S(1)} %get-tuple-element.36.own_far), channel_id=1, source_target_pairs={{48,96},{96,48},{144,192},{192,144},{240,288},{288,240},{336,384},... | collective-permute-start | bytes 786440 | tf_op jit(solution)/shard_map/ppermute | solution.py:26
  10.5 9.7 %collective-permute-start.1 = (bf16[4,2,64,128]{3,2,1,0:T(8,128)(2,1)S(1)}, bf16[4,2,64,128]{3,2,1,0:T(8,128)(2,1)S(1)}, u32[]{:S(2)}, u32[]{:S(2)}) collective-permute-start(bf16[4,2,64,128]{3,2,1,0:T(8,128)(2,1)S(1)} %get-tuple-element.37), channel_id=1, source_target_pairs={{1,2},{2,1},{3,4},{4,3},{5,6},{6,5},{7,8},{8,7},{9,10},{10,9},{11,... | collective-permute-start | bytes 393224 | tf_op jit(solution)/shard_map/ppermute | solution.py:26
  14.2 8.8 %collective-permute-start.2 = (bf16[4,2,64,128]{3,2,1,0:T(8,128)(2,1)S(1)}, bf16[4,2,64,128]{3,2,1,0:T(8,128)(2,1)S(1)}, u32[]{:S(2)}, u32[]{:S(2)}) collective-permute-start(bf16[4,2,64,128]{3,2,1,0:T(8,128)(2,1)S(1)} %get-tuple-element.38), channel_id=1, source_target_pairs={{0,1},{1,0},{2,3},{3,2},{4,5},{5,4},{6,7},{7,6},{8,9},{9,8},{10,11... | collective-permute-start | bytes 393224 | tf_op jit(solution)/shard_map/ppermute | solution.py:18
  23.0 10.1 %collective-permute-start.3 = (bf16[1,160,128]{2,1,0:T(8,128)(2,1)S(1)}, bf16[1,160,128]{2,1,0:T(8,128)(2,1)S(1)}, u32[]{:S(2)}, u32[]{:S(2)}) collective-permute-start(bf16[1,160,128]{2,1,0:T(8,128)(2,1)S(1)} %payload.1.first_ref), channel_id=1, source_target_pairs={{0,384},{48,432},{96,480},{144,528},{192,576},{240,624},{288,672},... | collective-permute-start | bytes 122888 | tf_op jit(solution)/shard_map/ppermute | solution.py:31
  25.5 12.4 %collective-permute-start.4 = (bf16[2,4,64,128]{3,2,1,0:T(8,128)(2,1)S(1)}, bf16[2,4,64,128]{3,2,1,0:T(8,128)(2,1)S(1)}, u32[]{:S(2)}, u32[]{:S(2)}) collective-permute-start(bf16[2,4,64,128]{3,2,1,0:T(8,128)(2,1)S(1)} %get-tuple-element.43), channel_id=1, source_target_pairs={{48,96},{96,48},{144,192},{192,144},{240,288},{288,240},{336,384},... | collective-permute-start | bytes 393224 | tf_op jit(solution)/shard_map/ppermute | solution.py:26
  31.0 7.0 %copy-start = (bf16[1,96,64,256]{3,2,1,0:T(8,128)(2,1)S(1)}, bf16[1,96,64,256]{3,2,1,0:T(8,128)(2,1)}, u32[]{:S(2)}) copy-start(bf16[1,96,64,256]{3,2,1,0:T(8,128)(2,1)} %param.7) | copy-start | bytes 9437188
  31.0 7.0 %copy-start.1 = (s32[1,96,4]{1,2,0:T(4,128)S(1)}, s32[1,96,4]{1,2,0:T(4,128)}, u32[]{:S(2)}) copy-start(s32[1,96,4]{1,2,0:T(4,128)} %param.8) | copy-start | bytes 4612
  31.0 7.0 %collective-permute-start.5 = (bf16[2,12,64,128]{3,2,1,0:T(8,128)(2,1)S(1)}, bf16[2,12,64,128]{3,2,1,0:T(8,128)(2,1)S(1)}, u32[]{:S(2)}, u32[]{:S(2)}) collective-permute-start(bf16[2,12,64,128]{3,2,1,0:T(8,128)(2,1)S(1)} %get-tuple-element.44), channel_id=1, source_target_pairs={{0,48},{48,0},{96,144},{144,96},{192,240},{240,192},{288,336},{336... | collective-permute-start | bytes 1179656 | tf_op jit(solution)/shard_map/ppermute | solution.py:18
  33.2 6.7 %collective-permute-start.6 = (bf16[2,160,128]{2,1,0:T(8,128)(2,1)S(1)}, bf16[2,160,128]{2,1,0:T(8,128)(2,1)S(1)}, u32[]{:S(2)}, u32[]{:S(2)}) collective-permute-start(bf16[2,160,128]{2,1,0:T(8,128)(2,1)S(1)} %join_pair.3.first_ref), channel_id=1, source_target_pairs={{0,192},{48,240},{96,288},{144,336},{192,0},{240,48},{288,96},{336... | collective-permute-start | bytes 245768 | tf_op jit(solution)/shard_map/ppermute | solution.py:31
  39.9 17.1 %collective-permute-start.7 = (bf16[2,12,64,128]{3,2,1,0:T(8,128)(2,1)S(1)}, bf16[2,12,64,128]{3,2,1,0:T(8,128)(2,1)S(1)}, u32[]{:S(2)}, u32[]{:S(2)}) collective-permute-start(bf16[2,12,64,128]{3,2,1,0:T(8,128)(2,1)S(1)} %get-tuple-element.51), channel_id=1, source_target_pairs={{0,48},{48,0},{96,144},{144,96},{192,240},{240,192},{288,336},{336... | collective-permute-start | bytes 1179656 | tf_op jit(solution)/shard_map/ppermute | solution.py:18
  43.5 14.8 %collective-permute-start.8 = (bf16[4,160,128]{2,1,0:T(8,128)(2,1)S(1)}, bf16[4,160,128]{2,1,0:T(8,128)(2,1)S(1)}, u32[]{:S(2)}, u32[]{:S(2)}) collective-permute-start(bf16[4,160,128]{2,1,0:T(8,128)(2,1)S(1)} %join_pair.4.first_ref), channel_id=1, source_target_pairs={{0,96},{48,144},{96,0},{144,48},{192,288},{240,336},{288,192},{336... | collective-permute-start | bytes 491528 | tf_op jit(solution)/shard_map/ppermute | solution.py:31
  45.4 14.8 %collective-permute-start.9 = (bf16[2,4,64,128]{3,2,1,0:T(8,128)(2,1)S(1)}, bf16[2,4,64,128]{3,2,1,0:T(8,128)(2,1)S(1)}, u32[]{:S(2)}, u32[]{:S(2)}) collective-permute-start(bf16[2,4,64,128]{3,2,1,0:T(8,128)(2,1)S(1)} %get-tuple-element.57), channel_id=1, source_target_pairs={{48,96},{96,48},{144,192},{192,144},{240,288},{288,240},{336,384},... | collective-permute-start | bytes 393224 | tf_op jit(solution)/shard_map/ppermute | solution.py:26
  51.5 22.1 %collective-permute-start.11 = (bf16[2,8,64,128]{3,2,1,0:T(8,128)(2,1)S(1)}, bf16[2,8,64,128]{3,2,1,0:T(8,128)(2,1)S(1)}, u32[]{:S(2)}, u32[]{:S(2)}) collective-permute-start(bf16[2,8,64,128]{3,2,1,0:T(8,128)(2,1)S(1)} %get-tuple-element.61), channel_id=1, source_target_pairs={{48,96},{96,48},{144,192},{192,144},{240,288},{288,240},{336,384},... | collective-permute-start | bytes 786440 | tf_op jit(solution)/shard_map/ppermute | solution.py:26
  58.3 12.2 %collective-permute-start.10 = (bf16[8,160,128]{2,1,0:T(8,128)(2,1)S(1)}, bf16[8,160,128]{2,1,0:T(8,128)(2,1)S(1)}, u32[]{:S(2)}, u32[]{:S(2)}) collective-permute-start(bf16[8,160,128]{2,1,0:T(8,128)(2,1)S(1)} %join_pair.5.refs_2_), channel_id=1, source_target_pairs={{0,48},{48,0},{96,144},{144,96},{192,240},{240,192},{288,336},{336... | collective-permute-start | bytes 983048 | tf_op jit(solution)/shard_map/ppermute | solution.py:31
  61.4 12.2 %collective-permute-start.12 = (bf16[4,2,64,128]{3,2,1,0:T(8,128)(2,1)S(1)}, bf16[4,2,64,128]{3,2,1,0:T(8,128)(2,1)S(1)}, u32[]{:S(2)}, u32[]{:S(2)}) collective-permute-start(bf16[4,2,64,128]{3,2,1,0:T(8,128)(2,1)S(1)} %fold_side.3), channel_id=1, source_target_pairs={{0,1},{1,0},{2,3},{3,2},{4,5},{5,4},{6,7},{7,6},{8,9},{9,8},{10,11... | collective-permute-start | bytes 393224 | tf_op jit(solution)/shard_map/ppermute | solution.py:18
  66.4 10.0 %collective-permute-start.13 = (bf16[4,2,64,128]{3,2,1,0:T(8,128)(2,1)S(1)}, bf16[4,2,64,128]{3,2,1,0:T(8,128)(2,1)S(1)}, u32[]{:S(2)}, u32[]{:S(2)}) collective-permute-start(bf16[4,2,64,128]{3,2,1,0:T(8,128)(2,1)S(1)} %fold_side.2), channel_id=1, source_target_pairs={{1,2},{2,1},{3,4},{4,3},{5,6},{6,5},{7,8},{8,7},{9,10},{10,9},{11,... | collective-permute-start | bytes 393224 | tf_op jit(solution)/shard_map/ppermute | solution.py:26

commit v8 on v7

--- a/solution.py
+++ b/solution.py
@@ -337,7 +337,7 @@
 
 
 def join_kernel(
-    info_ref, lifted_ref, center_ref, main_near, main_far, cross_near, cross_far, out_ref
+    info_ref, lifted_ref, center_ref, main_near, main_far, cross_far, cross_near, out_ref
 ):
     rows, columns, width, sides = center_ref.shape
     half = rows // 2
@@ -370,10 +370,10 @@
                 out_ref[i, j] = jnp.zeros((width, sides), F32)
 
 
-def join(info, lifted, center, main_near, main_far, cross_near, cross_far):
+def join(info, lifted, center, main_near, main_far, cross_far, cross_near):
     return call(
         join_kernel, "join", shaped(center.shape, F32),
-        (info, lifted, center, main_near, main_far, cross_near, cross_far),
+        (info, lifted, center, main_near, main_far, cross_far, cross_near),
         [SMEM] + [VMEM] * 6, VMEM, 6,
     )
 
@@ -422,7 +422,7 @@
     cross_far = swap_far(side_far, "cross")
     cross_near = swap_near(side_near, "cross")
     lifted = coarse_values(bits, info, block_aggregate, gathered, other)
-    return join(info, lifted, center, near, far, cross_near, cross_far)
+    return join(info, lifted, center, near, far, cross_far, cross_near)
 
 
 def solution(mesh):

time: 79.9 us -> 77.4 us (0.969); the launches traced: 78.4 us -> 76.9 us
  starting transfers between devices: 54.7 us -> 52.6 us
    ppermute x4, waiting for transfers between devices: 2.84 us -> 6.31 us  [swap_near(): lax.ppermute(values, axis, [(i, i ^ 1) for i in range(count) if i ^ 1 < c...]
    ppermute x4, starting transfers between devices: 12.7 us -> 9.59 us  [swap_near(): lax.ppermute(values, axis, [(i, i ^ 1) for i in range(count) if i ^ 1 < c...]
    ppermute x6, waiting for transfers between devices: 7.37 us -> 4.45 us  [swap_far(): return lax.ppermute(values, axis, pairs)]
    ppermute x6, starting transfers between devices: 32.7 us -> 33.7 us  [swap_far(): return lax.ppermute(values, axis, pairs)]
  transfers between devices with their start and end apart: 14 -> 14, of which waited for: 5 -> 5; matrix products, arithmetic and copies ran while one was open for 0% -> 0% of each run, Pallas kernels for 10% -> 11%
where the time goes in v8:
time: 77.4 us; the launch traced here: 76.9 us
  starting transfers between devices  52.6 us (68%)
  waiting for transfers between devices  11.3 us (15%)
  Pallas kernels  10.9 us (14%)
  local copies, waits for them, and re-layouts  1.06 us (1%)
  between operations  0.94 us (1%)
    ppermute x6, starting transfers between devices, swap_far(): return lax.ppermute(values, axis, pairs)  33.7 us
    pallas_call x12, Pallas kernels, call(): pl.pallas_call(kernel, out_shape=outs, in_specs=specs, out_specs=out_spec...  10.9 us
    ppermute x4, starting transfers between devices, swap_near(): lax.ppermute(values, axis, [(i, i ^ 1) for i in range(count) if i ^ 1 < c...  9.59 us
    ppermute x4, starting transfers between devices, swap_bit(): return lax.ppermute(values, axis, [(i, i ^ bit) for i in range(count)])  9.27 us
    ppermute x4, waiting for transfers between devices, swap_near(): lax.ppermute(values, axis, [(i, i ^ 1) for i in range(count) if i ^ 1 < c...  6.31 us
    ppermute x6, waiting for transfers between devices, swap_far(): return lax.ppermute(values, axis, pairs)  4.45 us
  transfers between devices with their start and end apart: 14, of which 5 were waited for; matrix products, arithmetic and copies ran while one was open for 0% of the time, Pallas kernels for 11%

profile of v8, /device:TPU:519, one launch (start us, length us, event | category | flops | bytes accessed | tf_op | source)
XLA Modules:
  0.0 76.9 jit_solution(8128955040716012423)
XLA Ops:
  0.7 0.1 pad_add_fusion.info_ref.refs_0_
  0.7 0.0 copy-start.2
  0.7 1.0 %copy-done.2 = bf16[4,8,64,128]{3,2,1,0:T(8,128)(2,1)S(1)} copy-done((bf16[4,8,64,128]{3,2,1,0:T(8,128)(2,1)S(1)}, bf16[4,8,64,128]{3,2,1,0:T(8,128)(2,1)}, u32[]{:S(2)}) %copy-start.2) | copy-done | bytes 524312
  1.8 0.0 copy-start.3
  1.8 0.0 copy-start.4
  1.8 0.7 mask_blocks.1
  2.5 7.9 %collective-permute-start = (bf16[2,8,64,128]{3,2,1,0:T(8,128)(2,1)S(1)}, bf16[2,8,64,128]{3,2,1,0:T(8,128)(2,1)S(1)}, u32[]{:S(2)}, u32[]{:S(2)}) collective-permute-start(bf16[2,8,64,128]{3,2,1,0:T(8,128)(2,1)S(1)} %get-tuple-element.36.own_far), channel_id=1, source_target_pairs={{48,96},{96,48},{144,192},{192,144},{240,288},{288,240},{336,384},... | collective-permute-start | bytes 786440 | tf_op jit(solution)/shard_map/ppermute | solution.py:26
  10.5 3.7 %collective-permute-start.1 = (bf16[4,2,64,128]{3,2,1,0:T(8,128)(2,1)S(1)}, bf16[4,2,64,128]{3,2,1,0:T(8,128)(2,1)S(1)}, u32[]{:S(2)}, u32[]{:S(2)}) collective-permute-start(bf16[4,2,64,128]{3,2,1,0:T(8,128)(2,1)S(1)} %get-tuple-element.37), channel_id=1, source_target_pairs={{1,2},{2,1},{3,4},{4,3},{5,6},{6,5},{7,8},{8,7},{9,10},{10,9},{11,... | collective-permute-start | bytes 393224 | tf_op jit(solution)/shard_map/ppermute | solution.py:26
  14.2 1.9 %collective-permute-start.2 = (bf16[4,2,64,128]{3,2,1,0:T(8,128)(2,1)S(1)}, bf16[4,2,64,128]{3,2,1,0:T(8,128)(2,1)S(1)}, u32[]{:S(2)}, u32[]{:S(2)}) collective-permute-start(bf16[4,2,64,128]{3,2,1,0:T(8,128)(2,1)S(1)} %get-tuple-element.38), channel_id=1, source_target_pairs={{0,1},{1,0},{2,3},{3,2},{4,5},{5,4},{6,7},{7,6},{8,9},{9,8},{10,11... | collective-permute-start | bytes 393224 | tf_op jit(solution)/shard_map/ppermute | solution.py:18
  16.1 0.0 copy-done.3
  16.1 0.0 copy-done.4
  16.2 0.8 %payload.1.first_ref = bf16[1,160,128]{2,1,0:T(8,128)(2,1)S(1)} custom-call(s32[3]{0:T(128)S(1)} %pad_add_fusion.info_ref.refs_0_, s32[4,8]{1,0:T(4,128)S(1)} %copy-done.4, bf16[1024,128]{1,0:T(8,128)(2,1)S(1)} %bitcast.15, bf16[1024,128]{1,0:T(8,128)(2,1)S(1)} %bitcast.14, f32[32,32]{1,0:T(8,128)S(1)} %copy-done.3), custom_call_target="tpu_custom_call" | custom-call | flops 17179869184 | bytes 1024 | tf_op jit(solution)/shard_map/payload/pallas_call | solution.py:39
  17.0 3.2 %collective-permute-done.1.cross_far = bf16[4,2,64,128]{3,2,1,0:T(8,128)(2,1)S(1)} collective-permute-done((bf16[4,2,64,128]{3,2,1,0:T(8,128)(2,1)S(1)}, bf16[4,2,64,128]{3,2,1,0:T(8,128)(2,1)S(1)}, u32[]{:S(2)}, u32[]{:S(2)}) %collective-permute-start.1) | collective-permute-done | bytes 131104 | tf_op jit(solution)/shard_map/ppermute | solution.py:26
  20.2 2.8 %collective-permute-done.2.cross_near = bf16[4,2,64,128]{3,2,1,0:T(8,128)(2,1)S(1)} collective-permute-done((bf16[4,2,64,128]{3,2,1,0:T(8,128)(2,1)S(1)}, bf16[4,2,64,128]{3,2,1,0:T(8,128)(2,1)S(1)}, u32[]{:S(2)}, u32[]{:S(2)}) %collective-permute-start.2) | collective-permute-done | bytes 131104 | tf_op jit(solution)/shard_map/ppermute | solution.py:18
  23.0 0.0 collective-permute-done.got_far
  23.0 1.9 %collective-permute-start.3 = (bf16[1,160,128]{2,1,0:T(8,128)(2,1)S(1)}, bf16[1,160,128]{2,1,0:T(8,128)(2,1)S(1)}, u32[]{:S(2)}, u32[]{:S(2)}) collective-permute-start(bf16[1,160,128]{2,1,0:T(8,128)(2,1)S(1)} %payload.1.first_ref), channel_id=1, source_target_pairs={{0,384},{48,432},{96,480},{144,528},{192,576},{240,624},{288,672},... | collective-permute-start | bytes 122888 | tf_op jit(solution)/shard_map/ppermute | solution.py:31
  24.9 0.6 corners.1
  25.5 5.4 %collective-permute-start.4 = (bf16[2,4,64,128]{3,2,1,0:T(8,128)(2,1)S(1)}, bf16[2,4,64,128]{3,2,1,0:T(8,128)(2,1)S(1)}, u32[]{:S(2)}, u32[]{:S(2)}) collective-permute-start(bf16[2,4,64,128]{3,2,1,0:T(8,128)(2,1)S(1)} %get-tuple-element.43), channel_id=1, source_target_pairs={{48,96},{96,48},{144,192},{192,144},{240,288},{288,240},{336,384},... | collective-permute-start | bytes 393224 | tf_op jit(solution)/shard_map/ppermute | solution.py:26
  31.0 0.0 copy-start
  31.0 0.0 copy-start.1
  31.0 2.2 %collective-permute-start.5 = (bf16[2,12,64,128]{3,2,1,0:T(8,128)(2,1)S(1)}, bf16[2,12,64,128]{3,2,1,0:T(8,128)(2,1)S(1)}, u32[]{:S(2)}, u32[]{:S(2)}) collective-permute-start(bf16[2,12,64,128]{3,2,1,0:T(8,128)(2,1)S(1)} %get-tuple-element.44), channel_id=1, source_target_pairs={{0,48},{48,0},{96,144},{144,96},{192,240},{240,192},{288,336},{336... | collective-permute-start | bytes 1179656 | tf_op jit(solution)/shard_map/ppermute | solution.py:18
  33.2 0.0 collective-permute-done.3.second_ref
  33.2 3.5 %collective-permute-start.6 = (bf16[2,160,128]{2,1,0:T(8,128)(2,1)S(1)}, bf16[2,160,128]{2,1,0:T(8,128)(2,1)S(1)}, u32[]{:S(2)}, u32[]{:S(2)}) collective-permute-start(bf16[2,160,128]{2,1,0:T(8,128)(2,1)S(1)} %join_pair.3.first_ref), channel_id=1, source_target_pairs={{0,192},{48,240},{96,288},{144,336},{192,0},{240,48},{288,96},{336... | collective-permute-start | bytes 245768 | tf_op jit(solution)/shard_map/ppermute | solution.py:31
  36.7 1.2 %collective-permute-done.4.corner_far = bf16[2,4,64,128]{3,2,1,0:T(8,128)(2,1)S(1)} collective-permute-done((bf16[2,4,64,128]{3,2,1,0:T(8,128)(2,1)S(1)}, bf16[2,4,64,128]{3,2,1,0:T(8,128)(2,1)S(1)}, u32[]{:S(2)}, u32[]{:S(2)}) %collective-permute-start.4) | collective-permute-done | bytes 131104 | tf_op jit(solution)/shard_map/ppermute | solution.py:26
  37.9 0.0 collective-permute-done.5.got_near
  37.9 0.0 copy-done
  37.9 0.0 copy-done.1
  37.9 1.4 %margin_fixes.1 = (bf16[2,12,64,128]{3,2,1,0:T(8,128)(2,1)S(1)}, bf16[2,8,64,128]{3,2,1,0:T(8,128)(2,1)S(1)}, bf16[2,4,64,128]{3,2,1,0:T(8,128)(2,1)S(1)}, bf16[96,64,128]{2,1,0:T(8,128)(2,1)S(1)}) custom-call(s32[3]{0:T(128)S(1)} %pad_add_fusion.info_ref.refs_0_, s32[4,96]{1,0:T(4,128)S(1)} %bitcast.12, bf16[96,64,256]{2,1,0:T(8,128)(2,1)S(1)} %bitcast.10, ...), custom_call_target="tpu_custom_call" | custom-call | flops 17179869184 | bytes 1024 | tf_op jit(solution)/shard_map/margin_fixes/pallas_call | solution.py:39
  39.4 0.5 collective-permute-done.6.second_ref
  39.9 3.5 %collective-permute-start.7 = (bf16[2,12,64,128]{3,2,1,0:T(8,128)(2,1)S(1)}, bf16[2,12,64,128]{3,2,1,0:T(8,128)(2,1)S(1)}, u32[]{:S(2)}, u32[]{:S(2)}) collective-permute-start(bf16[2,12,64,128]{3,2,1,0:T(8,128)(2,1)S(1)} %get-tuple-element.51), channel_id=1, source_target_pairs={{0,48},{48,0},{96,144},{144,96},{192,240},{240,192},{288,336},{336... | collective-permute-start | bytes 1179656 | tf_op jit(solution)/shard_map/ppermute | solution.py:18
  43.5 1.9 %collective-permute-start.8 = (bf16[4,160,128]{2,1,0:T(8,128)(2,1)S(1)}, bf16[4,160,128]{2,1,0:T(8,128)(2,1)S(1)}, u32[]{:S(2)}, u32[]{:S(2)}) collective-permute-start(bf16[4,160,128]{2,1,0:T(8,128)(2,1)S(1)} %join_pair.4.first_ref), channel_id=1, source_target_pairs={{0,96},{48,144},{96,0},{144,48},{192,288},{240,336},{288,192},{336... | collective-permute-start | bytes 491528 | tf_op jit(solution)/shard_map/ppermute | solution.py:31
  45.4 6.1 %collective-permute-start.9 = (bf16[2,4,64,128]{3,2,1,0:T(8,128)(2,1)S(1)}, bf16[2,4,64,128]{3,2,1,0:T(8,128)(2,1)S(1)}, u32[]{:S(2)}, u32[]{:S(2)}) collective-permute-start(bf16[2,4,64,128]{3,2,1,0:T(8,128)(2,1)S(1)} %get-tuple-element.57), channel_id=1, source_target_pairs={{48,96},{96,48},{144,192},{192,144},{240,288},{288,240},{336,384},... | collective-permute-start | bytes 393224 | tf_op jit(solution)/shard_map/ppermute | solution.py:26
  51.5 5.5 %collective-permute-start.11 = (bf16[2,8,64,128]{3,2,1,0:T(8,128)(2,1)S(1)}, bf16[2,8,64,128]{3,2,1,0:T(8,128)(2,1)S(1)}, u32[]{:S(2)}, u32[]{:S(2)}) collective-permute-start(bf16[2,8,64,128]{3,2,1,0:T(8,128)(2,1)S(1)} %get-tuple-element.61), channel_id=1, source_target_pairs={{48,96},{96,48},{144,192},{192,144},{240,288},{288,240},{336,384},... | collective-permute-start | bytes 786440 | tf_op jit(solution)/shard_map/ppermute | solution.py:26
  57.0 0.0 collective-permute-done.7.refs_3_.main_near
  57.0 1.2 %center_fixes.1 = (bf16[4,2,64,128]{3,2,1,0:T(8,128)(2,1)S(1)}, bf16[4,2,64,128]{3,2,1,0:T(8,128)(2,1)S(1)}, bf16[4,8,64,128]{3,2,1,0:T(8,128)(2,1)S(1)}) custom-call(s32[3]{0:T(128)S(1)} %pad_add_fusion.info_ref.refs_0_, s32[4,96]{1,0:T(4,128)S(1)} %bitcast.13, bf16[96,64,256]{2,1,0:T(8,128)(2,1)S(1)} %bitcast.11, ...), custom_call_target="tpu_custom_call" | custom-call | bytes 1024 | tf_op jit(solution)/shard_map/center_fixes/pallas_call | solution.py:39
  58.2 0.0 collective-permute-done.8.second_ref
  58.3 1.9 %collective-permute-start.10 = (bf16[8,160,128]{2,1,0:T(8,128)(2,1)S(1)}, bf16[8,160,128]{2,1,0:T(8,128)(2,1)S(1)}, u32[]{:S(2)}, u32[]{:S(2)}) collective-permute-start(bf16[8,160,128]{2,1,0:T(8,128)(2,1)S(1)} %join_pair.5.refs_2_), channel_id=1, source_target_pairs={{0,48},{48,0},{96,144},{144,96},{192,240},{240,192},{288,336},{336... | collective-permute-start | bytes 983048 | tf_op jit(solution)/shard_map/ppermute | solution.py:31
  60.2 0.0 collective-permute-done.9.refs_2_
  60.2 0.6 fold_side.2
  60.8 5.1 %collective-permute-start.12 = (bf16[4,2,64,128]{3,2,1,0:T(8,128)(2,1)S(1)}, bf16[4,2,64,128]{3,2,1,0:T(8,128)(2,1)S(1)}, u32[]{:S(2)}, u32[]{:S(2)}) collective-permute-start(bf16[4,2,64,128]{3,2,1,0:T(8,128)(2,1)S(1)} %fold_side.2), channel_id=1, source_target_pairs={{1,2},{2,1},{3,4},{4,3},{5,6},{6,5},{7,8},{8,7},{9,10},{10,9},{11,... | collective-permute-start | bytes 393224 | tf_op jit(solution)/shard_map/ppermute | solution.py:26
  65.9 0.6 fold_side.3
  66.5 1.9 %collective-permute-start.13 = (bf16[4,2,64,128]{3,2,1,0:T(8,128)(2,1)S(1)}, bf16[4,2,64,128]{3,2,1,0:T(8,128)(2,1)S(1)}, u32[]{:S(2)}, u32[]{:S(2)}) collective-permute-start(bf16[4,2,64,128]{3,2,1,0:T(8,128)(2,1)S(1)} %fold_side.3), channel_id=1, source_target_pairs={{0,1},{1,0},{2,3},{3,2},{4,5},{5,4},{6,7},{7,6},{8,9},{9,8},{10,11... | collective-permute-start | bytes 393224 | tf_op jit(solution)/shard_map/ppermute | solution.py:18
  68.4 0.0 collective-permute-done.10.refs_3_
  68.4 3.0 %coarse_values.1.lifted_ref = f32[128,128]{1,0:T(8,128)S(1)} custom-call(s32[3]{0:T(128)S(1)} %pad_add_fusion.info_ref.refs_0_, s32[4,8]{1,0:T(4,128)S(1)} %copy-done.4, bf16[8,160,128]{2,1,0:T(8,128)(2,1)S(1)} %join_pair.5.refs_2_, bf16[8,160,128]{2,1,0:T(8,128)(2,1)S(1)} %collective-permute-done.10.refs_3_), custom_call_target="tpu_custom_call" | custom-call | flops 17179869184 | bytes 1024 | tf_op jit(solution)/shard_map/coarse_values/pallas_call | solution.py:39
  71.4 0.0 collective-permute-done.11.main_far
  71.4 0.0 collective-permute-done.12.cross_far
  71.5 3.5 %collective-permute-done.13.cross_near = bf16[4,2,64,128]{3,2,1,0:T(8,128)(2,1)S(1)} collective-permute-done((bf16[4,2,64,128]{3,2,1,0:T(8,128)(2,1)S(1)}, bf16[4,2,64,128]{3,2,1,0:T(8,128)(2,1)S(1)}, u32[]{:S(2)}, u32[]{:S(2)}) %collective-permute-start.13) | collective-permute-done | bytes 131104 | tf_op jit(solution)/shard_map/ppermute | solution.py:18
  74.9 2.0 %join.1 = f32[4,8,64,128]{3,2,1,0:T(8,128)} custom-call(s32[3]{0:T(128)S(1)} %pad_add_fusion.info_ref.refs_0_, f32[128,128]{1,0:T(8,128)S(1)} %coarse_values.1.lifted_ref, bf16[4,8,64,128]{3,2,1,0:T(8,128)(2,1)S(1)} %get-tuple-element.59.center_ref, bf16[2,12,64,128]{3,2,1,0:T(8,128)(2,1)S(1)} %collective-permute-done.7.refs_3_.main_near, ...), custom_call_target="tpu_custom_call" | custom-call | flops 17179869184 | bytes 1024 | tf_op jit(solution)/shard_map/join/pallas_call | solution.py:39
  (3 shorter events, 0.0 us)
Async XLA Ops:
  0.7 1.0 %copy-start.2 = (bf16[4,8,64,128]{3,2,1,0:T(8,128)(2,1)S(1)}, bf16[4,8,64,128]{3,2,1,0:T(8,128)(2,1)}, u32[]{:S(2)}) copy-start(bf16[4,8,64,128]{3,2,1,0:T(8,128)(2,1)} %residual_ref.1) | copy-start | bytes 1572868
  1.8 14.4 %copy-start.3 = (f32[32,32]{1,0:T(8,128)S(1)}, f32[32,32]{1,0:T(8,128)}, u32[]{:S(2)}) copy-start(f32[32,32]{1,0:T(8,128)} %inverse_ref.1) | copy-start | bytes 12292
  1.8 14.4 %copy-start.4 = (s32[4,8]{1,0:T(4,128)S(1)}, s32[4,8]{1,0:T(4,128)}, u32[]{:S(2)}) copy-start(s32[4,8]{1,0:T(4,128)} %refs_1_.1) | copy-start | bytes 388
  2.5 20.5 %collective-permute-start = (bf16[2,8,64,128]{3,2,1,0:T(8,128)(2,1)S(1)}, bf16[2,8,64,128]{3,2,1,0:T(8,128)(2,1)S(1)}, u32[]{:S(2)}, u32[]{:S(2)}) collective-permute-start(bf16[2,8,64,128]{3,2,1,0:T(8,128)(2,1)S(1)} %get-tuple-element.36.own_far), channel_id=1, source_target_pairs={{48,96},{96,48},{144,192},{192,144},{240,288},{288,240},{336,384},... | collective-permute-start | bytes 786440 | tf_op jit(solution)/shard_map/ppermute | solution.py:26
  10.5 9.7 %collective-permute-start.1 = (bf16[4,2,64,128]{3,2,1,0:T(8,128)(2,1)S(1)}, bf16[4,2,64,128]{3,2,1,0:T(8,128)(2,1)S(1)}, u32[]{:S(2)}, u32[]{:S(2)}) collective-permute-start(bf16[4,2,64,128]{3,2,1,0:T(8,128)(2,1)S(1)} %get-tuple-element.37), channel_id=1, source_target_pairs={{1,2},{2,1},{3,4},{4,3},{5,6},{6,5},{7,8},{8,7},{9,10},{10,9},{11,... | collective-permute-start | bytes 393224 | tf_op jit(solution)/shard_map/ppermute | solution.py:26
  14.2 8.8 %collective-permute-start.2 = (bf16[4,2,64,128]{3,2,1,0:T(8,128)(2,1)S(1)}, bf16[4,2,64,128]{3,2,1,0:T(8,128)(2,1)S(1)}, u32[]{:S(2)}, u32[]{:S(2)}) collective-permute-start(bf16[4,2,64,128]{3,2,1,0:T(8,128)(2,1)S(1)} %get-tuple-element.38), channel_id=1, source_target_pairs={{0,1},{1,0},{2,3},{3,2},{4,5},{5,4},{6,7},{7,6},{8,9},{9,8},{10,11... | collective-permute-start | bytes 393224 | tf_op jit(solution)/shard_map/ppermute | solution.py:18
  23.0 10.1 %collective-permute-start.3 = (bf16[1,160,128]{2,1,0:T(8,128)(2,1)S(1)}, bf16[1,160,128]{2,1,0:T(8,128)(2,1)S(1)}, u32[]{:S(2)}, u32[]{:S(2)}) collective-permute-start(bf16[1,160,128]{2,1,0:T(8,128)(2,1)S(1)} %payload.1.first_ref), channel_id=1, source_target_pairs={{0,384},{48,432},{96,480},{144,528},{192,576},{240,624},{288,672},... | collective-permute-start | bytes 122888 | tf_op jit(solution)/shard_map/ppermute | solution.py:31
  25.5 12.4 %collective-permute-start.4 = (bf16[2,4,64,128]{3,2,1,0:T(8,128)(2,1)S(1)}, bf16[2,4,64,128]{3,2,1,0:T(8,128)(2,1)S(1)}, u32[]{:S(2)}, u32[]{:S(2)}) collective-permute-start(bf16[2,4,64,128]{3,2,1,0:T(8,128)(2,1)S(1)} %get-tuple-element.43), channel_id=1, source_target_pairs={{48,96},{96,48},{144,192},{192,144},{240,288},{288,240},{336,384},... | collective-permute-start | bytes 393224 | tf_op jit(solution)/shard_map/ppermute | solution.py:26
  31.0 7.0 %copy-start = (bf16[1,96,64,256]{3,2,1,0:T(8,128)(2,1)S(1)}, bf16[1,96,64,256]{3,2,1,0:T(8,128)(2,1)}, u32[]{:S(2)}) copy-start(bf16[1,96,64,256]{3,2,1,0:T(8,128)(2,1)} %param.7) | copy-start | bytes 9437188
  31.0 7.0 %copy-start.1 = (s32[1,96,4]{1,2,0:T(4,128)S(1)}, s32[1,96,4]{1,2,0:T(4,128)}, u32[]{:S(2)}) copy-start(s32[1,96,4]{1,2,0:T(4,128)} %param.8) | copy-start | bytes 4612
  31.0 7.0 %collective-permute-start.5 = (bf16[2,12,64,128]{3,2,1,0:T(8,128)(2,1)S(1)}, bf16[2,12,64,128]{3,2,1,0:T(8,128)(2,1)S(1)}, u32[]{:S(2)}, u32[]{:S(2)}) collective-permute-start(bf16[2,12,64,128]{3,2,1,0:T(8,128)(2,1)S(1)} %get-tuple-element.44), channel_id=1, source_target_pairs={{0,48},{48,0},{96,144},{144,96},{192,240},{240,192},{288,336},{336... | collective-permute-start | bytes 1179656 | tf_op jit(solution)/shard_map/ppermute | solution.py:18
  33.2 6.7 %collective-permute-start.6 = (bf16[2,160,128]{2,1,0:T(8,128)(2,1)S(1)}, bf16[2,160,128]{2,1,0:T(8,128)(2,1)S(1)}, u32[]{:S(2)}, u32[]{:S(2)}) collective-permute-start(bf16[2,160,128]{2,1,0:T(8,128)(2,1)S(1)} %join_pair.3.first_ref), channel_id=1, source_target_pairs={{0,192},{48,240},{96,288},{144,336},{192,0},{240,48},{288,96},{336... | collective-permute-start | bytes 245768 | tf_op jit(solution)/shard_map/ppermute | solution.py:31
  39.9 17.1 %collective-permute-start.7 = (bf16[2,12,64,128]{3,2,1,0:T(8,128)(2,1)S(1)}, bf16[2,12,64,128]{3,2,1,0:T(8,128)(2,1)S(1)}, u32[]{:S(2)}, u32[]{:S(2)}) collective-permute-start(bf16[2,12,64,128]{3,2,1,0:T(8,128)(2,1)S(1)} %get-tuple-element.51), channel_id=1, source_target_pairs={{0,48},{48,0},{96,144},{144,96},{192,240},{240,192},{288,336},{336... | collective-permute-start | bytes 1179656 | tf_op jit(solution)/shard_map/ppermute | solution.py:18
  43.5 14.8 %collective-permute-start.8 = (bf16[4,160,128]{2,1,0:T(8,128)(2,1)S(1)}, bf16[4,160,128]{2,1,0:T(8,128)(2,1)S(1)}, u32[]{:S(2)}, u32[]{:S(2)}) collective-permute-start(bf16[4,160,128]{2,1,0:T(8,128)(2,1)S(1)} %join_pair.4.first_ref), channel_id=1, source_target_pairs={{0,96},{48,144},{96,0},{144,48},{192,288},{240,336},{288,192},{336... | collective-permute-start | bytes 491528 | tf_op jit(solution)/shard_map/ppermute | solution.py:31
  45.4 14.8 %collective-permute-start.9 = (bf16[2,4,64,128]{3,2,1,0:T(8,128)(2,1)S(1)}, bf16[2,4,64,128]{3,2,1,0:T(8,128)(2,1)S(1)}, u32[]{:S(2)}, u32[]{:S(2)}) collective-permute-start(bf16[2,4,64,128]{3,2,1,0:T(8,128)(2,1)S(1)} %get-tuple-element.57), channel_id=1, source_target_pairs={{48,96},{96,48},{144,192},{192,144},{240,288},{288,240},{336,384},... | collective-permute-start | bytes 393224 | tf_op jit(solution)/shard_map/ppermute | solution.py:26
  51.5 20.0 %collective-permute-start.11 = (bf16[2,8,64,128]{3,2,1,0:T(8,128)(2,1)S(1)}, bf16[2,8,64,128]{3,2,1,0:T(8,128)(2,1)S(1)}, u32[]{:S(2)}, u32[]{:S(2)}) collective-permute-start(bf16[2,8,64,128]{3,2,1,0:T(8,128)(2,1)S(1)} %get-tuple-element.61), channel_id=1, source_target_pairs={{48,96},{96,48},{144,192},{192,144},{240,288},{288,240},{336,384},... | collective-permute-start | bytes 786440 | tf_op jit(solution)/shard_map/ppermute | solution.py:26
  58.3 10.1 %collective-permute-start.10 = (bf16[8,160,128]{2,1,0:T(8,128)(2,1)S(1)}, bf16[8,160,128]{2,1,0:T(8,128)(2,1)S(1)}, u32[]{:S(2)}, u32[]{:S(2)}) collective-permute-start(bf16[8,160,128]{2,1,0:T(8,128)(2,1)S(1)} %join_pair.5.refs_2_), channel_id=1, source_target_pairs={{0,48},{48,0},{96,144},{144,96},{192,240},{240,192},{288,336},{336... | collective-permute-start | bytes 983048 | tf_op jit(solution)/shard_map/ppermute | solution.py:31
  60.8 10.7 %collective-permute-start.12 = (bf16[4,2,64,128]{3,2,1,0:T(8,128)(2,1)S(1)}, bf16[4,2,64,128]{3,2,1,0:T(8,128)(2,1)S(1)}, u32[]{:S(2)}, u32[]{:S(2)}) collective-permute-start(bf16[4,2,64,128]{3,2,1,0:T(8,128)(2,1)S(1)} %fold_side.2), channel_id=1, source_target_pairs={{1,2},{2,1},{3,4},{4,3},{5,6},{6,5},{7,8},{8,7},{9,10},{10,9},{11,... | collective-permute-start | bytes 393224 | tf_op jit(solution)/shard_map/ppermute | solution.py:26
  66.5 8.5 %collective-permute-start.13 = (bf16[4,2,64,128]{3,2,1,0:T(8,128)(2,1)S(1)}, bf16[4,2,64,128]{3,2,1,0:T(8,128)(2,1)S(1)}, u32[]{:S(2)}, u32[]{:S(2)}) collective-permute-start(bf16[4,2,64,128]{3,2,1,0:T(8,128)(2,1)S(1)} %fold_side.3), channel_id=1, source_target_pairs={{0,1},{1,0},{2,3},{3,2},{4,5},{5,4},{6,7},{7,6},{8,9},{9,8},{10,11... | collective-permute-start | bytes 393224 | tf_op jit(solution)/shard_map/ppermute | solution.py:18
